TPU v7x, 32 devices: a whole 2x2x4 slice. The times are simulated.
32 devices in a mesh: gx: 4 (over z), gy: 4 (over x, core), gz: 2 (over y).
Axes of the slice: x: 2, y: 2, z: 4, core: 2. Of those that a mesh axis runs over, the one named last changes fastest.
Arguments:
- basis: bfloat16 [224, 64, 4096], P(('gx', 'gy', 'gz')), may hold values from -6 to 6
- density_blocks: bfloat16 [1536, 4096], P(('gx', 'gy', 'gz')), may hold values from -0.014953613 to 0.014953613
- pair_groups: int32 [2, 1536], P(None, ('gx', 'gy', 'gz')), may hold values from 0 to 6, as said below
- owner: int32 [1536, 1], P(('gx', 'gy', 'gz')), may hold values from 0 to 15; in each aligned block of 48 rows (0 to 47, 48 to 95, ...) at most 6 rows name the same one
- owner_slot: int32 [1536], P(('gx', 'gy', 'gz')), may hold values from 0 to 47
Outputs:
- ks_blocks: bfloat16 [1536, 4096], P(('gx', 'gy', 'gz'))
- xc_potential: float32 [32, 32, 16], P('gx', 'gy', 'gz')
Inputs may be any that keep to these rules, and one draw needn't show every extreme that they name: At most 6 pairs of one subdomain name the same owner, and in every draw some subdomain's pairs name one owner exactly 6 times; every owner is named by some pair. `pair_groups`: the pairs of one subdomain are distinct ordered pairs of its groups.
All inputs are finite; a program needn't handle non-finite values.
Results may differ from a plain program's by a relative error of at most 0.0055.
Values may be sent and summed in bfloat16 or wider, within the bound.
No kernel may reach another device: no remote copies, remote signals or barrier semaphores. Data moves between devices by JAX's collectives and lax.ppermute only.
A program may use at most 64 MiB of HBM per device.

v0:
```python
import jax
import jax.numpy as jnp
from jax import lax
from jax.sharding import PartitionSpec as P

BASIS = 64
CELLS = 8
RIM = 4
EXT = 16
EXT3 = 4096


XC_COEF = 0.9847450218426965
GRID_WEIGHT = 0.015625


def extended(cells, sides, width):
    for axis, dim in sides:
        count = lax.axis_size(axis)
        head = lax.slice_in_dim(cells, 0, width, axis=dim)
        tail = lax.slice_in_dim(cells, cells.shape[dim] - width, cells.shape[dim], axis=dim)
        cells = jnp.concatenate(
            [
                lax.ppermute(tail, axis, [(i, (i + 1) % count) for i in range(count)]),
                cells,
                lax.ppermute(head, axis, [((i + 1) % count, i) for i in range(count)]),
            ],
            axis=dim,
        )
    return cells


def slater_potential(density):
    return -XC_COEF * density / jnp.cbrt(density * density + 1.0)


def fold_axis(padded, dimension):
    lower = lax.slice_in_dim(padded, 0, RIM, axis=dimension)
    middle = lax.slice_in_dim(padded, 2 * RIM, 2 * RIM + CELLS, axis=dimension)
    upper = lax.slice_in_dim(padded, CELLS + 3 * RIM, CELLS + 4 * RIM, axis=dimension)
    widths_low = [
        (0, CELLS - RIM) if position == dimension else (0, 0) for position in range(padded.ndim)
    ]
    widths_high = [
        (CELLS - RIM, 0) if position == dimension else (0, 0) for position in range(padded.ndim)
    ]
    return middle + jnp.pad(lower, widths_low) + jnp.pad(upper, widths_high)


def per_device(basis, density_blocks, pair_groups, owner, owner_slot):
    groups = basis.shape[0]
    pairs = density_blocks.shape[0]
    square = BASIS * BASIS
    pair_codes = pair_groups[0] * groups + pair_groups[1]
    code_match = (
        pair_codes[:, None] == jnp.arange(groups * groups, dtype=jnp.int32)[None, :]
    ).astype(jnp.bfloat16)
    dense_blocks = lax.dot_general(
        code_match, density_blocks, (((0,), (0,)), ((), ())), preferred_element_type=jnp.float32
    ).astype(jnp.bfloat16)
    matrix = (
        dense_blocks.reshape(groups, groups, BASIS, BASIS)
        .transpose(0, 2, 1, 3)
        .reshape(groups * BASIS, groups * BASIS)
    )
    stacked = basis.reshape(groups * BASIS, EXT3)
    projected = jnp.dot(matrix, stacked, preferred_element_type=jnp.float32)
    box_density = jnp.sum(stacked.astype(jnp.float32) * projected, axis=0).reshape(EXT, EXT, EXT)
    along_x = fold_axis(extended(box_density, (("gx", 0),), RIM), 0)
    along_y = fold_axis(extended(along_x, (("gy", 1),), RIM), 1)
    density = fold_axis(extended(along_y, (("gz", 2),), RIM), 2)
    potential = slater_potential(density)
    potential_ext = extended(potential, (("gx", 0), ("gy", 1), ("gz", 2)), RIM).reshape(EXT3)
    weighted = (stacked.astype(jnp.float32) * potential_ext[None, :]).astype(jnp.bfloat16)
    ks_full = (
        lax.dot_general(
            weighted, stacked, (((1,), (1,)), ((), ())), preferred_element_type=jnp.float32
        )
        * GRID_WEIGHT
    )
    ks_table = (
        ks_full.reshape(groups, BASIS, groups, BASIS)
        .transpose(0, 2, 1, 3)
        .reshape(groups * groups, square)
    )
    pair_blocks = jnp.take(ks_table, pair_codes, axis=0).astype(jnp.bfloat16)
    rows_x = lax.axis_size("gx")
    rows_y = lax.axis_size("gy")
    owners = rows_x * rows_y
    capacity = max(2, 2 * pairs // owners)
    owner_ids = owner[:, 0]
    order_ids = jnp.arange(pairs, dtype=jnp.int32)
    earlier = (owner_ids[:, None] == owner_ids[None, :]) & (order_ids[:, None] > order_ids[None, :])
    rank_within = jnp.sum(earlier.astype(jnp.int32), axis=1)
    positions = owner_ids * capacity + rank_within
    slot_match = jnp.arange(owners * capacity, dtype=jnp.int32)[:, None] == positions[None, :]
    send_blocks = jnp.dot(
        slot_match.astype(jnp.bfloat16), pair_blocks, preferred_element_type=jnp.float32
    ).astype(jnp.bfloat16)
    send_slots = jnp.sum(jnp.where(slot_match, owner_slot[None, :] + 1, 0), axis=1) - 1
    got_blocks, got_slots = (
        lax.all_to_all(
            send_blocks.reshape(owners, capacity, square),
            ("gx", "gy"),
            split_axis=0,
            concat_axis=0,
            tiled=True,
        ),
        lax.all_to_all(
            send_slots.reshape(owners, capacity),
            ("gx", "gy"),
            split_axis=0,
            concat_axis=0,
            tiled=True,
        ),
    )
    got_blocks = got_blocks.reshape(owners * capacity, square)
    got_slots = got_slots.reshape(owners * capacity)
    store_match = (jnp.arange(pairs, dtype=jnp.int32)[:, None] == got_slots[None, :]).astype(
        jnp.bfloat16
    )
    ks_blocks = jnp.dot(store_match, got_blocks, preferred_element_type=jnp.float32).astype(
        jnp.bfloat16
    )
    return (ks_blocks, potential)


def solution(mesh):
    return jax.shard_map(
        per_device,
        mesh=mesh,
        in_specs=(
            P(("gx", "gy", "gz"), None, None),
            P(("gx", "gy", "gz"), None),
            P(None, ("gx", "gy", "gz")),
            P(("gx", "gy", "gz"), None),
            P(("gx", "gy", "gz")),
        ),
        out_specs=(P(("gx", "gy", "gz"), None), P("gx", "gy", "gz")),
        check_vma=False,
    )
```

profile of v0, /device:TPU:9, one launch (start us, length us, event | category | flops | bytes accessed | tf_op | source)
XLA Modules:
  0.0 87.8 jit_solution(1849117371157789186)
XLA Ops:
  2.0 0.9 reshape.139
  3.9 5.2 %multiply_reduce_fusion = f32[4096]{0:T(1024)S(1)} fusion(bf16[448,4096]{1,0:T(8,128)(2,1)} %bitcast.23, bf16[448,448]{1,0:T(8,128)(2,1)S(1)} %reshape.140), kind=kOutput, calls=%fused_computation.2 | convolution fusion | flops 1649668096 | bytes 4087808 | tf_op jit(solution)/shard_map/dot_general | solution.py:67
  9.3 1.3 %collective-permute-start = (f32[4,16,16]{2,1,0:T(8,128)S(1)}, f32[4,16,16]{2,1,0:T(8,128)S(1)}, u32[]{:S(2)}, u32[]{:S(2)}) collective-permute-start(f32[4,16,16]{2,1,0:T(8,128)S(1)} %slice.89), channel_id=1, source_target_pairs={{0,8},{8,16},{16,24},{24,0},{1,9},{9,17},{17,25},{25,1},{2,10},{10... | collective-permute-start | bytes 12296 | tf_op jit(solution)/shard_map/ppermute | solution.py:24
  11.1 0.9 %collective-permute-done = f32[4,16,16]{2,1,0:T(8,128)S(1)} collective-permute-done((f32[4,16,16]{2,1,0:T(8,128)S(1)}, f32[4,16,16]{2,1,0:T(8,128)S(1)}, u32[]{:S(2)}, u32[]{:S(2)}) %collective-permute-start) | collective-permute-done | bytes 4128 | tf_op jit(solution)/shard_map/ppermute | solution.py:24
  12.1 1.4 %collective-permute-done.1 = f32[4,16,16]{2,1,0:T(8,128)S(1)} collective-permute-done((f32[4,16,16]{2,1,0:T(8,128)S(1)}, f32[4,16,16]{2,1,0:T(8,128)S(1)}, u32[]{:S(2)}, u32[]{:S(2)}) %collective-permute-start.1) | collective-permute-done | bytes 4128 | tf_op jit(solution)/shard_map/ppermute | solution.py:26
  13.5 3.2 %collective-permute-start.2 = (f32[8,4,16]{2,1,0:T(4,128)S(1)}, f32[8,4,16]{2,1,0:T(4,128)S(1)}, u32[]{:S(2)}, u32[]{:S(2)}) collective-permute-start(f32[8,4,16]{2,1,0:T(4,128)S(1)} %get-tuple-element.8), channel_id=1, source_target_pairs={{0,2},{2,4},{4,6},{6,0},{1,3},{3,5},{5,7},{7,1},{8,10},{10,12},{12... | collective-permute-start | bytes 6152 | tf_op jit(solution)/shard_map/ppermute | solution.py:24
  17.6 2.3 %collective-permute-done.3 = f32[8,4,16]{2,1,0:T(4,128)S(1)} collective-permute-done((f32[8,4,16]{2,1,0:T(4,128)S(1)}, f32[8,4,16]{2,1,0:T(4,128)S(1)}, u32[]{:S(2)}, u32[]{:S(2)}) %collective-permute-start.3) | collective-permute-done | bytes 2080 | tf_op jit(solution)/shard_map/ppermute | solution.py:26
  20.0 1.3 %collective-permute-start.4 = (f32[8,8,4]{2,1,0:T(8,128)S(1)}, f32[8,8,4]{2,1,0:T(8,128)S(1)}, u32[]{:S(2)}, u32[]{:S(2)}) collective-permute-start(f32[8,8,4]{2,1,0:T(8,128)S(1)} %get-tuple-element.12), channel_id=1, source_target_pairs={{0,1},{1,0},{2,3},{3,2},{4,5},{5,4},{6,7},{7,6},{8,9},{9,8},{10,11... | collective-permute-start | bytes 3080 | tf_op jit(solution)/shard_map/ppermute | solution.py:24
  21.5 1.2 %collective-permute-done.4 = f32[8,8,4]{2,1,0:T(8,128)S(1)} collective-permute-done((f32[8,8,4]{2,1,0:T(8,128)S(1)}, f32[8,8,4]{2,1,0:T(8,128)S(1)}, u32[]{:S(2)}, u32[]{:S(2)}) %collective-permute-start.4) | collective-permute-done | bytes 1056 | tf_op jit(solution)/shard_map/ppermute | solution.py:24
  22.7 1.3 %collective-permute-done.5 = f32[8,8,4]{2,1,0:T(8,128)S(1)} collective-permute-done((f32[8,8,4]{2,1,0:T(8,128)S(1)}, f32[8,8,4]{2,1,0:T(8,128)S(1)}, u32[]{:S(2)}, u32[]{:S(2)}) %collective-permute-start.5) | collective-permute-done | bytes 1056 | tf_op jit(solution)/shard_map/ppermute | solution.py:26
  24.2 1.4 %collective-permute-start.6 = (f32[4,8,8]{2,1,0:T(8,128)S(1)}, f32[4,8,8]{2,1,0:T(8,128)S(1)}, u32[]{:S(2)}, u32[]{:S(2)}) collective-permute-start(f32[4,8,8]{2,1,0:T(8,128)S(1)} %get-tuple-element.10), channel_id=1, source_target_pairs={{0,8},{8,16},{16,24},{24,0},{1,9},{9,17},{17,25},{25,1},{2,10},{10... | collective-permute-start | bytes 3080 | tf_op jit(solution)/shard_map/ppermute | solution.py:24
  26.4 7.2 %all-to-all-start = ((s32[16,1,6]{2,1,0:T(1,128)}), s32[16,1,6]{2,1,0:T(1,128)S(1)}, u32[]{:S(2)}, u32[]{:S(2)}) async-start(s32[16,1,6]{2,1,0:T(1,128)} %bitcast.1), calls=%async_computation | async-start | bytes 16384 | tf_op jit(solution)/shard_map/all_to_all | solution.py:109
  33.7 1.5 %collective-permute-start.8 = (f32[16,4,8]{2,1,0:T(4,128)S(1)}, f32[16,4,8]{2,1,0:T(4,128)S(1)}, u32[]{:S(2)}, u32[]{:S(2)}) collective-permute-start(f32[16,4,8]{2,1,0:T(4,128)S(1)} %get-tuple-element.6), channel_id=1, source_target_pairs={{0,2},{2,4},{4,6},{6,0},{1,3},{3,5},{5,7},{7,1},{8,10},{10,12},{12... | collective-permute-start | bytes 6152 | tf_op jit(solution)/shard_map/ppermute | solution.py:24
  35.2 1.0 %collective-permute-done.8 = f32[16,4,8]{2,1,0:T(4,128)S(1)} collective-permute-done((f32[16,4,8]{2,1,0:T(4,128)S(1)}, f32[16,4,8]{2,1,0:T(4,128)S(1)}, u32[]{:S(2)}, u32[]{:S(2)}) %collective-permute-start.8) | collective-permute-done | bytes 2080 | tf_op jit(solution)/shard_map/ppermute | solution.py:24
  36.2 2.3 %collective-permute-done.9 = f32[16,4,8]{2,1,0:T(4,128)S(1)} collective-permute-done((f32[16,4,8]{2,1,0:T(4,128)S(1)}, f32[16,4,8]{2,1,0:T(4,128)S(1)}, u32[]{:S(2)}, u32[]{:S(2)}) %collective-permute-start.9) | collective-permute-done | bytes 2080 | tf_op jit(solution)/shard_map/ppermute | solution.py:26
  39.2 1.0 %collective-permute-start.11 = (f32[16,16,4]{2,1,0:T(8,128)S(1)}, f32[16,16,4]{2,1,0:T(8,128)S(1)}, u32[]{:S(2)}, u32[]{:S(2)}) collective-permute-start(f32[16,16,4]{2,1,0:T(8,128)S(1)} %get-tuple-element.5), channel_id=1, source_target_pairs={{1,0},{0,1},{3,2},{2,3},{5,4},{4,5},{7,6},{6,7},{9,8},{8,9},{11,10... | collective-permute-start | bytes 12296 | tf_op jit(solution)/shard_map/ppermute | solution.py:26
  40.2 4.0 %collective-permute-done.10 = f32[16,16,4]{2,1,0:T(8,128)S(1)} collective-permute-done((f32[16,16,4]{2,1,0:T(8,128)S(1)}, f32[16,16,4]{2,1,0:T(8,128)S(1)}, u32[]{:S(2)}, u32[]{:S(2)}) %collective-permute-start.10) | collective-permute-done | bytes 4128 | tf_op jit(solution)/shard_map/ppermute | solution.py:24
  44.3 1.9 %collective-permute-done.11 = f32[16,16,4]{2,1,0:T(8,128)S(1)} collective-permute-done((f32[16,16,4]{2,1,0:T(8,128)S(1)}, f32[16,16,4]{2,1,0:T(8,128)S(1)}, u32[]{:S(2)}, u32[]{:S(2)}) %collective-permute-start.11) | collective-permute-done | bytes 4128 | tf_op jit(solution)/shard_map/ppermute | solution.py:26
  46.4 3.1 %multiply_convert_fusion = bf16[7,64,4096]{2,1,0:T(8,128)(2,1)S(1)} fusion(bf16[7,64,4096]{2,1,0:T(8,128)(2,1)} %param.5, f32[4096]{0:T(1024)S(1)} %mul.67), kind=kLoop, calls=%fused_computation.1 | loop fusion | flops 5505024 | bytes 7356416 | tf_op jit(solution)/shard_map/convert_element_type | solution.py:74
  49.6 2.1 %convolution_multiply_fusion = bf16[448,448]{1,0:T(8,128)(2,1)S(1)} fusion(bf16[448,4096]{1,0:T(8,128)(2,1)S(1)} %bitcast.25, bf16[448,4096]{1,0:T(8,128)(2,1)S(1)} %bitcast.24), kind=kOutput, calls=%fused_computation.6 | convolution fusion | flops 1644568576 | bytes 7741440 | tf_op jit(solution)/shard_map/dot_general | solution.py:76
  54.4 1.2 %reshape.143 = bf16[16,6,4096]{2,1,0:T(8,128)(2,1)} reshape(bf16[96,4096]{1,0:T(8,128)(2,1)S(1)} %convolution_convert_fusion) | data formatting | bytes 1572864 | tf_op jit(solution)/shard_map/reshape | solution.py:103
  55.6 6.0 %all-to-all-start.1 = ((bf16[16,6,4096]{2,1,0:T(8,128)(2,1)}), bf16[16,6,4096]{2,1,0:T(8,128)(2,1)S(1)}, u32[]{:S(2)}, u32[]{:S(2)}) async-start(bf16[16,6,4096]{2,1,0:T(8,128)(2,1)} %reshape.143), calls=%async_computation.1 | async-start | bytes 2097152 | tf_op jit(solution)/shard_map/all_to_all | solution.py:102
  62.9 23.6 %all-to-all-done.1 = bf16[16,6,4096]{2,1,0:T(8,128)(2,1)S(1)} async-done(((bf16[16,6,4096]{2,1,0:T(8,128)(2,1)}), bf16[16,6,4096]{2,1,0:T(8,128)(2,1)S(1)}, u32[]{:S(2)}, u32[]{:S(2)}) %all-to-all-start.1) | async-done | bytes 786464 | tf_op jit(solution)/shard_map/all_to_all | solution.py:102
  86.8 1.0 %convolution_convert_fusion.2 = bf16[48,4096]{1,0:T(8,128)(2,1)} fusion(bf16[96,4096]{1,0:T(8,128)(2,1)S(1)} %reshape.144, s32[96]{0:T(128)S(1)} %eq.61), kind=kOutput, calls=%fused_computation.5 | convolution fusion | flops 37949952 | bytes 1180032 | tf_op jit(solution)/shard_map/dot_general | solution.py:122
  (57 shorter events, 10.4 us)
Async XLA Ops:
  0.6 1.0 %copy-start = (bf16[48,4096]{1,0:T(8,128)(2,1)S(1)}, bf16[48,4096]{1,0:T(8,128)(2,1)}, u32[]{:S(2)}) copy-start(bf16[48,4096]{1,0:T(8,128)(2,1)} %param.6) | copy-start | bytes 1179652
  3.9 6.9 %copy-start.3 = (s32[48,1]{0,1:T(1,128)S(1)}, s32[48,1]{0,1:T(1,128)}, u32[]{:S(2)}) copy-start(s32[48,1]{0,1:T(1,128)} %param.8) | copy-start | bytes 580
  3.9 12.8 %copy-start.4 = (s32[48]{0:T(128)S(1)}, s32[48]{0:T(128)}, u32[]{:S(2)}) copy-start(s32[48]{0:T(128)} %param.9) | copy-start | bytes 580
  9.3 2.8 %collective-permute-start = (f32[4,16,16]{2,1,0:T(8,128)S(1)}, f32[4,16,16]{2,1,0:T(8,128)S(1)}, u32[]{:S(2)}, u32[]{:S(2)}) collective-permute-start(f32[4,16,16]{2,1,0:T(8,128)S(1)} %slice.89), channel_id=1, source_target_pairs={{0,8},{8,16},{16,24},{24,0},{1,9},{9,17},{17,25},{25,1},{2,10},{10... | collective-permute-start | bytes 12296 | tf_op jit(solution)/shard_map/ppermute | solution.py:24
  10.7 2.8 %collective-permute-start.1 = (f32[4,16,16]{2,1,0:T(8,128)S(1)}, f32[4,16,16]{2,1,0:T(8,128)S(1)}, u32[]{:S(2)}, u32[]{:S(2)}) collective-permute-start(f32[4,16,16]{2,1,0:T(8,128)S(1)} %slice.91), channel_id=1, source_target_pairs={{8,0},{16,8},{24,16},{0,24},{9,1},{17,9},{25,17},{1,25},{10,2},{18... | collective-permute-start | bytes 12296 | tf_op jit(solution)/shard_map/ppermute | solution.py:26
  13.5 4.1 %collective-permute-start.2 = (f32[8,4,16]{2,1,0:T(4,128)S(1)}, f32[8,4,16]{2,1,0:T(4,128)S(1)}, u32[]{:S(2)}, u32[]{:S(2)}) collective-permute-start(f32[8,4,16]{2,1,0:T(4,128)S(1)} %get-tuple-element.8), channel_id=1, source_target_pairs={{0,2},{2,4},{4,6},{6,0},{1,3},{3,5},{5,7},{7,1},{8,10},{10,12},{12... | collective-permute-start | bytes 6152 | tf_op jit(solution)/shard_map/ppermute | solution.py:24
  16.7 3.2 %collective-permute-start.3 = (f32[8,4,16]{2,1,0:T(4,128)S(1)}, f32[8,4,16]{2,1,0:T(4,128)S(1)}, u32[]{:S(2)}, u32[]{:S(2)}) collective-permute-start(f32[8,4,16]{2,1,0:T(4,128)S(1)} %get-tuple-element.9), channel_id=1, source_target_pairs={{2,0},{4,2},{6,4},{0,6},{3,1},{5,3},{7,5},{1,7},{10,8},{12,10},{14... | collective-permute-start | bytes 6152 | tf_op jit(solution)/shard_map/ppermute | solution.py:26
  20.0 2.8 %collective-permute-start.4 = (f32[8,8,4]{2,1,0:T(8,128)S(1)}, f32[8,8,4]{2,1,0:T(8,128)S(1)}, u32[]{:S(2)}, u32[]{:S(2)}) collective-permute-start(f32[8,8,4]{2,1,0:T(8,128)S(1)} %get-tuple-element.12), channel_id=1, source_target_pairs={{0,1},{1,0},{2,3},{3,2},{4,5},{5,4},{6,7},{7,6},{8,9},{9,8},{10,11... | collective-permute-start | bytes 3080 | tf_op jit(solution)/shard_map/ppermute | solution.py:24
  21.2 2.8 %collective-permute-start.5 = (f32[8,8,4]{2,1,0:T(8,128)S(1)}, f32[8,8,4]{2,1,0:T(8,128)S(1)}, u32[]{:S(2)}, u32[]{:S(2)}) collective-permute-start(f32[8,8,4]{2,1,0:T(8,128)S(1)} %get-tuple-element.13), channel_id=1, source_target_pairs={{1,0},{0,1},{3,2},{2,3},{5,4},{4,5},{7,6},{6,7},{9,8},{8,9},{11,10... | collective-permute-start | bytes 3080 | tf_op jit(solution)/shard_map/ppermute | solution.py:26
  24.1 25.4 %copy-start.2 = (f32[8,8,8]{2,1,0:T(8,128)}, f32[8,8,8]{2,1,0:T(8,128)S(1)}, u32[]{:S(2)}) copy-start(f32[8,8,8]{2,1,0:T(8,128)S(1)} %cbrt_divide_fusion) | copy-start | bytes 6148
  24.2 9.4 %collective-permute-start.6 = (f32[4,8,8]{2,1,0:T(8,128)S(1)}, f32[4,8,8]{2,1,0:T(8,128)S(1)}, u32[]{:S(2)}, u32[]{:S(2)}) collective-permute-start(f32[4,8,8]{2,1,0:T(8,128)S(1)} %get-tuple-element.10), channel_id=1, source_target_pairs={{0,8},{8,16},{16,24},{24,0},{1,9},{9,17},{17,25},{25,1},{2,10},{10... | collective-permute-start | bytes 3080 | tf_op jit(solution)/shard_map/ppermute | solution.py:24
  25.5 8.1 %collective-permute-start.7 = (f32[4,8,8]{2,1,0:T(8,128)S(1)}, f32[4,8,8]{2,1,0:T(8,128)S(1)}, u32[]{:S(2)}, u32[]{:S(2)}) collective-permute-start(f32[4,8,8]{2,1,0:T(8,128)S(1)} %get-tuple-element.11), channel_id=1, source_target_pairs={{8,0},{16,8},{24,16},{0,24},{9,1},{17,9},{25,17},{1,25},{10,2},{18... | collective-permute-start | bytes 3080 | tf_op jit(solution)/shard_map/ppermute | solution.py:26
  26.4 29.2 %all-to-all-start = ((s32[16,1,6]{2,1,0:T(1,128)}), s32[16,1,6]{2,1,0:T(1,128)S(1)}, u32[]{:S(2)}, u32[]{:S(2)}) async-start(s32[16,1,6]{2,1,0:T(1,128)} %bitcast.1), calls=%async_computation | async-start | bytes 16384 | tf_op jit(solution)/shard_map/all_to_all | solution.py:109
  33.7 2.5 %collective-permute-start.8 = (f32[16,4,8]{2,1,0:T(4,128)S(1)}, f32[16,4,8]{2,1,0:T(4,128)S(1)}, u32[]{:S(2)}, u32[]{:S(2)}) collective-permute-start(f32[16,4,8]{2,1,0:T(4,128)S(1)} %get-tuple-element.6), channel_id=1, source_target_pairs={{0,2},{2,4},{4,6},{6,0},{1,3},{3,5},{5,7},{7,1},{8,10},{10,12},{12... | collective-permute-start | bytes 6152 | tf_op jit(solution)/shard_map/ppermute | solution.py:24
  35.2 3.4 %collective-permute-start.9 = (f32[16,4,8]{2,1,0:T(4,128)S(1)}, f32[16,4,8]{2,1,0:T(4,128)S(1)}, u32[]{:S(2)}, u32[]{:S(2)}) collective-permute-start(f32[16,4,8]{2,1,0:T(4,128)S(1)} %get-tuple-element.7), channel_id=1, source_target_pairs={{2,0},{4,2},{6,4},{0,6},{3,1},{5,3},{7,5},{1,7},{10,8},{12,10},{14... | collective-permute-start | bytes 6152 | tf_op jit(solution)/shard_map/ppermute | solution.py:26
  38.7 5.6 %collective-permute-start.10 = (f32[16,16,4]{2,1,0:T(8,128)S(1)}, f32[16,16,4]{2,1,0:T(8,128)S(1)}, u32[]{:S(2)}, u32[]{:S(2)}) collective-permute-start(f32[16,16,4]{2,1,0:T(8,128)S(1)} %get-tuple-element.4), channel_id=1, source_target_pairs={{0,1},{1,0},{2,3},{3,2},{4,5},{5,4},{6,7},{7,6},{8,9},{9,8},{10,11... | collective-permute-start | bytes 12296 | tf_op jit(solution)/shard_map/ppermute | solution.py:24
  39.2 7.0 %collective-permute-start.11 = (f32[16,16,4]{2,1,0:T(8,128)S(1)}, f32[16,16,4]{2,1,0:T(8,128)S(1)}, u32[]{:S(2)}, u32[]{:S(2)}) collective-permute-start(f32[16,16,4]{2,1,0:T(8,128)S(1)} %get-tuple-element.5), channel_id=1, source_target_pairs={{1,0},{0,1},{3,2},{2,3},{5,4},{4,5},{7,6},{6,7},{9,8},{8,9},{11,10... | collective-permute-start | bytes 12296 | tf_op jit(solution)/shard_map/ppermute | solution.py:26
  46.4 3.1 %copy-start.1 = (bf16[7,64,4096]{2,1,0:T(8,128)(2,1)S(1)}, bf16[7,64,4096]{2,1,0:T(8,128)(2,1)}, u32[]{:S(2)}) copy-start(bf16[7,64,4096]{2,1,0:T(8,128)(2,1)} %param.5) | copy-start | bytes 11010052
  55.6 30.9 %all-to-all-start.1 = ((bf16[16,6,4096]{2,1,0:T(8,128)(2,1)}), bf16[16,6,4096]{2,1,0:T(8,128)(2,1)S(1)}, u32[]{:S(2)}, u32[]{:S(2)}) async-start(bf16[16,6,4096]{2,1,0:T(8,128)(2,1)} %reshape.143), calls=%async_computation.1 | async-start | bytes 2097152 | tf_op jit(solution)/shard_map/all_to_all | solution.py:102
where the time goes:
time: 88.1 us; the launch traced here: 87.8 us
  waiting for transfers between devices  41 us (47%)
  starting transfers between devices  23.9 us (27%)
  matrix products  9.17 us (10%)
  local copies, waits for them, and re-layouts  7.69 us (9%)
  other arithmetic  5.15 us (6%)
  between operations  0.9 us (1%)
    all_to_all x1, waiting for transfers between devices, per_device(): lax.all_to_all(send_blocks.reshape(owners, capacity, square), ('gx', 'gy'...  23.6 us
    ppermute x6, waiting for transfers between devices, extended(): lax.ppermute(head, axis, [((i + 1) % count, i) for i in range(count)])  9.23 us
    ppermute x6, starting transfers between devices, extended(): lax.ppermute(tail, axis, [(i, (i + 1) % count) for i in range(count)])  9.11 us
    ppermute x6, waiting for transfers between devices, extended(): lax.ppermute(tail, axis, [(i, (i + 1) % count) for i in range(count)])  8.07 us
    all_to_all x1, starting transfers between devices, per_device(): lax.all_to_all(send_slots.reshape(owners, capacity), ('gx', 'gy'), split_...  7.23 us
    all_to_all x1, starting transfers between devices, per_device(): lax.all_to_all(send_blocks.reshape(owners, capacity, square), ('gx', 'gy'...  6 us
    dot_general x1, matrix products, per_device(): projected = jnp.dot(matrix, stacked, preferred_element_type=jnp.float32)  5.25 us
    convert_element_type x1, other arithmetic, per_device(): (stacked.astype(jnp.float32) * potential_ext[None, :]).astype(jnp.bfloat16)  3.07 us
  transfers between devices with their start and end apart: 14, of which 11 were waited for; matrix products, arithmetic and copies ran while one was open for 14% of the time, Pallas kernels for 0%

commit v1 on v0

--- a/solution.py
+++ b/solution.py
@@ -8,43 +8,62 @@
 RIM = 4
 EXT = 16
 EXT3 = 4096
-
+LANES = 128
 
 XC_COEF = 0.9847450218426965
 GRID_WEIGHT = 0.015625
-
-
-def extended(cells, sides, width):
-    for axis, dim in sides:
-        count = lax.axis_size(axis)
-        head = lax.slice_in_dim(cells, 0, width, axis=dim)
-        tail = lax.slice_in_dim(cells, cells.shape[dim] - width, cells.shape[dim], axis=dim)
-        cells = jnp.concatenate(
-            [
-                lax.ppermute(tail, axis, [(i, (i + 1) % count) for i in range(count)]),
-                cells,
-                lax.ppermute(head, axis, [((i + 1) % count, i) for i in range(count)]),
-            ],
-            axis=dim,
-        )
-    return cells
 
 
 def slater_potential(density):
     return -XC_COEF * density / jnp.cbrt(density * density + 1.0)
 
 
-def fold_axis(padded, dimension):
-    lower = lax.slice_in_dim(padded, 0, RIM, axis=dimension)
-    middle = lax.slice_in_dim(padded, 2 * RIM, 2 * RIM + CELLS, axis=dimension)
-    upper = lax.slice_in_dim(padded, CELLS + 3 * RIM, CELLS + 4 * RIM, axis=dimension)
-    widths_low = [
-        (0, CELLS - RIM) if position == dimension else (0, 0) for position in range(padded.ndim)
-    ]
-    widths_high = [
-        (CELLS - RIM, 0) if position == dimension else (0, 0) for position in range(padded.ndim)
-    ]
-    return middle + jnp.pad(lower, widths_low) + jnp.pad(upper, widths_high)
+def neighbour_swaps(count, first):
+    pairs = []
+    for low in range(first, count + first, 2):
+        left, right = low % count, (low + 1) % count
+        pairs += [(left, right), (right, left)]
+    return pairs
+
+
+def merged(low, high, axis, forward=False):
+    count = lax.axis_size(axis)
+    if count == 2:
+        got = lax.ppermute(jnp.stack([high, low]), axis, neighbour_swaps(count, 0))
+        return low + got[0], high + got[1]
+    odd = lax.axis_index(axis) % 2 == 1
+    near, far = jnp.where(odd, low, high), jnp.where(odd, high, low)
+    if forward and count == 4:
+        got = lax.ppermute(jnp.stack([near, far]), axis, neighbour_swaps(count, 0))
+        near = near + got[0]
+        far = far + lax.ppermute(got[1], axis, [(i, i ^ 2) for i in range(count)])
+    else:
+        got = lax.ppermute(near, axis, neighbour_swaps(count, 0))
+        other = lax.ppermute(far, axis, neighbour_swaps(count, 1))
+        near, far = near + got, far + other
+    return jnp.where(odd, near, far), jnp.where(odd, far, near)
+
+
+def z_halves_swapped(box):
+    lane = lax.broadcasted_iota(jnp.int32, box.shape, box.ndim - 1)
+    return jnp.where(
+        lane % EXT < EXT // 2,
+        jnp.roll(box, -EXT // 2, axis=-1),
+        jnp.roll(box, EXT // 2, axis=-1),
+    )
+
+
+def merged_z(box, axis):
+    count = lax.axis_size(axis)
+    swapped = z_halves_swapped(box)
+    if count == 2:
+        return box + lax.ppermute(swapped, axis, neighbour_swaps(count, 0))
+    odd = lax.axis_index(axis) % 2 == 1
+    lane = lax.broadcasted_iota(jnp.int32, box.shape, box.ndim - 1)
+    in_high = lane % EXT >= EXT // 2
+    first = lax.ppermute(swapped, axis, neighbour_swaps(count, 0))
+    second = lax.ppermute(swapped, axis, neighbour_swaps(count, 1))
+    return box + jnp.where(in_high != odd, first, second)
 
 
 def per_device(basis, density_blocks, pair_groups, owner, owner_slot):
@@ -65,13 +84,20 @@
     )
     stacked = basis.reshape(groups * BASIS, EXT3)
     projected = jnp.dot(matrix, stacked, preferred_element_type=jnp.float32)
-    box_density = jnp.sum(stacked.astype(jnp.float32) * projected, axis=0).reshape(EXT, EXT, EXT)
-    along_x = fold_axis(extended(box_density, (("gx", 0),), RIM), 0)
-    along_y = fold_axis(extended(along_x, (("gy", 1),), RIM), 1)
-    density = fold_axis(extended(along_y, (("gz", 2),), RIM), 2)
-    potential = slater_potential(density)
-    potential_ext = extended(potential, (("gx", 0), ("gy", 1), ("gz", 2)), RIM).reshape(EXT3)
-    weighted = (stacked.astype(jnp.float32) * potential_ext[None, :]).astype(jnp.bfloat16)
+    box = (
+        jnp.sum(stacked.astype(jnp.float32) * projected, axis=0)
+        .reshape(EXT, 2, LANES)
+        .transpose(1, 0, 2)
+    )
+    box = merged_z(box, "gz")
+    y_low, y_high = merged(box[0], box[1], "gy")
+    box = jnp.stack([y_low, y_high])
+    x_low, x_high = merged(box[:, : EXT // 2], box[:, EXT // 2 :], "gx", forward=True)
+    potential_ext = slater_potential(jnp.concatenate([x_low, x_high], axis=1))
+    potential = potential_ext.reshape(2, EXT, EXT // 2, EXT)[:, RIM : RIM + CELLS, :, RIM : RIM + CELLS]
+    potential = jnp.concatenate([potential[0, :, RIM:], potential[1, :, :RIM]], axis=1)
+    potential_row = potential_ext.transpose(1, 0, 2).reshape(EXT3)
+    weighted = (stacked.astype(jnp.float32) * potential_row[None, :]).astype(jnp.bfloat16)
     ks_full = (
         lax.dot_general(
             weighted, stacked, (((1,), (1,)), ((), ())), preferred_element_type=jnp.float32
@@ -84,9 +110,7 @@
         .reshape(groups * groups, square)
     )
     pair_blocks = jnp.take(ks_table, pair_codes, axis=0).astype(jnp.bfloat16)
-    rows_x = lax.axis_size("gx")
-    rows_y = lax.axis_size("gy")
-    owners = rows_x * rows_y
+    owners = lax.axis_size("gx") * lax.axis_size("gy")
     capacity = max(2, 2 * pairs // owners)
     owner_ids = owner[:, 0]
     order_ids = jnp.arange(pairs, dtype=jnp.int32)
@@ -100,7 +124,7 @@
     send_slots = jnp.sum(jnp.where(slot_match, owner_slot[None, :] + 1, 0), axis=1) - 1
     got_blocks, got_slots = (
         lax.all_to_all(
-            send_blocks.reshape(owners, capacity, square),
+            send_blocks.reshape(owners, capacity * square // LANES, LANES),
             ("gx", "gy"),
             split_axis=0,
             concat_axis=0,

time: 88.1 us -> 66.3 us (0.75)
  waiting for transfers between devices: 41 us -> 22.4 us
  starting transfers between devices: 23.9 us -> 20.1 us
    ppermute x12 -> x5, waiting for transfers between devices: 17.3 us -> 5.12 us  [the longest x1 2.77 us: merged(): got = lax.ppermute(jnp.stack([near, far]), axis, neighbour_swaps(count, 0))]
    all_to_all x1, waiting for transfers between devices: 23.6 us -> 17.3 us  [per_device(): lax.all_to_all(send_blocks.reshape(owners, capacity * square // LANES, LA...]
    ppermute x12 -> x5, starting transfers between devices: 10.7 us -> 6.57 us  [the longest x1 2.99 us: merged(): other = lax.ppermute(far, axis, neighbour_swaps(count, 1))]
    all_to_all x1, starting transfers between devices: 6 us -> 8.11 us  [per_device(): lax.all_to_all(send_blocks.reshape(owners, capacity * square // LANES, LA...]
    all_to_all x1, starting transfers between devices: 7.23 us -> 5.45 us  [per_device(): lax.all_to_all(send_slots.reshape(owners, capacity), ('gx', 'gy'), split_...]
  transfers between devices with their start and end apart: 14 -> 7, of which waited for: 11 -> 4; matrix products, arithmetic and copies ran while one was open for 14% -> 19% of each run, Pallas kernels for 0% -> 0%
where the time goes in v1:
time: 66.3 us; the launch traced here: 66.1 us
  waiting for transfers between devices  22.4 us (34%)
  starting transfers between devices  20.1 us (30%)
  matrix products  9.17 us (14%)
  local copies, waits for them, and re-layouts  7.67 us (12%)
  other arithmetic  5.77 us (9%)
  between operations  0.92 us (1%)
    all_to_all x1, waiting for transfers between devices, per_device(): lax.all_to_all(send_blocks.reshape(owners, capacity * square // LANES, LA...  17.3 us
    all_to_all x1, starting transfers between devices, per_device(): lax.all_to_all(send_blocks.reshape(owners, capacity * square // LANES, LA...  8.11 us
    all_to_all x1, starting transfers between devices, per_device(): lax.all_to_all(send_slots.reshape(owners, capacity), ('gx', 'gy'), split_...  5.45 us
    dot_general x1, matrix products, per_device(): projected = jnp.dot(matrix, stacked, preferred_element_type=jnp.float32)  5.25 us
    convert_element_type x1, other arithmetic, per_device(): (stacked.astype(jnp.float32) * potential_row[None, :]).astype(jnp.bfloat16)  3.08 us
    ppermute x1, starting transfers between devices, merged(): other = lax.ppermute(far, axis, neighbour_swaps(count, 1))  2.99 us
    ppermute x1, waiting for transfers between devices, merged(): got = lax.ppermute(jnp.stack([near, far]), axis, neighbour_swaps(count, 0))  2.77 us
    ppermute x1, starting transfers between devices, merged(): far = far + lax.ppermute(got[1], axis, [(i, i ^ 2) for i in range(count)])  2.09 us
  transfers between devices with their start and end apart: 7, of which 4 were waited for; matrix products, arithmetic and copies ran while one was open for 19% of the time, Pallas kernels for 0%

profile of v1, /device:TPU:9, one launch (start us, length us, event | category | flops | bytes accessed | tf_op | source)
XLA Modules:
  0.0 66.1 jit_solution(9477021515885684479)
XLA Ops:
  0.6 0.8 %compare_and_fusion.1 = (pred[48]{0:T(512)(128)(4,1)S(1)}, s32[1,48]{1,0:T(1,128)S(1)}) fusion(s32[2,48]{1,0:T(2,128)} %param.7), kind=kLoop, calls=%fused_computation.51 | loop fusion | flops 384 | bytes 624 | tf_op jit(solution)/shard_map/jit(_take)/and | solution.py:112
  2.0 0.9 %reshape.121 = bf16[7,7,64,64]{3,2,1,0:T(8,128)(2,1)S(1)} reshape(bf16[49,4096]{1,0:T(8,128)(2,1)S(1)} %convolution_convert_fusion.1) | data formatting | bytes 802816 | tf_op jit(solution)/shard_map/reshape | solution.py:81
  2.9 0.6 copy.33
  3.9 5.2 %multiply_reduce_fusion = f32[4096]{0:T(1024)S(1)} fusion(bf16[448,4096]{1,0:T(8,128)(2,1)} %bitcast.58, bf16[448,448]{1,0:T(8,128)(2,1)S(1)} %reshape.122), kind=kOutput, calls=%fused_computation.2 | convolution fusion | flops 1649668096 | bytes 4087808 | tf_op jit(solution)/shard_map/dot_general | solution.py:86
  9.5 1.3 %collective-permute-start = (f32[2,16,128]{2,0,1:T(2,128)S(1)}, f32[2,16,128]{2,0,1:T(2,128)S(1)}, u32[]{:S(2)}, u32[]{:S(2)}) collective-permute-start(f32[2,16,128]{2,0,1:T(2,128)S(1)} %compare_select_fusion), channel_id=1, source_target_pairs={{0,1},{1,0},{2,3},{3,2},{4,5},{5,4},{6,7},{7,6},{8,9},{9,8},{10,11... | collective-permute-start | bytes 49160 | tf_op jit(solution)/shard_map/ppermute | solution.py:60
  11.1 1.0 %collective-permute-done = f32[2,16,128]{2,0,1:T(2,128)S(1)} collective-permute-done((f32[2,16,128]{2,0,1:T(2,128)S(1)}, f32[2,16,128]{2,0,1:T(2,128)S(1)}, u32[]{:S(2)}, u32[]{:S(2)}) %collective-permute-start) | collective-permute-done | bytes 16416 | tf_op jit(solution)/shard_map/ppermute | solution.py:60
  12.2 3.0 %collective-permute-start.2 = (f32[16,128]{1,0:T(8,128)S(1)}, f32[16,128]{1,0:T(8,128)S(1)}, u32[]{:S(2)}, u32[]{:S(2)}) collective-permute-start(f32[16,128]{1,0:T(8,128)S(1)} %bitcast.67), channel_id=1, source_target_pairs={{2,4},{4,2},{6,0},{0,6},{3,5},{5,3},{7,1},{1,7},{10,12},{12,10},{1... | collective-permute-start | bytes 24584 | tf_op jit(solution)/shard_map/ppermute | solution.py:42
  15.2 0.7 %sub.7 = s32[16,1,6]{2,0,1:T(8,128)} reshape(s32[96]{0:T(128)S(1)} %broadcast_add_fusion.1) | data formatting | bytes 768 | tf_op jit(solution)/shard_map/sub | solution.py:124
  15.9 5.4 %all-to-all-start = ((s32[16,1,6]{2,1,0:T(1,128)}), s32[16,1,6]{2,1,0:T(1,128)S(1)}, u32[]{:S(2)}, u32[]{:S(2)}) async-start(s32[16,1,6]{2,1,0:T(1,128)} %bitcast.1), calls=%async_computation | async-start | bytes 16384 | tf_op jit(solution)/shard_map/all_to_all | solution.py:133
  21.6 2.8 %collective-permute-done.3 = f32[2,2,8,128]{3,2,1,0:T(8,128)S(1)} collective-permute-done((f32[2,2,8,128]{3,2,1,0:T(8,128)S(1)}, f32[2,2,8,128]{3,2,1,0:T(8,128)S(1)}, u32[]{:S(2)}, u32[]{:S(2)}) %collective-permute-start.3) | collective-permute-done | bytes 16416 | tf_op jit(solution)/shard_map/ppermute | solution.py:37
  24.4 2.1 %collective-permute-start.4 = (f32[2,8,128]{2,1,0:T(8,128)S(1)}, f32[2,8,128]{2,1,0:T(8,128)S(1)}, u32[]{:S(2)}, u32[]{:S(2)}) collective-permute-start(f32[2,8,128]{2,1,0:T(8,128)S(1)} %slice_bitcast_fusion.2), channel_id=1, source_target_pairs={{0,16},{8,24},{16,0},{24,8},{1,17},{9,25},{17,1},{25,9},{2,18},{10... | collective-permute-start | bytes 24584 | tf_op jit(solution)/shard_map/ppermute | solution.py:39
  26.5 1.3 %collective-permute-done.4 = f32[2,8,128]{2,1,0:T(8,128)S(1)} collective-permute-done((f32[2,8,128]{2,1,0:T(8,128)S(1)}, f32[2,8,128]{2,1,0:T(8,128)S(1)}, u32[]{:S(2)}, u32[]{:S(2)}) %collective-permute-start.4) | collective-permute-done | bytes 8224 | tf_op jit(solution)/shard_map/ppermute | solution.py:39
  27.8 3.1 %multiply_convert_fusion = bf16[7,64,4096]{2,1,0:T(8,128)(2,1)S(1)} fusion(bf16[7,64,4096]{2,1,0:T(8,128)(2,1)} %param.5, f32[4096]{0:T(1024)S(1)} %bitcast.66), kind=kLoop, calls=%fused_computation.1 | loop fusion | flops 5505024 | bytes 7356416 | tf_op jit(solution)/shard_map/convert_element_type | solution.py:100
  31.0 2.1 %convolution_multiply_fusion = bf16[448,448]{1,0:T(8,128)(2,1)S(1)} fusion(bf16[448,4096]{1,0:T(8,128)(2,1)S(1)} %bitcast.60, bf16[448,4096]{1,0:T(8,128)(2,1)S(1)} %bitcast.59), kind=kOutput, calls=%fused_computation.6 | convolution fusion | flops 1644568576 | bytes 7741440 | tf_op jit(solution)/shard_map/dot_general | solution.py:102
  33.0 0.5 reshape.124
  33.8 0.7 %reshape.125 = bf16[49,4096]{1,0:T(8,128)(2,1)S(1)} reshape(bf16[7,7,64,64]{3,2,1,0:T(8,128)(2,1)S(1)} %copy.30) | data formatting | bytes 802816 | tf_op jit(solution)/shard_map/reshape | solution.py:110
  34.5 0.8 %gather_fusion = bf16[48,4096]{1,0:T(8,128)(2,1)S(1)} fusion(bf16[49,4096]{1,0:T(8,128)(2,1)S(1)} %reshape.125, s32[1024]{0:T(1024)S(1)} %pad_clamp_fusion), kind=kCustom, calls=%fused_computation | custom fusion | bytes 786624 | tf_op jit(solution)/shard_map/jit(_take)/gather | solution.py:112
  35.8 1.2 %reshape.126 = bf16[16,192,128]{2,1,0:T(8,128)(2,1)} reshape(bf16[96,4096]{1,0:T(8,128)(2,1)S(1)} %convolution_convert_fusion) | data formatting | bytes 1572864 | tf_op jit(solution)/shard_map/reshape | solution.py:127
  37.0 8.1 %all-to-all-start.1 = ((bf16[16,192,128]{2,1,0:T(8,128)(2,1)}), bf16[16,192,128]{2,1,0:T(8,128)(2,1)S(1)}, u32[]{:S(2)}, u32[]{:S(2)}) async-start(bf16[16,192,128]{2,1,0:T(8,128)(2,1)} %reshape.126), calls=%async_computation.1 | async-start | bytes 1572864 | tf_op jit(solution)/shard_map/all_to_all | solution.py:126
  45.1 0.5 broadcast.93
  45.6 0.7 %reduce.3 = s32[16,6]{1,0:T(8,128)S(1)} reduce(s32[16,1,6]{2,1,0:T(1,128)S(1)} %all-to-all-done, s32[]{:T(128)} %broadcast.93), dimensions={1}, to_apply=%all_to_all.7.reduce_sub_computation.3 | reduce | bytes 772 | tf_op jit(solution)/shard_map/all_to_all | solution.py:133
  46.8 0.6 pad_maximum_fusion
  47.4 17.3 %all-to-all-done.1 = bf16[16,192,128]{2,1,0:T(8,128)(2,1)S(1)} async-done(((bf16[16,192,128]{2,1,0:T(8,128)(2,1)}), bf16[16,192,128]{2,1,0:T(8,128)(2,1)S(1)}, u32[]{:S(2)}, u32[]{:S(2)}) %all-to-all-start.1) | async-done | bytes 786464 | tf_op jit(solution)/shard_map/all_to_all | solution.py:126
  65.1 1.0 %convolution_convert_fusion.2 = bf16[48,4096]{1,0:T(8,128)(2,1)} fusion(bf16[96,4096]{1,0:T(8,128)(2,1)S(1)} %reshape.127, s32[96]{0:T(128)S(1)} %eq.72), kind=kOutput, calls=%fused_computation.5 | convolution fusion | flops 37949952 | bytes 1180032 | tf_op jit(solution)/shard_map/dot_general | solution.py:146
  (47 shorter events, 3.5 us)
Async XLA Ops:
  0.6 1.0 %copy-start = (bf16[48,4096]{1,0:T(8,128)(2,1)S(1)}, bf16[48,4096]{1,0:T(8,128)(2,1)}, u32[]{:S(2)}) copy-start(bf16[48,4096]{1,0:T(8,128)(2,1)} %param.6) | copy-start | bytes 1179652
  3.9 6.9 %copy-start.2 = (s32[48,1]{0,1:T(1,128)S(1)}, s32[48,1]{0,1:T(1,128)}, u32[]{:S(2)}) copy-start(s32[48,1]{0,1:T(1,128)} %param.8) | copy-start | bytes 580
  3.9 7.1 %copy-start.3 = (s32[48]{0:T(128)S(1)}, s32[48]{0:T(128)}, u32[]{:S(2)}) copy-start(s32[48]{0:T(128)} %param.9) | copy-start | bytes 580
  9.5 2.7 %collective-permute-start = (f32[2,16,128]{2,0,1:T(2,128)S(1)}, f32[2,16,128]{2,0,1:T(2,128)S(1)}, u32[]{:S(2)}, u32[]{:S(2)}) collective-permute-start(f32[2,16,128]{2,0,1:T(2,128)S(1)} %compare_select_fusion), channel_id=1, source_target_pairs={{0,1},{1,0},{2,3},{3,2},{4,5},{5,4},{6,7},{7,6},{8,9},{9,8},{10,11... | collective-permute-start | bytes 49160 | tf_op jit(solution)/shard_map/ppermute | solution.py:60
  12.2 9.1 %collective-permute-start.2 = (f32[16,128]{1,0:T(8,128)S(1)}, f32[16,128]{1,0:T(8,128)S(1)}, u32[]{:S(2)}, u32[]{:S(2)}) collective-permute-start(f32[16,128]{1,0:T(8,128)S(1)} %bitcast.67), channel_id=1, source_target_pairs={{2,4},{4,2},{6,0},{0,6},{3,5},{5,3},{7,1},{1,7},{10,12},{12,10},{1... | collective-permute-start | bytes 24584 | tf_op jit(solution)/shard_map/ppermute | solution.py:42
  15.2 6.2 %collective-permute-start.1 = (f32[16,128]{1,0:T(8,128)S(1)}, f32[16,128]{1,0:T(8,128)S(1)}, u32[]{:S(2)}, u32[]{:S(2)}) collective-permute-start(f32[16,128]{1,0:T(8,128)S(1)} %select_bitcast_fusion.2), channel_id=1, source_target_pairs={{0,2},{2,0},{4,6},{6,4},{1,3},{3,1},{5,7},{7,5},{8,10},{10,8},{12,... | collective-permute-start | bytes 24584 | tf_op jit(solution)/shard_map/ppermute | solution.py:41
  15.9 21.1 %all-to-all-start = ((s32[16,1,6]{2,1,0:T(1,128)}), s32[16,1,6]{2,1,0:T(1,128)S(1)}, u32[]{:S(2)}, u32[]{:S(2)}) async-start(s32[16,1,6]{2,1,0:T(1,128)} %bitcast.1), calls=%async_computation | async-start | bytes 16384 | tf_op jit(solution)/shard_map/all_to_all | solution.py:133
  21.4 2.9 %collective-permute-start.3 = (f32[2,2,8,128]{3,2,1,0:T(8,128)S(1)}, f32[2,2,8,128]{3,2,1,0:T(8,128)S(1)}, u32[]{:S(2)}, u32[]{:S(2)}) collective-permute-start(f32[2,2,8,128]{3,2,1,0:T(8,128)S(1)} %pad_maximum_fusion.1), channel_id=1, source_target_pairs={{0,8},{8,0},{16,24},{24,16},{1,9},{9,1},{17,25},{25,17},{2,10},{10... | collective-permute-start | bytes 49160 | tf_op jit(solution)/shard_map/ppermute | solution.py:37
  24.4 3.4 %collective-permute-start.4 = (f32[2,8,128]{2,1,0:T(8,128)S(1)}, f32[2,8,128]{2,1,0:T(8,128)S(1)}, u32[]{:S(2)}, u32[]{:S(2)}) collective-permute-start(f32[2,8,128]{2,1,0:T(8,128)S(1)} %slice_bitcast_fusion.2), channel_id=1, source_target_pairs={{0,16},{8,24},{16,0},{24,8},{1,17},{9,25},{17,1},{25,9},{2,18},{10... | collective-permute-start | bytes 24584 | tf_op jit(solution)/shard_map/ppermute | solution.py:39
  27.8 3.1 %copy-start.1 = (bf16[7,64,4096]{2,1,0:T(8,128)(2,1)S(1)}, bf16[7,64,4096]{2,1,0:T(8,128)(2,1)}, u32[]{:S(2)}) copy-start(bf16[7,64,4096]{2,1,0:T(8,128)(2,1)} %param.5) | copy-start | bytes 11010052
  37.0 27.7 %all-to-all-start.1 = ((bf16[16,192,128]{2,1,0:T(8,128)(2,1)}), bf16[16,192,128]{2,1,0:T(8,128)(2,1)S(1)}, u32[]{:S(2)}, u32[]{:S(2)}) async-start(bf16[16,192,128]{2,1,0:T(8,128)(2,1)} %reshape.126), calls=%async_computation.1 | async-start | bytes 1572864 | tf_op jit(solution)/shard_map/all_to_all | solution.py:126

commit v2 on v1

v2 whole, which is shorter than its diff:
```python
import functools

import jax
import jax.numpy as jnp
from jax import lax
from jax.experimental import pallas as pl
from jax.experimental.pallas import tpu as pltpu
from jax.sharding import PartitionSpec as P

BASIS = 64
CELLS = 8
RIM = 4
EXT = 16
EXT3 = 4096
LANES = 128

XC_COEF = 0.9847450218426965
GRID_WEIGHT = 0.015625


def slater_potential(density):
    return -XC_COEF * density / jnp.cbrt(density * density + 1.0)


def neighbour_swaps(count, first):
    pairs = []
    for low in range(first, count + first, 2):
        left, right = low % count, (low + 1) % count
        pairs += [(left, right), (right, left)]
    return pairs


def merged(low, high, axis, forward=False):
    count = lax.axis_size(axis)
    if count == 2:
        got = lax.ppermute(jnp.stack([high, low]), axis, neighbour_swaps(count, 0))
        return low + got[0], high + got[1]
    odd = lax.axis_index(axis) % 2 == 1
    near, far = jnp.where(odd, low, high), jnp.where(odd, high, low)
    if forward and count == 4:
        got = lax.ppermute(jnp.stack([near, far]), axis, neighbour_swaps(count, 0))
        near = near + got[0]
        far = far + lax.ppermute(got[1], axis, [(i, i ^ 2) for i in range(count)])
    else:
        got = lax.ppermute(near, axis, neighbour_swaps(count, 0))
        other = lax.ppermute(far, axis, neighbour_swaps(count, 1))
        near, far = near + got, far + other
    return jnp.where(odd, near, far), jnp.where(odd, far, near)


def merged_z(box, swapped, axis):
    count = lax.axis_size(axis)
    if count == 2:
        return box + lax.ppermute(swapped, axis, neighbour_swaps(count, 0))
    odd = lax.axis_index(axis) % 2 == 1
    lane = lax.broadcasted_iota(jnp.int32, box.shape, box.ndim - 1)
    in_high = lane % EXT >= EXT // 2
    first = lax.ppermute(swapped, axis, neighbour_swaps(count, 0))
    second = lax.ppermute(swapped, axis, neighbour_swaps(count, 1))
    return box + jnp.where(in_high != odd, first, second)


def collocate_kernel(groups, pair_groups, blocks, basis, box, swapped, table, spread, matrix, arrived):
    rows = groups * BASIS
    chunk = 2 * EXT * EXT
    copies = []
    for c in range(EXT3 // chunk):
        cells = pl.ds(c * chunk, chunk)
        copies.append(
            pltpu.make_async_copy(basis.at[:, cells], table.at[:, cells], arrived.at[c])
        )
        copies[-1].start()
    pairs = blocks.shape[0]
    in_low = lax.broadcasted_iota(jnp.int32, (pairs, LANES), 1) < BASIS
    for j in range(BASIS // 2):
        two_rows = blocks[:, j * LANES : (j + 1) * LANES].astype(jnp.float32)
        turned = pltpu.roll(two_rows, BASIS, axis=1)
        spread[pl.ds(2 * j, pairs, stride=BASIS), :] = jnp.where(in_low, two_rows, turned)
        spread[pl.ds(2 * j + 1, pairs, stride=BASIS), :] = jnp.where(in_low, turned, two_rows)
    matrix[...] = jnp.zeros_like(matrix)
    half_of_lane = lax.broadcasted_iota(jnp.int32, (BASIS, LANES), 1) // BASIS

    def place(p, carry):
        first, second = pair_groups[0, p], pair_groups[1, p]
        at = (
            pl.ds(pl.multiple_of(first * BASIS, BASIS), BASIS),
            pl.ds(pl.multiple_of((second // 2) * LANES, LANES), LANES),
        )
        block = spread[pl.ds(pl.multiple_of(p * BASIS, BASIS), BASIS), :]
        matrix[at] = jnp.where(half_of_lane == second % 2, block, matrix[at])
        return carry

    lax.fori_loop(0, pairs, place, 0)
    dense = matrix[:, :rows].astype(jnp.bfloat16)
    for c in range(EXT3 // chunk):
        copies[c].wait()
        values = table[:, c * chunk : (c + 1) * chunk]
        projected = jnp.dot(dense, values, preferred_element_type=jnp.float32)
        summed = jnp.sum(values.astype(jnp.float32) * projected, axis=0, keepdims=True)
        for t in range(chunk // LANES):
            box[t % 2, 2 * c + t // 2, :] = summed[0, t * LANES : (t + 1) * LANES]
    lane = lax.broadcasted_iota(jnp.int32, (EXT, LANES), 1)
    for half in range(2):
        cells = box[half]
        swapped[half] = jnp.where(
            lane % EXT < EXT // 2,
            pltpu.roll(cells, LANES - EXT // 2, axis=1),
            pltpu.roll(cells, EXT // 2, axis=1),
        )


def collocated(basis, density_blocks, pair_groups):
    groups, pairs = basis.shape[0], density_blocks.shape[0]
    rows = groups * BASIS
    vmem, smem = pl.BlockSpec(memory_space=pltpu.VMEM), pl.BlockSpec(memory_space=pltpu.SMEM)
    return pl.pallas_call(
        functools.partial(collocate_kernel, groups),
        name="collocate",
        out_shape=(
            jax.ShapeDtypeStruct((2, EXT, LANES), jnp.float32),
            jax.ShapeDtypeStruct((2, EXT, LANES), jnp.float32),
            jax.ShapeDtypeStruct((rows, EXT3), basis.dtype),
        ),
        in_specs=[smem, vmem, pl.BlockSpec(memory_space=pl.ANY)],
        out_specs=[vmem, vmem, vmem],
        scratch_shapes=[
            pltpu.VMEM((pairs * BASIS, LANES), jnp.float32),
            pltpu.VMEM((rows, -(-rows // LANES) * LANES), jnp.float32),
            pltpu.SemaphoreType.DMA((EXT // 2,)),
        ],
        compiler_params=pltpu.CompilerParams(vmem_limit_bytes=24 << 20),
        cost_estimate=pl.CostEstimate(
            flops=2 * rows * rows * EXT3, bytes_accessed=2 * rows * EXT3, transcendentals=0
        ),
    )(pair_groups, density_blocks, basis.reshape(rows, EXT3))


def integrate_kernel(groups, capacity, pair_groups, places, potential, slots, table, send, total):
    rows = groups * BASIS
    pairs = places.shape[1]
    lines = BASIS // 2
    chunk = 4 * EXT * EXT
    for c in range(EXT3 // chunk):
        values = table[:, c * chunk : (c + 1) * chunk]
        weight = jnp.concatenate(
            [
                potential[t % 2, chunk // (2 * LANES) * c + t // 2 : chunk // (2 * LANES) * c + t // 2 + 1, :]
                for t in range(chunk // LANES)
            ],
            axis=1,
        )
        weighted = (values.astype(jnp.float32) * weight).astype(jnp.bfloat16)
        part = lax.dot_general(
            weighted, values, (((1,), (1,)), ((), ())), preferred_element_type=jnp.float32
        )
        if c == 0:
            total[:, :rows] = part
        else:
            total[:, :rows] += part
    send[:, capacity * lines :, :] = slots[...]
    in_low = lax.broadcasted_iota(jnp.int32, (lines, LANES), 1) < BASIS

    def place(p, carry):
        first, second = pair_groups[0, p], pair_groups[1, p]
        block = total[
            pl.ds(pl.multiple_of(first * BASIS, BASIS), BASIS),
            pl.ds(pl.multiple_of((second // 2) * LANES, LANES), LANES),
        ]
        turned = pltpu.roll(block, BASIS, axis=1)
        is_low = second % 2 == 0
        upper = jnp.where(is_low, block[:lines], turned[:lines])
        lower = jnp.where(is_low, turned[lines:], block[lines:])
        line = pl.multiple_of(places[1, p] * lines, lines)
        send[places[0, p], pl.ds(line, lines), :] = (
            jnp.where(in_low, upper, lower) * GRID_WEIGHT
        ).astype(send.dtype)
        return carry

    lax.fori_loop(0, pairs, place, 0)


def integrated(table, potential, slots, pair_groups, places, owners, capacity):
    rows = table.shape[0]
    vmem, smem = pl.BlockSpec(memory_space=pltpu.VMEM), pl.BlockSpec(memory_space=pltpu.SMEM)
    return pl.pallas_call(
        functools.partial(integrate_kernel, rows // BASIS, capacity),
        name="integrate",
        out_shape=jax.ShapeDtypeStruct(
            (owners, capacity * BASIS // 2 + slots.shape[1], LANES), jnp.bfloat16
        ),
        in_specs=[smem, smem, vmem, vmem, vmem],
        out_specs=vmem,
        scratch_shapes=[pltpu.VMEM((rows, -(-rows // LANES) * LANES), jnp.float32)],
        compiler_params=pltpu.CompilerParams(vmem_limit_bytes=24 << 20),
        cost_estimate=pl.CostEstimate(
            flops=2 * rows * rows * EXT3, bytes_accessed=2 * rows * EXT3, transcendentals=0
        ),
    )(pair_groups, places, potential, slots, table)


def store_kernel(capacity, got, store, total, slots_vector, slots, moved):
    lines = BASIS // 2
    sources = got.shape[0]
    stored = store.shape[0]
    for s in range(sources):
        slots_vector[s : s + 1, :] = (
            got[s, capacity * lines : capacity * lines + 8, :].astype(jnp.float32)[:1].astype(jnp.int32)
        )
    copy = pltpu.make_async_copy(slots_vector, slots, moved)
    copy.start()
    total[...] = jnp.zeros_like(total)
    copy.wait()

    def add(s, carry):
        for r in range(capacity):
            at = pl.ds(pl.multiple_of(slots[s, r] * lines, lines), lines)
            total[at, :] += got[s, r * lines : (r + 1) * lines, :].astype(jnp.float32)
        return carry

    lax.fori_loop(0, sources, add, 0)
    in_low = lax.broadcasted_iota(jnp.int32, (stored, LANES), 1) < BASIS
    for i in range(lines // 2):
        even = total[pl.ds(2 * i, stored, stride=lines), :]
        odd = total[pl.ds(2 * i + 1, stored, stride=lines), :]
        for j, row in (
            (i, jnp.where(in_low, even, pltpu.roll(odd, BASIS, axis=1))),
            (i + lines // 2, jnp.where(in_low, pltpu.roll(even, BASIS, axis=1), odd)),
        ):
            store[:, j * LANES : (j + 1) * LANES] = row.astype(store.dtype)


def stored_blocks(got, rows, capacity):
    vmem = pl.BlockSpec(memory_space=pltpu.VMEM)
    return pl.pallas_call(
        functools.partial(store_kernel, capacity),
        name="store",
        out_shape=jax.ShapeDtypeStruct((rows, BASIS * BASIS), jnp.bfloat16),
        in_specs=[vmem],
        out_specs=vmem,
        scratch_shapes=[
            pltpu.VMEM(((rows + 1) * BASIS // 2, LANES), jnp.float32),
            pltpu.VMEM((got.shape[0], LANES), jnp.int32),
            pltpu.SMEM((got.shape[0], LANES), jnp.int32),
            pltpu.SemaphoreType.DMA(()),
        ],
        compiler_params=pltpu.CompilerParams(vmem_limit_bytes=24 << 20),
        cost_estimate=pl.CostEstimate(
            flops=got.size, bytes_accessed=2 * got.size, transcendentals=0
        ),
    )(got)


def per_device(basis, density_blocks, pair_groups, owner, owner_slot):
    pairs = density_blocks.shape[0]
    owners = lax.axis_size("gx") * lax.axis_size("gy")
    capacity = max(2, 2 * pairs // owners)
    box, swapped, table = collocated(basis, density_blocks, pair_groups)

    owner_ids = owner[:, 0]
    order_ids = jnp.arange(pairs, dtype=jnp.int32)
    earlier = (owner_ids[:, None] == owner_ids[None, :]) & (order_ids[:, None] > order_ids[None, :])
    rank_within = jnp.sum(earlier.astype(jnp.int32), axis=1)
    places = jnp.stack([owner_ids, rank_within])
    lane_ids = jnp.arange(LANES, dtype=jnp.int32)
    chosen = (jnp.arange(owners, dtype=jnp.int32)[:, None, None] == owner_ids[None, None, :]) & (
        lane_ids[None, :, None] == rank_within[None, None, :]
    )
    slots = jnp.sum(jnp.where(chosen, owner_slot[None, None, :] - pairs, 0), axis=2) + pairs
    slots = jnp.broadcast_to(slots.astype(jnp.bfloat16)[:, None, :], (owners, 8, LANES))

    box = merged_z(box, swapped, "gz")
    y_low, y_high = merged(box[0], box[1], "gy")
    box = jnp.stack([y_low, y_high])
    x_low, x_high = merged(box[:, : EXT // 2], box[:, EXT // 2 :], "gx", forward=True)
    potential_ext = slater_potential(jnp.concatenate([x_low, x_high], axis=1))
    potential = potential_ext.reshape(2, EXT, EXT // 2, EXT)[:, RIM : RIM + CELLS, :, RIM : RIM + CELLS]
    potential = jnp.concatenate([potential[0, :, RIM:], potential[1, :, :RIM]], axis=1)

    send = integrated(table, potential_ext, slots, pair_groups, places, owners, capacity)
    got = lax.all_to_all(send, ("gx", "gy"), split_axis=0, concat_axis=0, tiled=True)
    return stored_blocks(got, pairs, capacity), potential


def solution(mesh):
    return jax.shard_map(
        per_device,
        mesh=mesh,
        in_specs=(
            P(("gx", "gy", "gz"), None, None),
            P(("gx", "gy", "gz"), None),
            P(None, ("gx", "gy", "gz")),
            P(("gx", "gy", "gz"), None),
            P(("gx", "gy", "gz")),
        ),
        out_specs=(P(("gx", "gy", "gz"), None), P("gx", "gy", "gz")),
        check_vma=False,
    )
```

time: 66.3 us -> 67.5 us (1.018)
  Pallas kernels: 0 us -> 16.6 us
  matrix products: 9.17 us -> 0 us
  starting transfers between devices: 20.1 us -> 14.9 us
  other arithmetic: 5.77 us -> 1.31 us
  waiting for transfers between devices: 22.4 us -> 25.6 us
    pallas_call x0 -> x3, Pallas kernels: none -> 16.6 us  [the longest x1 7.32 us: integrated(): pl.pallas_call(functools.partial(integrate_kernel, rows // BASIS, capacit...]
    dot_general x5 -> x0, matrix products: 9.17 us -> none  [the longest x1 5.25 us: per_device(): projected = jnp.dot(matrix, stacked, preferred_element_type=jnp.float32)]
    unnamed x9 -> x17, local copies, waits for them, and re-layouts: 0.33 us -> 7.56 us
    all_to_all x2 -> x1, starting transfers between devices: 13.6 us -> 8.25 us  [per_device(): lax.all_to_all(send, ('gx', 'gy'), split_axis=0, concat_axis=0, tiled=True)]
    reshape x7 -> x0, local copies, waits for them, and re-layouts: 4.65 us -> none  [the longest x2 1.42 us: per_device(): dense_blocks.reshape(groups, groups, BASIS, BASIS).transpose(0, 2, 1, 3)]
    convert_element_type x1, other arithmetic: 3.08 us -> 0.01 us  [per_device(): slots.astype(jnp.bfloat16)[:, None, :]]
    all_to_all x2 -> x1, waiting for transfers between devices: 17.3 us -> 19.2 us  [per_device(): lax.all_to_all(send, ('gx', 'gy'), split_axis=0, concat_axis=0, tiled=True)]
    ppermute x1, starting transfers between devices: 0.01 us -> 1.89 us  [merged(): got = lax.ppermute(near, axis, neighbour_swaps(count, 0))]
  transfers between devices with their start and end apart: 7 -> 6, of which waited for: 4 -> 5; matrix products, arithmetic and copies ran while one was open for 19% -> 2% of each run, Pallas kernels for 0% -> 0%
where the time goes in v2:
time: 67.5 us; the launch traced here: 67.1 us
  waiting for transfers between devices  25.6 us (38%)
  Pallas kernels  16.6 us (25%)
  starting transfers between devices  14.9 us (22%)
  local copies, waits for them, and re-layouts  7.8 us (12%)
  other arithmetic  1.31 us (2%)
  between operations  0.84 us (1%)
    all_to_all x1, waiting for transfers between devices, per_device(): lax.all_to_all(send, ('gx', 'gy'), split_axis=0, concat_axis=0, tiled=True)  19.2 us
    all_to_all x1, starting transfers between devices, per_device(): lax.all_to_all(send, ('gx', 'gy'), split_axis=0, concat_axis=0, tiled=True)  8.25 us
    unnamed x17, local copies, waits for them, and re-layouts  7.56 us
    pallas_call x1, Pallas kernels, integrated(): pl.pallas_call(functools.partial(integrate_kernel, rows // BASIS, capacit...  7.32 us
    pallas_call x1, Pallas kernels, collocated(): pl.pallas_call(functools.partial(collocate_kernel, groups), name='colloca...  6.8 us
    ppermute x1, waiting for transfers between devices, merged(): got = lax.ppermute(jnp.stack([near, far]), axis, neighbour_swaps(count, 0))  2.56 us
    pallas_call x1, Pallas kernels, stored_blocks(): pl.pallas_call(functools.partial(store_kernel, capacity), name='store', o...  2.47 us
    ppermute x1, starting transfers between devices, merged(): far = far + lax.ppermute(got[1], axis, [(i, i ^ 2) for i in range(count)])  2.31 us
  transfers between devices with their start and end apart: 6, of which 5 were waited for; matrix products, arithmetic and copies ran while one was open for 2% of the time, Pallas kernels for 0%

profile of v2, /device:TPU:9, one launch (start us, length us, event | category | flops | bytes accessed | tf_op | source)
XLA Modules:
  0.0 67.1 jit_solution(17648857760706970399)
XLA Ops:
  0.7 2.0 %copy-done = bf16[7,64,4096]{2,1,0:T(8,128)(2,1)S(1)} copy-done((bf16[7,64,4096]{2,1,0:T(8,128)(2,1)S(1)}, bf16[7,64,4096]{2,1,0:T(8,128)(2,1)}, u32[]{:S(2)}) %copy-start) | copy-done | bytes 3670040
  2.7 1.0 %copy-done.1 = bf16[48,4096]{1,0:T(8,128)(2,1)S(1)} copy-done((bf16[48,4096]{1,0:T(8,128)(2,1)S(1)}, bf16[48,4096]{1,0:T(8,128)(2,1)}, u32[]{:S(2)}) %copy-start.1) | copy-done | bytes 393240
  3.7 0.7 %copy-done.2 = s32[2,48]{1,0:T(2,128)S(1)} copy-done((s32[2,48]{1,0:T(2,128)S(1)}, s32[2,48]{1,0:T(2,128)}, u32[]{:S(2)}) %copy-start.2) | copy-done | bytes 408
  4.4 6.8 %collocate.1 = (f32[2,16,128]{2,1,0:T(8,128)S(1)}, f32[2,16,128]{2,1,0:T(8,128)S(1)}, bf16[448,4096]{1,0:T(8,128)(2,1)S(1)}) custom-call(s32[2,48]{1,0:T(2,128)S(1)} %copy-done.2, bf16[48,4096]{1,0:T(8,128)(2,1)S(1)} %copy-done.1, bf16[448,4096]{1,0:T(8,128)(2,1)S(1)} %bitcast.30), custom_call_target="tpu_custom_call" | custom-call | flops 1644167168 | bytes 3670016 | tf_op jit(solution)/shard_map/collocate/pallas_call | solution.py:116
  11.2 1.8 %copy-done.4 = bf16[448,4096]{1,0:T(8,128)(2,1)} copy-done((bf16[448,4096]{1,0:T(8,128)(2,1)}, bf16[448,4096]{1,0:T(8,128)(2,1)S(1)}, u32[]{:S(2)}) %copy-start.4) | copy-done | bytes 3670040
  13.0 1.2 %collective-permute-start = (f32[2,16,128]{2,1,0:T(8,128)S(1)}, f32[2,16,128]{2,1,0:T(8,128)S(1)}, u32[]{:S(2)}, u32[]{:S(2)}) collective-permute-start(f32[2,16,128]{2,1,0:T(8,128)S(1)} %get-tuple-element.6), channel_id=1, source_target_pairs={{0,1},{1,0},{2,3},{3,2},{4,5},{5,4},{6,7},{7,6},{8,9},{9,8},{10,11... | collective-permute-start | bytes 49160 | tf_op jit(solution)/shard_map/ppermute | solution.py:54
  14.2 0.2 convert_reduce_fusion
  14.5 1.0 %collective-permute-done = f32[2,16,128]{2,1,0:T(8,128)S(1)} collective-permute-done((f32[2,16,128]{2,1,0:T(8,128)S(1)}, f32[2,16,128]{2,1,0:T(8,128)S(1)}, u32[]{:S(2)}, u32[]{:S(2)}) %collective-permute-start) | collective-permute-done | bytes 16416 | tf_op jit(solution)/shard_map/ppermute | solution.py:54
  15.6 1.9 %collective-permute-start.1 = (f32[16,128]{1,0:T(8,128)S(1)}, f32[16,128]{1,0:T(8,128)S(1)}, u32[]{:S(2)}, u32[]{:S(2)}) collective-permute-start(f32[16,128]{1,0:T(8,128)S(1)} %get-tuple-element.17), channel_id=1, source_target_pairs={{0,2},{2,0},{4,6},{6,4},{1,3},{3,1},{5,7},{7,5},{8,10},{10,8},{12,... | collective-permute-start | bytes 24584 | tf_op jit(solution)/shard_map/ppermute | solution.py:45
  17.5 1.2 %collective-permute-start.2 = (f32[16,128]{1,0:T(8,128)S(1)}, f32[16,128]{1,0:T(8,128)S(1)}, u32[]{:S(2)}, u32[]{:S(2)}) collective-permute-start(f32[16,128]{1,0:T(8,128)S(1)} %get-tuple-element.18), channel_id=1, source_target_pairs={{2,4},{4,2},{6,0},{0,6},{3,5},{5,3},{7,1},{1,7},{10,12},{12,10},{1... | collective-permute-start | bytes 24584 | tf_op jit(solution)/shard_map/ppermute | solution.py:46
  18.6 0.2 select_reduce_fusion
  18.9 1.7 %collective-permute-done.2 = f32[16,128]{1,0:T(8,128)S(1)} collective-permute-done((f32[16,128]{1,0:T(8,128)S(1)}, f32[16,128]{1,0:T(8,128)S(1)}, u32[]{:S(2)}, u32[]{:S(2)}) %collective-permute-start.2) | collective-permute-done | bytes 8224 | tf_op jit(solution)/shard_map/ppermute | solution.py:46
  20.7 2.6 %collective-permute-done.3 = f32[2,2,8,128]{3,2,1,0:T(8,128)S(1)} collective-permute-done((f32[2,2,8,128]{3,2,1,0:T(8,128)S(1)}, f32[2,2,8,128]{3,2,1,0:T(8,128)S(1)}, u32[]{:S(2)}, u32[]{:S(2)}) %collective-permute-start.3) | collective-permute-done | bytes 16416 | tf_op jit(solution)/shard_map/ppermute | solution.py:41
  23.2 2.3 %collective-permute-start.4 = (f32[2,8,128]{2,1,0:T(8,128)S(1)}, f32[2,8,128]{2,1,0:T(8,128)S(1)}, u32[]{:S(2)}, u32[]{:S(2)}) collective-permute-start(f32[2,8,128]{2,1,0:T(8,128)S(1)} %slice_bitcast_fusion.2), channel_id=1, source_target_pairs={{0,16},{8,24},{16,0},{24,8},{1,17},{9,25},{17,1},{25,9},{2,18},{10... | collective-permute-start | bytes 24584 | tf_op jit(solution)/shard_map/ppermute | solution.py:43
  25.6 1.1 %collective-permute-done.4 = f32[2,8,128]{2,1,0:T(8,128)S(1)} collective-permute-done((f32[2,8,128]{2,1,0:T(8,128)S(1)}, f32[2,8,128]{2,1,0:T(8,128)S(1)}, u32[]{:S(2)}, u32[]{:S(2)}) %collective-permute-start.4) | collective-permute-done | bytes 8224 | tf_op jit(solution)/shard_map/ppermute | solution.py:43
  26.7 2.0 %copy-done.5 = bf16[448,4096]{1,0:T(8,128)(2,1)S(1)} copy-done((bf16[448,4096]{1,0:T(8,128)(2,1)S(1)}, bf16[448,4096]{1,0:T(8,128)(2,1)}, u32[]{:S(2)}) %copy-start.5) | copy-done | bytes 3670040
  28.8 7.3 %integrate.1 = bf16[16,200,128]{2,1,0:T(8,128)(2,1)} custom-call(s32[2,48]{1,0:T(2,128)S(1)} %copy-done.3, s32[2,48]{1,0:T(2,128)S(1)} %pad_add_fusion.places, f32[2,16,128]{2,1,0:T(8,128)S(1)} %cbrt_divide_fusion.1.potential, bf16[16,8,128]{2,1,0:T(8,128)(2,1)S(1)} %broadcast_in_dim.16.slots, bf16[448,4096]{1,0:T(8,128)(2,1)S(1)} %copy-done.5), custom_call_target="tpu_custom_call" | custom-call | flops 1644167168 | bytes 3670016 | tf_op jit(solution)/shard_map/integrate/pallas_call | solution.py:185
  36.1 8.3 %all-to-all-start = ((bf16[16,200,128]{2,1,0:T(8,128)(2,1)}), bf16[16,200,128]{2,1,0:T(8,128)(2,1)S(1)}, u32[]{:S(2)}, u32[]{:S(2)}) async-start(bf16[16,200,128]{2,1,0:T(8,128)(2,1)} %integrate.1), calls=%async_computation | async-start | bytes 1638400 | tf_op jit(solution)/shard_map/all_to_all | solution.py:280
  44.4 0.1 concatenate.15
  44.5 0.1 cbrt_divide_fusion
  44.7 0.1 slice_bitcast_fusion.1
  44.7 0.6 pad_maximum_fusion
  45.4 19.2 %all-to-all-done.got = bf16[16,200,128]{2,1,0:T(8,128)(2,1)S(1)} async-done(((bf16[16,200,128]{2,1,0:T(8,128)(2,1)}), bf16[16,200,128]{2,1,0:T(8,128)(2,1)S(1)}, u32[]{:S(2)}, u32[]{:S(2)}) %all-to-all-start) | async-done | bytes 819232 | tf_op jit(solution)/shard_map/all_to_all | solution.py:280
  64.6 2.5 %store.1 = bf16[48,4096]{1,0:T(8,128)(2,1)} custom-call(bf16[16,200,128]{2,1,0:T(8,128)(2,1)S(1)} %all-to-all-done.got), custom_call_target="tpu_custom_call" | custom-call | flops 409600 | bytes 819200 | tf_op jit(solution)/shard_map/store/pallas_call | solution.py:234
  (31 shorter events, 0.4 us)
Async XLA Ops:
  0.6 26.1 %copy-start.3 = (s32[2,48]{1,0:T(2,128)S(1)}, s32[2,48]{1,0:T(2,128)}, u32[]{:S(2)}) copy-start(s32[2,48]{1,0:T(2,128)} %pair_groups.3) | copy-start | bytes 1156
  0.6 13.6 %copy-start.6 = (s32[48,1]{0,1:T(1,128)S(1)}, s32[48,1]{0,1:T(1,128)}, u32[]{:S(2)}) copy-start(s32[48,1]{0,1:T(1,128)} %param.8) | copy-start | bytes 580
  0.7 2.1 %copy-start = (bf16[7,64,4096]{2,1,0:T(8,128)(2,1)S(1)}, bf16[7,64,4096]{2,1,0:T(8,128)(2,1)}, u32[]{:S(2)}) copy-start(bf16[7,64,4096]{2,1,0:T(8,128)(2,1)} %param.5) | copy-start | bytes 11010052
  2.7 1.0 %copy-start.1 = (bf16[48,4096]{1,0:T(8,128)(2,1)S(1)}, bf16[48,4096]{1,0:T(8,128)(2,1)}, u32[]{:S(2)}) copy-start(bf16[48,4096]{1,0:T(8,128)(2,1)} %blocks.1) | copy-start | bytes 1179652
  3.7 0.7 %copy-start.2 = (s32[2,48]{1,0:T(2,128)S(1)}, s32[2,48]{1,0:T(2,128)}, u32[]{:S(2)}) copy-start(s32[2,48]{1,0:T(2,128)} %pair_groups.3) | copy-start | bytes 1156
  4.4 10.1 %copy-start.7 = (s32[48]{0:T(128)S(1)}, s32[48]{0:T(128)}, u32[]{:S(2)}) copy-start(s32[48]{0:T(128)} %param.9) | copy-start | bytes 580
  11.2 1.8 %copy-start.4 = (bf16[448,4096]{1,0:T(8,128)(2,1)}, bf16[448,4096]{1,0:T(8,128)(2,1)S(1)}, u32[]{:S(2)}) copy-start(bf16[448,4096]{1,0:T(8,128)(2,1)S(1)} %get-tuple-element.7.table) | copy-start | bytes 11010052
  13.0 2.6 %collective-permute-start = (f32[2,16,128]{2,1,0:T(8,128)S(1)}, f32[2,16,128]{2,1,0:T(8,128)S(1)}, u32[]{:S(2)}, u32[]{:S(2)}) collective-permute-start(f32[2,16,128]{2,1,0:T(8,128)S(1)} %get-tuple-element.6), channel_id=1, source_target_pairs={{0,1},{1,0},{2,3},{3,2},{4,5},{5,4},{6,7},{7,6},{8,9},{9,8},{10,11... | collective-permute-start | bytes 49160 | tf_op jit(solution)/shard_map/ppermute | solution.py:54
  15.6 3.3 %collective-permute-start.1 = (f32[16,128]{1,0:T(8,128)S(1)}, f32[16,128]{1,0:T(8,128)S(1)}, u32[]{:S(2)}, u32[]{:S(2)}) collective-permute-start(f32[16,128]{1,0:T(8,128)S(1)} %get-tuple-element.17), channel_id=1, source_target_pairs={{0,2},{2,0},{4,6},{6,4},{1,3},{3,1},{5,7},{7,5},{8,10},{10,8},{12,... | collective-permute-start | bytes 24584 | tf_op jit(solution)/shard_map/ppermute | solution.py:45
  17.5 3.1 %collective-permute-start.2 = (f32[16,128]{1,0:T(8,128)S(1)}, f32[16,128]{1,0:T(8,128)S(1)}, u32[]{:S(2)}, u32[]{:S(2)}) collective-permute-start(f32[16,128]{1,0:T(8,128)S(1)} %get-tuple-element.18), channel_id=1, source_target_pairs={{2,4},{4,2},{6,0},{0,6},{3,5},{5,3},{7,1},{1,7},{10,12},{12,10},{1... | collective-permute-start | bytes 24584 | tf_op jit(solution)/shard_map/ppermute | solution.py:46
  20.6 2.7 %collective-permute-start.3 = (f32[2,2,8,128]{3,2,1,0:T(8,128)S(1)}, f32[2,2,8,128]{3,2,1,0:T(8,128)S(1)}, u32[]{:S(2)}, u32[]{:S(2)}) collective-permute-start(f32[2,2,8,128]{3,2,1,0:T(8,128)S(1)} %pad_maximum_fusion.1), channel_id=1, source_target_pairs={{0,8},{8,0},{16,24},{24,16},{1,9},{9,1},{17,25},{25,17},{2,10},{10... | collective-permute-start | bytes 49160 | tf_op jit(solution)/shard_map/ppermute | solution.py:41
  23.2 3.4 %collective-permute-start.4 = (f32[2,8,128]{2,1,0:T(8,128)S(1)}, f32[2,8,128]{2,1,0:T(8,128)S(1)}, u32[]{:S(2)}, u32[]{:S(2)}) collective-permute-start(f32[2,8,128]{2,1,0:T(8,128)S(1)} %slice_bitcast_fusion.2), channel_id=1, source_target_pairs={{0,16},{8,24},{16,0},{24,8},{1,17},{9,25},{17,1},{25,9},{2,18},{10... | collective-permute-start | bytes 24584 | tf_op jit(solution)/shard_map/ppermute | solution.py:43
  26.7 2.0 %copy-start.5 = (bf16[448,4096]{1,0:T(8,128)(2,1)S(1)}, bf16[448,4096]{1,0:T(8,128)(2,1)}, u32[]{:S(2)}) copy-start(bf16[448,4096]{1,0:T(8,128)(2,1)} %copy-done.4) | copy-start | bytes 11010052
  36.1 28.5 %all-to-all-start = ((bf16[16,200,128]{2,1,0:T(8,128)(2,1)}), bf16[16,200,128]{2,1,0:T(8,128)(2,1)S(1)}, u32[]{:S(2)}, u32[]{:S(2)}) async-start(bf16[16,200,128]{2,1,0:T(8,128)(2,1)} %integrate.1), calls=%async_computation | async-start | bytes 1638400 | tf_op jit(solution)/shard_map/all_to_all | solution.py:280

commit v3 on v2

v3 whole, which is shorter than its diff:
```python
import functools

import jax
import jax.numpy as jnp
from jax import lax
from jax.experimental import pallas as pl
from jax.experimental.pallas import tpu as pltpu
from jax.sharding import PartitionSpec as P

BASIS = 64
CELLS = 8
RIM = 4
EXT = 16
EXT3 = 4096
LANES = 128

XC_COEF = 0.9847450218426965
GRID_WEIGHT = 0.015625


def slater_potential(density):
    return -XC_COEF * density / jnp.cbrt(density * density + 1.0)


def neighbour_swaps(count, first):
    pairs = []
    for low in range(first, count + first, 2):
        left, right = low % count, (low + 1) % count
        pairs += [(left, right), (right, left)]
    return pairs


def merged(low, high, axis, forward=False):
    count = lax.axis_size(axis)
    if count == 2:
        got = lax.ppermute(jnp.stack([high, low]), axis, neighbour_swaps(count, 0))
        return low + got[0], high + got[1]
    odd = lax.axis_index(axis) % 2 == 1
    near, far = jnp.where(odd, low, high), jnp.where(odd, high, low)
    if forward and count == 4:
        got = lax.ppermute(jnp.stack([near, far]), axis, neighbour_swaps(count, 0))
        near = near + got[0]
        far = far + lax.ppermute(got[1], axis, [(i, i ^ 2) for i in range(count)])
    else:
        got = lax.ppermute(near, axis, neighbour_swaps(count, 0))
        other = lax.ppermute(far, axis, neighbour_swaps(count, 1))
        near, far = near + got, far + other
    return jnp.where(odd, near, far), jnp.where(odd, far, near)


def merged_z(box, swapped, axis):
    count = lax.axis_size(axis)
    if count == 2:
        return box + lax.ppermute(swapped, axis, neighbour_swaps(count, 0))
    odd = lax.axis_index(axis) % 2 == 1
    lane = lax.broadcasted_iota(jnp.int32, box.shape, box.ndim - 1)
    in_high = lane % EXT >= EXT // 2
    first = lax.ppermute(swapped, axis, neighbour_swaps(count, 0))
    second = lax.ppermute(swapped, axis, neighbour_swaps(count, 1))
    return box + jnp.where(in_high != odd, first, second)


def resident_cells():
    return 8 * EXT * EXT


def fetches(basis, head, tail, arrived, chunk, first):
    kept = head.shape[1]
    copies = []
    for c in range(first, EXT3 // chunk):
        source = basis.at[:, pl.ds(c * chunk, chunk)]
        begin = c * chunk if c * chunk < kept else c * chunk - kept
        place = (head if c * chunk < kept else tail).at[:, pl.ds(begin, chunk)]
        copies.append((pltpu.make_async_copy(source, place, arrived.at[c]), place))
    return copies


def collocate_kernel(
    groups, pair_groups, blocks, basis, box, swapped, head,
    tail, codes, local, spread, matrix, owner_of, arrived, staged,
):
    pairs = blocks.shape[0]
    pitch = BASIS + 1
    codes_copy = pltpu.make_async_copy(pair_groups, codes, staged.at[0])
    blocks_copy = pltpu.make_async_copy(blocks, local, staged.at[1])
    codes_copy.start()
    blocks_copy.start()
    copies = fetches(basis, head, tail, arrived, 2 * EXT * EXT, 0)
    for copy, _ in copies:
        copy.start()
    spread[pl.ds(pairs * pitch, BASIS), :] = jnp.zeros((BASIS, LANES), jnp.float32)
    codes_copy.wait()
    for code in range(groups * groups):
        owner_of[code] = pairs
    for p in range(pairs):
        owner_of[codes[0, p] * groups + codes[1, p]] = p
    blocks_copy.wait()
    in_low = lax.broadcasted_iota(jnp.int32, (pairs, LANES), 1) < BASIS
    for j in range(BASIS // 2):
        two_rows = local[:, j * LANES : (j + 1) * LANES].astype(jnp.float32)
        turned = pltpu.roll(two_rows, BASIS, axis=1)
        spread[pl.ds(2 * j, pairs, stride=pitch), :] = jnp.where(in_low, two_rows, turned)
        spread[pl.ds(2 * j + 1, pairs, stride=pitch), :] = jnp.where(in_low, turned, two_rows)
    left = lax.broadcasted_iota(jnp.int32, (BASIS, LANES), 1) < BASIS
    for first in range(groups):
        for second in range(0, groups, 2):
            code = first * groups + second
            block = spread[pl.ds(owner_of[code] * pitch, BASIS), :]
            if second + 1 < groups:
                block = jnp.where(left, block, spread[pl.ds(owner_of[code + 1] * pitch, BASIS), :])
            matrix[
                first * BASIS : (first + 1) * BASIS, second * BASIS : second * BASIS + LANES
            ] = block.astype(matrix.dtype)
    dense = matrix[:, : groups * BASIS]
    for c, (copy, place) in enumerate(copies):
        copy.wait()
        values = place[...]
        projected = jnp.dot(dense, values, preferred_element_type=jnp.float32)
        summed = jnp.sum(values.astype(jnp.float32) * projected, axis=0, keepdims=True)
        for t in range(summed.shape[1] // LANES):
            box[t % 2, 2 * c + t // 2, :] = summed[0, t * LANES : (t + 1) * LANES]
    lane = lax.broadcasted_iota(jnp.int32, (EXT, LANES), 1)
    for half in range(2):
        cells = box[half]
        swapped[half] = jnp.where(
            lane % EXT < EXT // 2,
            pltpu.roll(cells, LANES - EXT // 2, axis=1),
            pltpu.roll(cells, EXT // 2, axis=1),
        )


def collocated(basis, density_blocks, pair_groups):
    rows, pairs = basis.shape[0], density_blocks.shape[0]
    groups = rows // BASIS
    kept = resident_cells()
    vmem, hbm = pl.BlockSpec(memory_space=pltpu.VMEM), pl.BlockSpec(memory_space=pltpu.HBM)
    return pl.pallas_call(
        functools.partial(collocate_kernel, groups),
        name="collocate",
        out_shape=(
            jax.ShapeDtypeStruct((2, EXT, LANES), jnp.float32),
            jax.ShapeDtypeStruct((2, EXT, LANES), jnp.float32),
            jax.ShapeDtypeStruct((rows, kept), basis.dtype),
        ),
        in_specs=[hbm, hbm, hbm],
        out_specs=[vmem, vmem, vmem],
        scratch_shapes=[
            pltpu.VMEM((rows, EXT3 - kept), basis.dtype),
            pltpu.SMEM(pair_groups.shape, jnp.int32),
            pltpu.VMEM(density_blocks.shape, density_blocks.dtype),
            pltpu.VMEM(((pairs + 1) * (BASIS + 1) + 7, LANES), jnp.float32),
            pltpu.VMEM((rows, -(-rows // LANES) * LANES), jnp.bfloat16),
            pltpu.SMEM((groups * groups,), jnp.int32),
            pltpu.SemaphoreType.DMA((EXT // 2,)),
            pltpu.SemaphoreType.DMA((2,)),
        ],
        compiler_params=pltpu.CompilerParams(vmem_limit_bytes=24 << 20),
        cost_estimate=pl.CostEstimate(
            flops=2 * rows * rows * EXT3, bytes_accessed=2 * rows * EXT3, transcendentals=0
        ),
    )(*[pltpu.with_memory_space_constraint(x, pltpu.HBM) for x in (pair_groups, density_blocks, basis)])


def integrate_kernel(
    groups, capacity, lines_of, potential, slots, head, basis, send, tail, total, arrived
):
    rows = groups * BASIS
    lines = BASIS // 2
    planes = 4
    chunk = planes * EXT * EXT
    kept = head.shape[1]
    copies = fetches(basis, head, tail, arrived, chunk, kept // chunk)
    for copy, _ in copies:
        copy.start()
    send[:, capacity * lines : capacity * lines + slots.shape[1], :] = slots[...]
    for c in range(EXT3 // chunk):
        if c * chunk < kept:
            values = head[:, c * chunk : (c + 1) * chunk]
        else:
            copy, place = copies[c - kept // chunk]
            copy.wait()
            values = place[...]
        weight = jnp.concatenate(
            [
                potential[t % 2, planes * c + t // 2 : planes * c + t // 2 + 1, :]
                for t in range(chunk // LANES)
            ],
            axis=1,
        )
        weighted = (values.astype(jnp.float32) * weight).astype(jnp.bfloat16)
        part = lax.dot_general(
            weighted, values, (((1,), (1,)), ((), ())), preferred_element_type=jnp.float32
        )
        if c == 0:
            total[:, :rows] = part
        else:
            total[:, :rows] += part
    left = lax.broadcasted_iota(jnp.int32, (lines, LANES), 1) < BASIS
    for first in range(groups):
        for second in range(groups):
            code = first * groups + second
            begin = second // 2 * LANES
            upper = total[first * BASIS : first * BASIS + lines, begin : begin + LANES]
            lower = total[first * BASIS + lines : (first + 1) * BASIS, begin : begin + LANES]
            if second % 2 == 0:
                lower = pltpu.roll(lower, BASIS, axis=1)
            else:
                upper = pltpu.roll(upper, BASIS, axis=1)
            line = pl.multiple_of(lines_of[1, code], lines)
            send[lines_of[0, code], pl.ds(line, lines), :] = (
                jnp.where(left, upper, lower) * GRID_WEIGHT
            ).astype(send.dtype)


def integrated(head, basis, potential, slots, lines_of, owners, capacity):
    rows = basis.shape[0]
    kept = head.shape[1]
    vmem, hbm = pl.BlockSpec(memory_space=pltpu.VMEM), pl.BlockSpec(memory_space=pltpu.HBM)
    return pl.pallas_call(
        functools.partial(integrate_kernel, rows // BASIS, capacity),
        name="integrate",
        out_shape=jax.ShapeDtypeStruct(
            (owners, capacity * BASIS // 2 + slots.shape[1], LANES), jnp.bfloat16
        ),
        in_specs=[pl.BlockSpec(memory_space=pltpu.SMEM), vmem, vmem, vmem, hbm],
        out_specs=vmem,
        scratch_shapes=[
            pltpu.VMEM((rows, EXT3 - kept), basis.dtype),
            pltpu.VMEM((rows, -(-rows // LANES) * LANES), jnp.float32),
            pltpu.SemaphoreType.DMA((EXT // 2,)),
        ],
        compiler_params=pltpu.CompilerParams(vmem_limit_bytes=24 << 20),
        cost_estimate=pl.CostEstimate(
            flops=2 * rows * rows * EXT3, bytes_accessed=2 * rows * EXT3, transcendentals=0
        ),
    )(lines_of, potential, slots, head, pltpu.with_memory_space_constraint(basis, pltpu.HBM))


def store_kernel(capacity, got, store, total, slots_vector, slots, moved):
    lines = BASIS // 2
    pitch = lines + 1
    sources = got.shape[0]
    stored = store.shape[0]
    for s in range(sources):
        slots_vector[s : s + 1, :] = (
            got[s, capacity * lines : capacity * lines + 8, :].astype(jnp.float32)[:1].astype(jnp.int32)
        )
    copy = pltpu.make_async_copy(slots_vector, slots, moved)
    copy.start()
    total[...] = jnp.zeros_like(total)
    copy.wait()

    def add(s, carry):
        for r in range(capacity):
            at = pl.ds(slots[s, r] * pitch, lines)
            total[at, :] += got[s, r * lines : (r + 1) * lines, :].astype(jnp.float32)
        return carry

    lax.fori_loop(0, sources, add, 0)
    in_low = lax.broadcasted_iota(jnp.int32, (stored, LANES), 1) < BASIS
    for i in range(lines // 2):
        even = total[pl.ds(2 * i, stored, stride=pitch), :]
        odd = total[pl.ds(2 * i + 1, stored, stride=pitch), :]
        for j, row in (
            (i, jnp.where(in_low, even, pltpu.roll(odd, BASIS, axis=1))),
            (i + lines // 2, jnp.where(in_low, pltpu.roll(even, BASIS, axis=1), odd)),
        ):
            store[:, j * LANES : (j + 1) * LANES] = row.astype(store.dtype)


def stored_blocks(got, rows, capacity):
    vmem = pl.BlockSpec(memory_space=pltpu.VMEM)
    return pl.pallas_call(
        functools.partial(store_kernel, capacity),
        name="store",
        out_shape=jax.ShapeDtypeStruct((rows, BASIS * BASIS), jnp.bfloat16),
        in_specs=[vmem],
        out_specs=vmem,
        scratch_shapes=[
            pltpu.VMEM(((rows + 1) * (BASIS // 2 + 1) + 7, LANES), jnp.float32),
            pltpu.VMEM((got.shape[0], LANES), jnp.int32),
            pltpu.SMEM((got.shape[0], LANES), jnp.int32),
            pltpu.SemaphoreType.DMA(()),
        ],
        compiler_params=pltpu.CompilerParams(vmem_limit_bytes=24 << 20),
        cost_estimate=pl.CostEstimate(
            flops=got.size, bytes_accessed=2 * got.size, transcendentals=0
        ),
    )(got)


def per_device(basis, density_blocks, pair_groups, owner, owner_slot):
    pairs = density_blocks.shape[0]
    owners = lax.axis_size("gx") * lax.axis_size("gy")
    capacity = max(2, 2 * pairs // owners)
    groups = basis.shape[0]
    basis = basis.reshape(groups * BASIS, EXT3)
    box, swapped, head = collocated(basis, density_blocks, pair_groups)

    owner_ids = owner[:, 0]
    order_ids = jnp.arange(pairs, dtype=jnp.int32)
    earlier = (owner_ids[:, None] == owner_ids[None, :]) & (order_ids[:, None] > order_ids[None, :])
    rank_within = jnp.sum(earlier.astype(jnp.int32), axis=1)
    counts = jnp.sum((owner_ids[None, :] == jnp.arange(owners)[:, None]).astype(jnp.int32), axis=1)
    least = jnp.min(counts * owners + jnp.arange(owners))
    free = jnp.stack([least % owners, least // owners])
    pair_codes = pair_groups[0] * groups + pair_groups[1]
    present = jnp.arange(groups * groups, dtype=jnp.int32)[:, None] == pair_codes[None, :]
    places = jnp.stack([owner_ids, rank_within]) - free[:, None]
    places = jnp.sum(jnp.where(present[None], places[:, None, :], 0), axis=2) + free[:, None]
    lines_of = places * jnp.array([1, BASIS // 2], dtype=jnp.int32)[:, None]
    lane_ids = jnp.arange(LANES, dtype=jnp.int32)
    chosen = (jnp.arange(owners, dtype=jnp.int32)[:, None, None] == owner_ids[None, None, :]) & (
        lane_ids[None, :, None] == rank_within[None, None, :]
    )
    slots = jnp.sum(jnp.where(chosen, owner_slot[None, None, :] - pairs, 0), axis=2) + pairs
    slots = jnp.broadcast_to(slots.astype(jnp.bfloat16)[:, None, :], (owners, 8, LANES))

    box = merged_z(box, swapped, "gz")
    y_low, y_high = merged(box[0], box[1], "gy")
    box = jnp.stack([y_low, y_high])
    x_low, x_high = merged(box[:, : EXT // 2], box[:, EXT // 2 :], "gx", forward=True)
    potential_ext = slater_potential(jnp.concatenate([x_low, x_high], axis=1))
    potential = potential_ext.reshape(2, EXT, EXT // 2, EXT)[:, RIM : RIM + CELLS, :, RIM : RIM + CELLS]
    potential = jnp.concatenate([potential[0, :, RIM:], potential[1, :, :RIM]], axis=1)

    send = integrated(head, basis, potential_ext, slots, lines_of, owners, capacity)
    got = lax.all_to_all(send, ("gx", "gy"), split_axis=0, concat_axis=0, tiled=True)
    return stored_blocks(got, pairs, capacity), potential


def solution(mesh):
    return jax.shard_map(
        per_device,
        mesh=mesh,
        in_specs=(
            P(("gx", "gy", "gz"), None, None),
            P(("gx", "gy", "gz"), None),
            P(None, ("gx", "gy", "gz")),
            P(("gx", "gy", "gz"), None),
            P(("gx", "gy", "gz")),
        ),
        out_specs=(P(("gx", "gy", "gz"), None), P("gx", "gy", "gz")),
        check_vma=False,
    )
```

time: 67.5 us -> 58.1 us (0.86)
  local copies, waits for them, and re-layouts: 7.8 us -> 0.27 us
  Pallas kernels: 16.6 us -> 13 us
  between operations: 0.84 us -> 3.44 us
  waiting for transfers between devices: 25.6 us -> 24.4 us
  other arithmetic: 1.31 us -> 2.46 us
    unnamed x17 -> x9, local copies, waits for them, and re-layouts: 7.56 us -> 0.03 us
    pallas_call x1, Pallas kernels: 7.32 us -> 5.17 us  [integrated(): pl.pallas_call(functools.partial(integrate_kernel, rows // BASIS, capacit...]
    ppermute x1, waiting for transfers between devices: 1.05 us -> 0.01 us  [merged_z(): return box + lax.ppermute(swapped, axis, neighbour_swaps(count, 0))]
    pallas_call x1, Pallas kernels: 6.8 us -> 5.77 us  [collocated(): pl.pallas_call(functools.partial(collocate_kernel, groups), name='colloca...]
    ppermute x1, starting transfers between devices: 1.89 us -> 1.03 us  [merged(): got = lax.ppermute(near, axis, neighbour_swaps(count, 0))]
  transfers between devices with their start and end apart: 6 -> 6, of which waited for: 5 -> 4; matrix products, arithmetic and copies ran while one was open for 2% -> 5% of each run, Pallas kernels for 0% -> 0%
where the time goes in v3:
time: 58.1 us; the launch traced here: 57.8 us
  waiting for transfers between devices  24.4 us (42%)
  starting transfers between devices  14.3 us (25%)
  Pallas kernels  13 us (22%)
  between operations  3.44 us (6%)
  other arithmetic  2.46 us (4%)
    all_to_all x1, waiting for transfers between devices, per_device(): lax.all_to_all(send, ('gx', 'gy'), split_axis=0, concat_axis=0, tiled=True)  19.2 us
    all_to_all x1, starting transfers between devices, per_device(): lax.all_to_all(send, ('gx', 'gy'), split_axis=0, concat_axis=0, tiled=True)  8.25 us
    pallas_call x1, Pallas kernels, collocated(): pl.pallas_call(functools.partial(collocate_kernel, groups), name='colloca...  5.77 us
    pallas_call x1, Pallas kernels, integrated(): pl.pallas_call(functools.partial(integrate_kernel, rows // BASIS, capacit...  5.17 us
    ppermute x1, waiting for transfers between devices, merged(): got = lax.ppermute(jnp.stack([near, far]), axis, neighbour_swaps(count, 0))  2.33 us
    ppermute x1, starting transfers between devices, merged(): far = far + lax.ppermute(got[1], axis, [(i, i ^ 2) for i in range(count)])  2.31 us
    pallas_call x1, Pallas kernels, stored_blocks(): pl.pallas_call(functools.partial(store_kernel, capacity), name='store', o...  2.01 us
    ppermute x1, waiting for transfers between devices, merged(): other = lax.ppermute(far, axis, neighbour_swaps(count, 1))  1.83 us
  transfers between devices with their start and end apart: 6, of which 4 were waited for; matrix products, arithmetic and copies ran while one was open for 5% of the time, Pallas kernels for 0%

profile of v3, /device:TPU:9, one launch (start us, length us, event | category | flops | bytes accessed | tf_op | source)
XLA Modules:
  0.0 57.8 jit_solution(1336531018237622767)
XLA Ops:
  0.7 5.8 %collocate.1 = (f32[2,16,128]{2,1,0:T(8,128)S(1)}, f32[2,16,128]{2,1,0:T(8,128)S(1)}, bf16[448,2048]{1,0:T(8,128)(2,1)S(1)}) custom-call(s32[2,48]{1,0:T(2,128)} %pair_groups.1, bf16[48,4096]{1,0:T(8,128)(2,1)} %blocks.1, bf16[448,4096]{1,0:T(8,128)(2,1)} %bitcast.34), custom_call_target="tpu_custom_call" | custom-call | flops 1644167168 | bytes 3670016 | tf_op jit(solution)/shard_map/collocate/pallas_call | solution.py:137
  6.5 1.3 %collective-permute-start = (f32[2,16,128]{2,1,0:T(8,128)S(1)}, f32[2,16,128]{2,1,0:T(8,128)S(1)}, u32[]{:S(2)}, u32[]{:S(2)}) collective-permute-start(f32[2,16,128]{2,1,0:T(8,128)S(1)} %get-tuple-element.6), channel_id=1, source_target_pairs={{0,1},{1,0},{2,3},{3,2},{4,5},{5,4},{6,7},{7,6},{8,9},{9,8},{10,11... | collective-permute-start | bytes 49160 | tf_op jit(solution)/shard_map/ppermute | solution.py:54
  7.8 0.2 convert_reduce_fusion
  7.9 0.1 convert_reduce_fusion.1
  8.1 0.6 %add_reduce_fusion = s32[]{:T(128)} fusion(s32[16]{0:T(128)S(1)} %convert_reduce_fusion.1), kind=kLoop, calls=%fused_computation.39 | loop fusion | flops 47 | bytes 68 | tf_op jit(solution)/shard_map/reduce_min | solution.py:305
  11.5 0.2 select_reduce_fusion
  11.8 0.1 pad_add_fusion
  11.8 1.0 %collective-permute-start.1 = (f32[16,128]{1,0:T(8,128)S(1)}, f32[16,128]{1,0:T(8,128)S(1)}, u32[]{:S(2)}, u32[]{:S(2)}) collective-permute-start(f32[16,128]{1,0:T(8,128)S(1)} %get-tuple-element.17), channel_id=1, source_target_pairs={{0,2},{2,0},{4,6},{6,4},{1,3},{3,1},{5,7},{7,5},{8,10},{10,8},{12,... | collective-permute-start | bytes 24584 | tf_op jit(solution)/shard_map/ppermute | solution.py:45
  12.9 1.2 %collective-permute-start.2 = (f32[16,128]{1,0:T(8,128)S(1)}, f32[16,128]{1,0:T(8,128)S(1)}, u32[]{:S(2)}, u32[]{:S(2)}) collective-permute-start(f32[16,128]{1,0:T(8,128)S(1)} %get-tuple-element.18), channel_id=1, source_target_pairs={{2,4},{4,2},{6,0},{0,6},{3,5},{5,3},{7,1},{1,7},{10,12},{12,10},{1... | collective-permute-start | bytes 24584 | tf_op jit(solution)/shard_map/ppermute | solution.py:46
  14.1 1.8 %collective-permute-done.2 = f32[16,128]{1,0:T(8,128)S(1)} collective-permute-done((f32[16,128]{1,0:T(8,128)S(1)}, f32[16,128]{1,0:T(8,128)S(1)}, u32[]{:S(2)}, u32[]{:S(2)}) %collective-permute-start.2) | collective-permute-done | bytes 8224 | tf_op jit(solution)/shard_map/ppermute | solution.py:46
  16.0 0.2 collective-permute-start.3
  16.2 0.1 select_reduce_fusion.1
  16.3 2.3 %collective-permute-done.3 = f32[2,2,8,128]{3,2,1,0:T(8,128)S(1)} collective-permute-done((f32[2,2,8,128]{3,2,1,0:T(8,128)S(1)}, f32[2,2,8,128]{3,2,1,0:T(8,128)S(1)}, u32[]{:S(2)}, u32[]{:S(2)}) %collective-permute-start.3) | collective-permute-done | bytes 16416 | tf_op jit(solution)/shard_map/ppermute | solution.py:41
  18.6 2.3 %collective-permute-start.4 = (f32[2,8,128]{2,1,0:T(8,128)S(1)}, f32[2,8,128]{2,1,0:T(8,128)S(1)}, u32[]{:S(2)}, u32[]{:S(2)}) collective-permute-start(f32[2,8,128]{2,1,0:T(8,128)S(1)} %slice_bitcast_fusion.2), channel_id=1, source_target_pairs={{0,16},{8,24},{16,0},{24,8},{1,17},{9,25},{17,1},{25,9},{2,18},{10... | collective-permute-start | bytes 24584 | tf_op jit(solution)/shard_map/ppermute | solution.py:43
  21.0 1.0 %collective-permute-done.4 = f32[2,8,128]{2,1,0:T(8,128)S(1)} collective-permute-done((f32[2,8,128]{2,1,0:T(8,128)S(1)}, f32[2,8,128]{2,1,0:T(8,128)S(1)}, u32[]{:S(2)}, u32[]{:S(2)}) %collective-permute-start.4) | collective-permute-done | bytes 8224 | tf_op jit(solution)/shard_map/ppermute | solution.py:43
  22.1 5.2 %integrate.1 = bf16[16,200,128]{2,1,0:T(8,128)(2,1)} custom-call(s32[2,49]{1,0:T(2,128)S(1)} %add_multiply_fusion.lines_of, f32[2,16,128]{2,1,0:T(8,128)S(1)} %cbrt_divide_fusion.1.potential, bf16[16,8,128]{2,1,0:T(8,128)(2,1)S(1)} %broadcast_in_dim.39.slots, bf16[448,2048]{1,0:T(8,128)(2,1)S(1)} %get-tuple-element.7.head, bf16[448,4096]{1,0:T(8,128)(2,1)} %bitcast.35), custom_call_target="tpu_custom_call" | custom-call | flops 1644167168 | bytes 3670016 | tf_op jit(solution)/shard_map/integrate/pallas_call | solution.py:219
  27.3 8.3 %all-to-all-start = ((bf16[16,200,128]{2,1,0:T(8,128)(2,1)}), bf16[16,200,128]{2,1,0:T(8,128)(2,1)S(1)}, u32[]{:S(2)}, u32[]{:S(2)}) async-start(bf16[16,200,128]{2,1,0:T(8,128)(2,1)} %integrate.1), calls=%async_computation | async-start | bytes 1638400 | tf_op jit(solution)/shard_map/all_to_all | solution.py:328
  35.5 0.1 concatenate.18
  35.6 0.1 concatenate.19
  35.7 0.1 cbrt_divide_fusion
  35.9 0.1 slice_bitcast_fusion.1
  36.0 0.6 %pad_maximum_fusion = f32[8,8,8]{2,1,0:T(8,128)} fusion(f32[8,4,8]{2,1,0:T(4,128)S(1)} %get-tuple-element.12, f32[8,4,8]{2,1,0:T(4,128)S(1)} %get-tuple-element.11), kind=kLoop, calls=%fused_computation.3 | loop fusion | flops 512 | bytes 4096 | tf_op jit(solution)/shard_map/concatenate | solution.py:325
  36.6 19.2 %all-to-all-done.got = bf16[16,200,128]{2,1,0:T(8,128)(2,1)S(1)} async-done(((bf16[16,200,128]{2,1,0:T(8,128)(2,1)}), bf16[16,200,128]{2,1,0:T(8,128)(2,1)S(1)}, u32[]{:S(2)}, u32[]{:S(2)}) %all-to-all-start) | async-done | bytes 819232 | tf_op jit(solution)/shard_map/all_to_all | solution.py:328
  55.8 2.0 %store.1 = bf16[48,4096]{1,0:T(8,128)(2,1)} custom-call(bf16[16,200,128]{2,1,0:T(8,128)(2,1)S(1)} %all-to-all-done.got), custom_call_target="tpu_custom_call" | custom-call | flops 409600 | bytes 819200 | tf_op jit(solution)/shard_map/store/pallas_call | solution.py:273
  (30 shorter events, 0.4 us)
Async XLA Ops:
  0.6 20.3 %copy-start.1 = (s32[2]{0:T(128)S(1)}, s32[2]{0:T(128)}, u32[]{:S(2)}) copy-start(s32[2]{0:T(128)} %constant.66.clone) | copy-start | bytes 28
  0.6 7.1 %copy-start.2 = (s32[2,48]{1,0:T(2,128)S(1)}, s32[2,48]{1,0:T(2,128)}, u32[]{:S(2)}) copy-start(s32[2,48]{1,0:T(2,128)} %pair_groups.1) | copy-start | bytes 1156
  0.7 7.1 %copy-start = (s32[48,1]{0,1:T(1,128)S(1)}, s32[48,1]{0,1:T(1,128)}, u32[]{:S(2)}) copy-start(s32[48,1]{0,1:T(1,128)} %param.9) | copy-start | bytes 580
  0.7 10.7 %copy-start.3 = (s32[48]{0:T(128)S(1)}, s32[48]{0:T(128)}, u32[]{:S(2)}) copy-start(s32[48]{0:T(128)} %param.10) | copy-start | bytes 580
  6.5 5.4 %collective-permute-start = (f32[2,16,128]{2,1,0:T(8,128)S(1)}, f32[2,16,128]{2,1,0:T(8,128)S(1)}, u32[]{:S(2)}, u32[]{:S(2)}) collective-permute-start(f32[2,16,128]{2,1,0:T(8,128)S(1)} %get-tuple-element.6), channel_id=1, source_target_pairs={{0,1},{1,0},{2,3},{3,2},{4,5},{5,4},{6,7},{7,6},{8,9},{9,8},{10,11... | collective-permute-start | bytes 49160 | tf_op jit(solution)/shard_map/ppermute | solution.py:54
  11.8 2.3 %collective-permute-start.1 = (f32[16,128]{1,0:T(8,128)S(1)}, f32[16,128]{1,0:T(8,128)S(1)}, u32[]{:S(2)}, u32[]{:S(2)}) collective-permute-start(f32[16,128]{1,0:T(8,128)S(1)} %get-tuple-element.17), channel_id=1, source_target_pairs={{0,2},{2,0},{4,6},{6,4},{1,3},{3,1},{5,7},{7,5},{8,10},{10,8},{12,... | collective-permute-start | bytes 24584 | tf_op jit(solution)/shard_map/ppermute | solution.py:45
  12.9 3.1 %collective-permute-start.2 = (f32[16,128]{1,0:T(8,128)S(1)}, f32[16,128]{1,0:T(8,128)S(1)}, u32[]{:S(2)}, u32[]{:S(2)}) collective-permute-start(f32[16,128]{1,0:T(8,128)S(1)} %get-tuple-element.18), channel_id=1, source_target_pairs={{2,4},{4,2},{6,0},{0,6},{3,5},{5,3},{7,1},{1,7},{10,12},{12,10},{1... | collective-permute-start | bytes 24584 | tf_op jit(solution)/shard_map/ppermute | solution.py:46
  16.0 2.7 %collective-permute-start.3 = (f32[2,2,8,128]{3,2,1,0:T(8,128)S(1)}, f32[2,2,8,128]{3,2,1,0:T(8,128)S(1)}, u32[]{:S(2)}, u32[]{:S(2)}) collective-permute-start(f32[2,2,8,128]{3,2,1,0:T(8,128)S(1)} %pad_maximum_fusion.1), channel_id=1, source_target_pairs={{0,8},{8,0},{16,24},{24,16},{1,9},{9,1},{17,25},{25,17},{2,10},{10... | collective-permute-start | bytes 49160 | tf_op jit(solution)/shard_map/ppermute | solution.py:41
  18.6 3.4 %collective-permute-start.4 = (f32[2,8,128]{2,1,0:T(8,128)S(1)}, f32[2,8,128]{2,1,0:T(8,128)S(1)}, u32[]{:S(2)}, u32[]{:S(2)}) collective-permute-start(f32[2,8,128]{2,1,0:T(8,128)S(1)} %slice_bitcast_fusion.2), channel_id=1, source_target_pairs={{0,16},{8,24},{16,0},{24,8},{1,17},{9,25},{17,1},{25,9},{2,18},{10... | collective-permute-start | bytes 24584 | tf_op jit(solution)/shard_map/ppermute | solution.py:43
  27.3 28.5 %all-to-all-start = ((bf16[16,200,128]{2,1,0:T(8,128)(2,1)}), bf16[16,200,128]{2,1,0:T(8,128)(2,1)S(1)}, u32[]{:S(2)}, u32[]{:S(2)}) async-start(bf16[16,200,128]{2,1,0:T(8,128)(2,1)} %integrate.1), calls=%async_computation | async-start | bytes 1638400 | tf_op jit(solution)/shard_map/all_to_all | solution.py:328

commit v4 on v3

--- a/solution.py
+++ b/solution.py
@@ -30,21 +30,15 @@
     return pairs
 
 
-def merged(low, high, axis, forward=False):
+def merged(low, high, axis):
     count = lax.axis_size(axis)
     if count == 2:
         got = lax.ppermute(jnp.stack([high, low]), axis, neighbour_swaps(count, 0))
         return low + got[0], high + got[1]
     odd = lax.axis_index(axis) % 2 == 1
     near, far = jnp.where(odd, low, high), jnp.where(odd, high, low)
-    if forward and count == 4:
-        got = lax.ppermute(jnp.stack([near, far]), axis, neighbour_swaps(count, 0))
-        near = near + got[0]
-        far = far + lax.ppermute(got[1], axis, [(i, i ^ 2) for i in range(count)])
-    else:
-        got = lax.ppermute(near, axis, neighbour_swaps(count, 0))
-        other = lax.ppermute(far, axis, neighbour_swaps(count, 1))
-        near, far = near + got, far + other
+    near = near + lax.ppermute(near, axis, neighbour_swaps(count, 0))
+    far = far + lax.ppermute(far, axis, neighbour_swaps(count, 1))
     return jnp.where(odd, near, far), jnp.where(odd, far, near)
 
 
@@ -61,7 +55,7 @@
 
 
 def resident_cells():
-    return 8 * EXT * EXT
+    return 12 * EXT * EXT
 
 
 def fetches(basis, head, tail, arrived, chunk, first):
@@ -83,10 +77,9 @@
     pitch = BASIS + 1
     codes_copy = pltpu.make_async_copy(pair_groups, codes, staged.at[0])
     blocks_copy = pltpu.make_async_copy(blocks, local, staged.at[1])
-    codes_copy.start()
-    blocks_copy.start()
-    copies = fetches(basis, head, tail, arrived, 2 * EXT * EXT, 0)
-    for copy, _ in copies:
+    ahead, planes = 2, 4
+    copies = fetches(basis, head, tail, arrived, planes * EXT * EXT, 0)
+    for copy in [codes_copy, blocks_copy] + [copy for copy, _ in copies[:ahead]]:
         copy.start()
     spread[pl.ds(pairs * pitch, BASIS), :] = jnp.zeros((BASIS, LANES), jnp.float32)
     codes_copy.wait()
@@ -114,11 +107,13 @@
     dense = matrix[:, : groups * BASIS]
     for c, (copy, place) in enumerate(copies):
         copy.wait()
+        if c + ahead < len(copies):
+            copies[c + ahead][0].start()
         values = place[...]
         projected = jnp.dot(dense, values, preferred_element_type=jnp.float32)
         summed = jnp.sum(values.astype(jnp.float32) * projected, axis=0, keepdims=True)
         for t in range(summed.shape[1] // LANES):
-            box[t % 2, 2 * c + t // 2, :] = summed[0, t * LANES : (t + 1) * LANES]
+            box[t % 2, planes * c + t // 2, :] = summed[0, t * LANES : (t + 1) * LANES]
     lane = lax.broadcasted_iota(jnp.int32, (EXT, LANES), 1)
     for half in range(2):
         cells = box[half]
@@ -158,28 +153,64 @@
         cost_estimate=pl.CostEstimate(
             flops=2 * rows * rows * EXT3, bytes_accessed=2 * rows * EXT3, transcendentals=0
         ),
-    )(*[pltpu.with_memory_space_constraint(x, pltpu.HBM) for x in (pair_groups, density_blocks, basis)])
+    )(*in_hbm(pair_groups, density_blocks, basis))
+
+
+def tabulate(groups, capacity, codes, owner, slot, counts, place, slot_rows):
+    pairs, owners = codes.shape[1], counts.shape[0]
+    for o in range(owners):
+        counts[o] = 0
+    for code in range(groups * groups):
+        place[0, code] = -1
+    slot_rows[...] = jnp.full(slot_rows.shape, pairs, jnp.float32)
+    lane = lax.broadcasted_iota(jnp.int32, (1, LANES), 1)
+    for p in range(pairs):
+        o = owner[0, p]
+        rank = counts[o]
+        counts[o] = rank + 1
+        code = codes[0, p] * groups + codes[1, p]
+        place[0, code] = o
+        place[1, code] = rank
+        row = slot_rows[pl.ds(o, 1), :]
+        slot_rows[pl.ds(o, 1), :] = jnp.where(lane == rank, slot[0, p].astype(jnp.float32), row)
+    free_owner, free_rank = jnp.int32(0), counts[0]
+    for o in range(1, owners):
+        fewer = counts[o] < free_rank
+        free_owner = jnp.where(fewer, o, free_owner)
+        free_rank = jnp.where(fewer, counts[o], free_rank)
+    for code in range(groups * groups):
+        absent = place[0, code] < 0
+        place[1, code] = jnp.where(absent, free_rank, place[1, code])
+        place[0, code] = jnp.where(absent, free_owner, place[0, code])
 
 
 def integrate_kernel(
-    groups, capacity, lines_of, potential, slots, head, basis, send, tail, total, arrived
+    groups, capacity, pair_groups, owner, owner_slot, potential, head, basis, send,
+    tail, total, slot_rows, codes, owners_of, slots_of, counts, place, arrived, staged,
 ):
     rows = groups * BASIS
     lines = BASIS // 2
     planes = 4
     chunk = planes * EXT * EXT
     kept = head.shape[1]
+    tables = [
+        pltpu.make_async_copy(source, target, staged.at[i])
+        for i, (source, target) in enumerate(
+            [(pair_groups, codes), (owner, owners_of), (owner_slot, slots_of)]
+        )
+    ]
+    for copy in tables:
+        copy.start()
     copies = fetches(basis, head, tail, arrived, chunk, kept // chunk)
     for copy, _ in copies:
         copy.start()
-    send[:, capacity * lines : capacity * lines + slots.shape[1], :] = slots[...]
     for c in range(EXT3 // chunk):
         if c * chunk < kept:
             values = head[:, c * chunk : (c + 1) * chunk]
         else:
-            copy, place = copies[c - kept // chunk]
+            copy, fetched = copies[c - kept // chunk]
             copy.wait()
-            values = place[...]
+            values = fetched[...]
         weight = jnp.concatenate(
             [
                 potential[t % 2, planes * c + t // 2 : planes * c + t // 2 + 1, :]
@@ -193,8 +224,15 @@
         )
         if c == 0:
             total[:, :rows] = part
+            for copy in tables:
+                copy.wait()
+            tabulate(groups, capacity, codes, owners_of, slots_of, counts, place, slot_rows)
         else:
             total[:, :rows] += part
+    for o in range(send.shape[0]):
+        send[o, capacity * lines :, :] = jnp.broadcast_to(
+            slot_rows[o : o + 1, :], (send.shape[1] - capacity * lines, LANES)
+        ).astype(send.dtype)
     left = lax.broadcasted_iota(jnp.int32, (lines, LANES), 1) < BASIS
     for first in range(groups):
         for second in range(groups):
@@ -206,34 +244,49 @@
                 lower = pltpu.roll(lower, BASIS, axis=1)
             else:
                 upper = pltpu.roll(upper, BASIS, axis=1)
-            line = pl.multiple_of(lines_of[1, code], lines)
-            send[lines_of[0, code], pl.ds(line, lines), :] = (
+            line = pl.multiple_of(place[1, code] * lines, lines)
+            send[place[0, code], pl.ds(line, lines), :] = (
                 jnp.where(left, upper, lower) * GRID_WEIGHT
             ).astype(send.dtype)
 
 
-def integrated(head, basis, potential, slots, lines_of, owners, capacity):
-    rows = basis.shape[0]
+def in_hbm(*arrays):
+    return [pltpu.with_memory_space_constraint(x, pltpu.HBM) for x in arrays]
+
+
+def integrated(head, basis, potential, pair_groups, owner, owner_slot, owners, capacity):
+    rows, pairs = basis.shape[0], pair_groups.shape[1]
+    groups = rows // BASIS
     kept = head.shape[1]
     vmem, hbm = pl.BlockSpec(memory_space=pltpu.VMEM), pl.BlockSpec(memory_space=pltpu.HBM)
     return pl.pallas_call(
-        functools.partial(integrate_kernel, rows // BASIS, capacity),
+        functools.partial(integrate_kernel, groups, capacity),
         name="integrate",
-        out_shape=jax.ShapeDtypeStruct(
-            (owners, capacity * BASIS // 2 + slots.shape[1], LANES), jnp.bfloat16
-        ),
-        in_specs=[pl.BlockSpec(memory_space=pltpu.SMEM), vmem, vmem, vmem, hbm],
+        out_shape=jax.ShapeDtypeStruct((owners, capacity * BASIS // 2 + 8, LANES), jnp.bfloat16),
+        in_specs=[hbm, hbm, hbm, vmem, vmem, hbm],
         out_specs=vmem,
         scratch_shapes=[
             pltpu.VMEM((rows, EXT3 - kept), basis.dtype),
             pltpu.VMEM((rows, -(-rows // LANES) * LANES), jnp.float32),
+            pltpu.VMEM((owners, LANES), jnp.float32),
+            pltpu.SMEM((2, pairs), jnp.int32),
+            pltpu.SMEM((1, pairs), jnp.int32),
+            pltpu.SMEM((1, pairs), jnp.int32),
+            pltpu.SMEM((owners,), jnp.int32),
+            pltpu.SMEM((2, groups * groups), jnp.int32),
             pltpu.SemaphoreType.DMA((EXT // 2,)),
+            pltpu.SemaphoreType.DMA((3,)),
         ],
         compiler_params=pltpu.CompilerParams(vmem_limit_bytes=24 << 20),
         cost_estimate=pl.CostEstimate(
             flops=2 * rows * rows * EXT3, bytes_accessed=2 * rows * EXT3, transcendentals=0
         ),
-    )(lines_of, potential, slots, head, pltpu.with_memory_space_constraint(basis, pltpu.HBM))
+    )(
+        *in_hbm(pair_groups, owner.reshape(1, pairs), owner_slot.reshape(1, pairs)),
+        potential,
+        head,
+        *in_hbm(basis),
+    )
 
 
 def store_kernel(capacity, got, store, total, slots_vector, slots, moved):
@@ -296,35 +349,17 @@
     groups = basis.shape[0]
     basis = basis.reshape(groups * BASIS, EXT3)
     box, swapped, head = collocated(basis, density_blocks, pair_groups)
-
-    owner_ids = owner[:, 0]
-    order_ids = jnp.arange(pairs, dtype=jnp.int32)
-    earlier = (owner_ids[:, None] == owner_ids[None, :]) & (order_ids[:, None] > order_ids[None, :])
-    rank_within = jnp.sum(earlier.astype(jnp.int32), axis=1)
-    counts = jnp.sum((owner_ids[None, :] == jnp.arange(owners)[:, None]).astype(jnp.int32), axis=1)
-    least = jnp.min(counts * owners + jnp.arange(owners))
-    free = jnp.stack([least % owners, least // owners])
-    pair_codes = pair_groups[0] * groups + pair_groups[1]
-    present = jnp.arange(groups * groups, dtype=jnp.int32)[:, None] == pair_codes[None, :]
-    places = jnp.stack([owner_ids, rank_within]) - free[:, None]
-    places = jnp.sum(jnp.where(present[None], places[:, None, :], 0), axis=2) + free[:, None]
-    lines_of = places * jnp.array([1, BASIS // 2], dtype=jnp.int32)[:, None]
-    lane_ids = jnp.arange(LANES, dtype=jnp.int32)
-    chosen = (jnp.arange(owners, dtype=jnp.int32)[:, None, None] == owner_ids[None, None, :]) & (
-        lane_ids[None, :, None] == rank_within[None, None, :]
-    )
-    slots = jnp.sum(jnp.where(chosen, owner_slot[None, None, :] - pairs, 0), axis=2) + pairs
-    slots = jnp.broadcast_to(slots.astype(jnp.bfloat16)[:, None, :], (owners, 8, LANES))
-
     box = merged_z(box, swapped, "gz")
     y_low, y_high = merged(box[0], box[1], "gy")
     box = jnp.stack([y_low, y_high])
-    x_low, x_high = merged(box[:, : EXT // 2], box[:, EXT // 2 :], "gx", forward=True)
+    x_low, x_high = merged(box[:, : EXT // 2], box[:, EXT // 2 :], "gx")
     potential_ext = slater_potential(jnp.concatenate([x_low, x_high], axis=1))
     potential = potential_ext.reshape(2, EXT, EXT // 2, EXT)[:, RIM : RIM + CELLS, :, RIM : RIM + CELLS]
     potential = jnp.concatenate([potential[0, :, RIM:], potential[1, :, :RIM]], axis=1)
 
-    send = integrated(head, basis, potential_ext, slots, lines_of, owners, capacity)
+    send = integrated(
+        head, basis, potential_ext, pair_groups, owner, owner_slot, owners, capacity
+    )
     got = lax.all_to_all(send, ("gx", "gy"), split_axis=0, concat_axis=0, tiled=True)
     return stored_blocks(got, pairs, capacity), potential
 

time: 58.1 us -> 51 us (0.88)
  Pallas kernels: 13 us -> 10.2 us
  between operations: 3.44 us -> 0.7 us
  other arithmetic: 2.46 us -> 0.83 us
  starting transfers between devices: 14.3 us -> 15.2 us
  waiting for transfers between devices: 24.4 us -> 23.5 us
    ppermute x4, waiting for transfers between devices: 5.17 us -> 2.94 us  [the longest x2 2.94 us: merged(): far = far + lax.ppermute(far, axis, neighbour_swaps(count, 1))]
    pallas_call x1, Pallas kernels: 5.17 us -> 3.7 us  [integrated(): pl.pallas_call(functools.partial(integrate_kernel, groups, capacity), nam...]
    pallas_call x1, Pallas kernels: 5.77 us -> 4.35 us  [collocated(): pl.pallas_call(functools.partial(collocate_kernel, groups), name='colloca...]
    ppermute x1, waiting for transfers between devices: 0.01 us -> 1.35 us  [merged_z(): return box + lax.ppermute(swapped, axis, neighbour_swaps(count, 0))]
    ppermute x4, starting transfers between devices: 4.75 us -> 5.71 us  [the longest x2 3.75 us: merged(): far = far + lax.ppermute(far, axis, neighbour_swaps(count, 1))]
    reduce_min x1 -> x0, other arithmetic: 0.65 us -> none  [per_device(): least = jnp.min(counts * owners + jnp.arange(owners))]
    reduce_sum x4 -> x0, other arithmetic: 0.59 us -> none  [the longest x1 0.2 us: per_device(): jnp.sum(jnp.where(chosen, owner_slot[None, None, :] - pairs, 0), axis=2)]
  transfers between devices with their start and end apart: 6 -> 6, of which waited for: 4 -> 4; matrix products, arithmetic and copies ran while one was open for 5% -> 2% of each run, Pallas kernels for 0% -> 0%
where the time goes in v4:
time: 51 us; the launch traced here: 50.8 us
  waiting for transfers between devices  23.5 us (46%)
  starting transfers between devices  15.2 us (30%)
  Pallas kernels  10.2 us (20%)
  other arithmetic  0.83 us (2%)
  between operations  0.7 us (1%)
    all_to_all x1, waiting for transfers between devices, per_device(): lax.all_to_all(send, ('gx', 'gy'), split_axis=0, concat_axis=0, tiled=True)  19.2 us
    all_to_all x1, starting transfers between devices, per_device(): lax.all_to_all(send, ('gx', 'gy'), split_axis=0, concat_axis=0, tiled=True)  8.23 us
    pallas_call x1, Pallas kernels, collocated(): pl.pallas_call(functools.partial(collocate_kernel, groups), name='colloca...  4.35 us
    ppermute x2, starting transfers between devices, merged(): far = far + lax.ppermute(far, axis, neighbour_swaps(count, 1))  3.75 us
    pallas_call x1, Pallas kernels, integrated(): pl.pallas_call(functools.partial(integrate_kernel, groups, capacity), nam...  3.7 us
    ppermute x2, waiting for transfers between devices, merged(): far = far + lax.ppermute(far, axis, neighbour_swaps(count, 1))  2.94 us
    pallas_call x1, Pallas kernels, stored_blocks(): pl.pallas_call(functools.partial(store_kernel, capacity), name='store', o...  2.15 us
    ppermute x2, starting transfers between devices, merged(): near = near + lax.ppermute(near, axis, neighbour_swaps(count, 0))  1.96 us
  transfers between devices with their start and end apart: 6, of which 4 were waited for; matrix products, arithmetic and copies ran while one was open for 2% of the time, Pallas kernels for 0%

profile of v4, /device:TPU:9, one launch (start us, length us, event | category | flops | bytes accessed | tf_op | source)
XLA Modules:
  0.0 50.8 jit_solution(1939990136535802222)
XLA Ops:
  0.6 4.4 %collocate.1 = (f32[2,16,128]{2,1,0:T(8,128)S(1)}, f32[2,16,128]{2,1,0:T(8,128)S(1)}, bf16[448,3072]{1,0:T(8,128)(2,1)S(1)}) custom-call(s32[2,48]{1,0:T(2,128)} %pair_groups.3, bf16[48,4096]{1,0:T(8,128)(2,1)} %blocks.1, bf16[448,4096]{1,0:T(8,128)(2,1)} %bitcast.15), custom_call_target="tpu_custom_call" | custom-call | flops 1644167168 | bytes 3670016 | tf_op jit(solution)/shard_map/collocate/pallas_call | solution.py:132
  5.0 1.3 %collective-permute-start = (f32[2,16,128]{2,1,0:T(8,128)S(1)}, f32[2,16,128]{2,1,0:T(8,128)S(1)}, u32[]{:S(2)}, u32[]{:S(2)}) collective-permute-start(f32[2,16,128]{2,1,0:T(8,128)S(1)} %get-tuple-element.6), channel_id=1, source_target_pairs={{0,1},{1,0},{2,3},{3,2},{4,5},{5,4},{6,7},{7,6},{8,9},{9,8},{10,11... | collective-permute-start | bytes 49160 | tf_op jit(solution)/shard_map/ppermute | solution.py:48
  6.3 1.4 %collective-permute-done = f32[2,16,128]{2,1,0:T(8,128)S(1)} collective-permute-done((f32[2,16,128]{2,1,0:T(8,128)S(1)}, f32[2,16,128]{2,1,0:T(8,128)S(1)}, u32[]{:S(2)}, u32[]{:S(2)}) %collective-permute-start) | collective-permute-done | bytes 16416 | tf_op jit(solution)/shard_map/ppermute | solution.py:48
  7.7 1.9 %collective-permute-start.1 = (f32[16,128]{1,0:T(8,128)S(1)}, f32[16,128]{1,0:T(8,128)S(1)}, u32[]{:S(2)}, u32[]{:S(2)}) collective-permute-start(f32[16,128]{1,0:T(8,128)S(1)} %get-tuple-element.16), channel_id=1, source_target_pairs={{0,2},{2,0},{4,6},{6,4},{1,3},{3,1},{5,7},{7,5},{8,10},{10,8},{12,... | collective-permute-start | bytes 24584 | tf_op jit(solution)/shard_map/ppermute | solution.py:40
  9.6 1.2 %collective-permute-start.2 = (f32[16,128]{1,0:T(8,128)S(1)}, f32[16,128]{1,0:T(8,128)S(1)}, u32[]{:S(2)}, u32[]{:S(2)}) collective-permute-start(f32[16,128]{1,0:T(8,128)S(1)} %get-tuple-element.17), channel_id=1, source_target_pairs={{2,4},{4,2},{6,0},{0,6},{3,5},{5,3},{7,1},{1,7},{10,12},{12,10},{1... | collective-permute-start | bytes 24584 | tf_op jit(solution)/shard_map/ppermute | solution.py:41
  10.7 0.0 collective-permute-done.1
  10.7 1.9 %collective-permute-done.2 = f32[16,128]{1,0:T(8,128)S(1)} collective-permute-done((f32[16,128]{1,0:T(8,128)S(1)}, f32[16,128]{1,0:T(8,128)S(1)}, u32[]{:S(2)}, u32[]{:S(2)}) %collective-permute-start.2) | collective-permute-done | bytes 8224 | tf_op jit(solution)/shard_map/ppermute | solution.py:41
  12.6 0.1 collective-permute-start.3
  12.7 2.6 %collective-permute-start.4 = (f32[2,8,128]{2,1,0:T(8,128)S(1)}, f32[2,8,128]{2,1,0:T(8,128)S(1)}, u32[]{:S(2)}, u32[]{:S(2)}) collective-permute-start(f32[2,8,128]{2,1,0:T(8,128)S(1)} %get-tuple-element.15), channel_id=1, source_target_pairs={{8,16},{16,8},{24,0},{0,24},{9,17},{17,9},{25,1},{1,25},{10,18},{1... | collective-permute-start | bytes 24584 | tf_op jit(solution)/shard_map/ppermute | solution.py:41
  15.3 0.0 collective-permute-done.3
  15.3 1.0 %collective-permute-done.4 = f32[2,8,128]{2,1,0:T(8,128)S(1)} collective-permute-done((f32[2,8,128]{2,1,0:T(8,128)S(1)}, f32[2,8,128]{2,1,0:T(8,128)S(1)}, u32[]{:S(2)}, u32[]{:S(2)}) %collective-permute-start.4) | collective-permute-done | bytes 8224 | tf_op jit(solution)/shard_map/ppermute | solution.py:41
  16.4 3.7 %integrate.1 = bf16[16,200,128]{2,1,0:T(8,128)(2,1)} custom-call(s32[2,48]{1,0:T(2,128)} %pair_groups.3, s32[1,48]{1,0:T(1,128)} %bitcast.17, s32[1,48]{1,0:T(1,128)} %bitcast.18, f32[2,16,128]{2,1,0:T(8,128)S(1)} %cbrt_divide_fusion.1.potential, bf16[448,3072]{1,0:T(8,128)(2,1)S(1)} %get-tuple-element.7.head, bf16[448,4096]{1,0:T(8,128)(2,1)} %bitcast.16), custom_call_target="tpu_custom_call" | custom-call | flops 1644167168 | bytes 3670016 | tf_op jit(solution)/shard_map/integrate/pallas_call | solution.py:262
  20.1 8.2 %all-to-all-start = ((bf16[16,200,128]{2,1,0:T(8,128)(2,1)}), bf16[16,200,128]{2,1,0:T(8,128)(2,1)S(1)}, u32[]{:S(2)}, u32[]{:S(2)}) async-start(bf16[16,200,128]{2,1,0:T(8,128)(2,1)} %integrate.1), calls=%async_computation | async-start | bytes 1638400 | tf_op jit(solution)/shard_map/all_to_all | solution.py:363
  28.3 0.1 concatenate.14
  28.4 0.1 concatenate.15
  28.5 0.1 cbrt_divide_fusion
  28.7 0.1 slice_bitcast_fusion.1
  28.7 0.6 %pad_maximum_fusion = f32[8,8,8]{2,1,0:T(8,128)} fusion(f32[8,4,8]{2,1,0:T(4,128)S(1)} %get-tuple-element.9, f32[8,4,8]{2,1,0:T(4,128)S(1)} %get-tuple-element.8), kind=kLoop, calls=%fused_computation.1 | loop fusion | flops 512 | bytes 4096 | tf_op jit(solution)/shard_map/concatenate | solution.py:358
  29.4 19.2 %all-to-all-done.got = bf16[16,200,128]{2,1,0:T(8,128)(2,1)S(1)} async-done(((bf16[16,200,128]{2,1,0:T(8,128)(2,1)}), bf16[16,200,128]{2,1,0:T(8,128)(2,1)S(1)}, u32[]{:S(2)}, u32[]{:S(2)}) %all-to-all-start) | async-done | bytes 819232 | tf_op jit(solution)/shard_map/all_to_all | solution.py:363
  48.6 2.2 %store.1 = bf16[48,4096]{1,0:T(8,128)(2,1)} custom-call(bf16[16,200,128]{2,1,0:T(8,128)(2,1)S(1)} %all-to-all-done.got), custom_call_target="tpu_custom_call" | custom-call | flops 409600 | bytes 819200 | tf_op jit(solution)/shard_map/store/pallas_call | solution.py:326
  (8 shorter events, 0.1 us)
Async XLA Ops:
  5.0 2.7 %collective-permute-start = (f32[2,16,128]{2,1,0:T(8,128)S(1)}, f32[2,16,128]{2,1,0:T(8,128)S(1)}, u32[]{:S(2)}, u32[]{:S(2)}) collective-permute-start(f32[2,16,128]{2,1,0:T(8,128)S(1)} %get-tuple-element.6), channel_id=1, source_target_pairs={{0,1},{1,0},{2,3},{3,2},{4,5},{5,4},{6,7},{7,6},{8,9},{9,8},{10,11... | collective-permute-start | bytes 49160 | tf_op jit(solution)/shard_map/ppermute | solution.py:48
  7.7 3.1 %collective-permute-start.1 = (f32[16,128]{1,0:T(8,128)S(1)}, f32[16,128]{1,0:T(8,128)S(1)}, u32[]{:S(2)}, u32[]{:S(2)}) collective-permute-start(f32[16,128]{1,0:T(8,128)S(1)} %get-tuple-element.16), channel_id=1, source_target_pairs={{0,2},{2,0},{4,6},{6,4},{1,3},{3,1},{5,7},{7,5},{8,10},{10,8},{12,... | collective-permute-start | bytes 24584 | tf_op jit(solution)/shard_map/ppermute | solution.py:40
  9.6 3.1 %collective-permute-start.2 = (f32[16,128]{1,0:T(8,128)S(1)}, f32[16,128]{1,0:T(8,128)S(1)}, u32[]{:S(2)}, u32[]{:S(2)}) collective-permute-start(f32[16,128]{1,0:T(8,128)S(1)} %get-tuple-element.17), channel_id=1, source_target_pairs={{2,4},{4,2},{6,0},{0,6},{3,5},{5,3},{7,1},{1,7},{10,12},{12,10},{1... | collective-permute-start | bytes 24584 | tf_op jit(solution)/shard_map/ppermute | solution.py:41
  12.6 2.7 %collective-permute-start.3 = (f32[2,8,128]{2,1,0:T(8,128)S(1)}, f32[2,8,128]{2,1,0:T(8,128)S(1)}, u32[]{:S(2)}, u32[]{:S(2)}) collective-permute-start(f32[2,8,128]{2,1,0:T(8,128)S(1)} %get-tuple-element.14), channel_id=1, source_target_pairs={{0,8},{8,0},{16,24},{24,16},{1,9},{9,1},{17,25},{25,17},{2,10},{10... | collective-permute-start | bytes 24584 | tf_op jit(solution)/shard_map/ppermute | solution.py:40
  12.7 3.6 %collective-permute-start.4 = (f32[2,8,128]{2,1,0:T(8,128)S(1)}, f32[2,8,128]{2,1,0:T(8,128)S(1)}, u32[]{:S(2)}, u32[]{:S(2)}) collective-permute-start(f32[2,8,128]{2,1,0:T(8,128)S(1)} %get-tuple-element.15), channel_id=1, source_target_pairs={{8,16},{16,8},{24,0},{0,24},{9,17},{17,9},{25,1},{1,25},{10,18},{1... | collective-permute-start | bytes 24584 | tf_op jit(solution)/shard_map/ppermute | solution.py:41
  20.1 28.5 %all-to-all-start = ((bf16[16,200,128]{2,1,0:T(8,128)(2,1)}), bf16[16,200,128]{2,1,0:T(8,128)(2,1)S(1)}, u32[]{:S(2)}, u32[]{:S(2)}) async-start(bf16[16,200,128]{2,1,0:T(8,128)(2,1)} %integrate.1), calls=%async_computation | async-start | bytes 1638400 | tf_op jit(solution)/shard_map/all_to_all | solution.py:363

commit v5 on v4

--- a/solution.py
+++ b/solution.py
@@ -30,15 +30,17 @@
     return pairs
 
 
-def merged(low, high, axis):
+def merged_halves(low, high, axis):
     count = lax.axis_size(axis)
-    if count == 2:
-        got = lax.ppermute(jnp.stack([high, low]), axis, neighbour_swaps(count, 0))
-        return low + got[0], high + got[1]
     odd = lax.axis_index(axis) % 2 == 1
     near, far = jnp.where(odd, low, high), jnp.where(odd, high, low)
     near = near + lax.ppermute(near, axis, neighbour_swaps(count, 0))
     far = far + lax.ppermute(far, axis, neighbour_swaps(count, 1))
+    return odd, near, far
+
+
+def merged(low, high, axis):
+    odd, near, far = merged_halves(low, high, axis)
     return jnp.where(odd, near, far), jnp.where(odd, far, near)
 
 
@@ -54,31 +56,35 @@
     return box + jnp.where(in_high != odd, first, second)
 
 
-def resident_cells():
-    return 12 * EXT * EXT
-
-
-def fetches(basis, head, tail, arrived, chunk, first):
-    kept = head.shape[1]
-    copies = []
-    for c in range(first, EXT3 // chunk):
-        source = basis.at[:, pl.ds(c * chunk, chunk)]
-        begin = c * chunk if c * chunk < kept else c * chunk - kept
-        place = (head if c * chunk < kept else tail).at[:, pl.ds(begin, chunk)]
-        copies.append((pltpu.make_async_copy(source, place, arrived.at[c]), place))
-    return copies
+def halves():
+    odd = lax.axis_index("gx") % 2
+    return (1 - odd) * (EXT3 // 2), odd * (EXT3 // 2)
 
 
 def collocate_kernel(
-    groups, pair_groups, blocks, basis, box, swapped, head,
-    tail, codes, local, spread, matrix, owner_of, arrived, staged,
+    groups, pair_groups, blocks, basis, box, swapped, near,
+    far, codes, local, spread, matrix, owner_of, arrived, staged,
 ):
     pairs = blocks.shape[0]
     pitch = BASIS + 1
     codes_copy = pltpu.make_async_copy(pair_groups, codes, staged.at[0])
     blocks_copy = pltpu.make_async_copy(blocks, local, staged.at[1])
     ahead, planes = 2, 4
-    copies = fetches(basis, head, tail, arrived, planes * EXT * EXT, 0)
+    cells = planes * EXT * EXT
+    copies, plane_of = [], []
+    for begin, half in zip(halves(), (near, far)):
+        for c in range(half.shape[1] // cells):
+            first = pl.multiple_of(begin + c * cells, LANES)
+            place = half.at[:, pl.ds(c * cells, cells)]
+            copies.append(
+                (
+                    pltpu.make_async_copy(
+                        basis.at[:, pl.ds(first, cells)], place, arrived.at[len(copies)]
+                    ),
+                    place,
+                )
+            )
+            plane_of.append(begin // (EXT * EXT) + c * planes)
     for copy in [codes_copy, blocks_copy] + [copy for copy, _ in copies[:ahead]]:
         copy.start()
     spread[pl.ds(pairs * pitch, BASIS), :] = jnp.zeros((BASIS, LANES), jnp.float32)
@@ -113,7 +119,7 @@
         projected = jnp.dot(dense, values, preferred_element_type=jnp.float32)
         summed = jnp.sum(values.astype(jnp.float32) * projected, axis=0, keepdims=True)
         for t in range(summed.shape[1] // LANES):
-            box[t % 2, planes * c + t // 2, :] = summed[0, t * LANES : (t + 1) * LANES]
+            box[t % 2, pl.ds(plane_of[c] + t // 2, 1), :] = summed[:, t * LANES : (t + 1) * LANES]
     lane = lax.broadcasted_iota(jnp.int32, (EXT, LANES), 1)
     for half in range(2):
         cells = box[half]
@@ -127,7 +133,6 @@
 def collocated(basis, density_blocks, pair_groups):
     rows, pairs = basis.shape[0], density_blocks.shape[0]
     groups = rows // BASIS
-    kept = resident_cells()
     vmem, hbm = pl.BlockSpec(memory_space=pltpu.VMEM), pl.BlockSpec(memory_space=pltpu.HBM)
     return pl.pallas_call(
         functools.partial(collocate_kernel, groups),
@@ -135,16 +140,16 @@
         out_shape=(
             jax.ShapeDtypeStruct((2, EXT, LANES), jnp.float32),
             jax.ShapeDtypeStruct((2, EXT, LANES), jnp.float32),
-            jax.ShapeDtypeStruct((rows, kept), basis.dtype),
+            jax.ShapeDtypeStruct((rows, EXT3 // 2), basis.dtype),
         ),
         in_specs=[hbm, hbm, hbm],
         out_specs=[vmem, vmem, vmem],
         scratch_shapes=[
-            pltpu.VMEM((rows, EXT3 - kept), basis.dtype),
+            pltpu.VMEM((rows, EXT3 // 2), basis.dtype),
             pltpu.SMEM(pair_groups.shape, jnp.int32),
             pltpu.VMEM(density_blocks.shape, density_blocks.dtype),
             pltpu.VMEM(((pairs + 1) * (BASIS + 1) + 7, LANES), jnp.float32),
-            pltpu.VMEM((rows, -(-rows // LANES) * LANES), jnp.bfloat16),
+            pltpu.VMEM((rows, padded(rows)), jnp.bfloat16),
             pltpu.SMEM((groups * groups,), jnp.int32),
             pltpu.SemaphoreType.DMA((EXT // 2,)),
             pltpu.SemaphoreType.DMA((2,)),
@@ -184,15 +189,42 @@
         place[0, code] = jnp.where(absent, free_owner, place[0, code])
 
 
-def integrate_kernel(
-    groups, capacity, pair_groups, owner, owner_slot, potential, head, basis, send,
-    tail, total, slot_rows, codes, owners_of, slots_of, counts, place, arrived, staged,
+def overlaps(table, potential, planes=4):
+    cells = planes * EXT * EXT
+    for c in range(table.shape[1] // cells):
+        values = table[:, c * cells : (c + 1) * cells]
+        weight = jnp.concatenate(
+            [
+                potential[t % 2, planes * c + t // 2 : planes * c + t // 2 + 1, :]
+                for t in range(cells // LANES)
+            ],
+            axis=1,
+        )
+        weighted = (values.astype(jnp.float32) * weight).astype(jnp.bfloat16)
+        yield lax.dot_general(
+            weighted, values, (((1,), (1,)), ((), ())), preferred_element_type=jnp.float32
+        )
+
+
+def near_kernel(potential, near, basis, total, far, arrived):
+    rows = near.shape[0]
+    begin = pl.multiple_of(halves()[1], LANES)
+    copy = pltpu.make_async_copy(basis.at[:, pl.ds(begin, far.shape[1])], far, arrived)
+    copy.start()
+    for c, part in enumerate(overlaps(near, potential)):
+        if c == 0:
+            total[:, :rows] = part
+        else:
+            total[:, :rows] += part
+    copy.wait()
+
+
+def far_kernel(
+    groups, capacity, pair_groups, owner, owner_slot, potential, far, near_total, send,
+    total, slot_rows, codes, owners_of, slots_of, counts, place, staged,
 ):
     rows = groups * BASIS
     lines = BASIS // 2
-    planes = 4
-    chunk = planes * EXT * EXT
-    kept = head.shape[1]
     tables = [
         pltpu.make_async_copy(source, target, staged.at[i])
         for i, (source, target) in enumerate(
@@ -201,29 +233,9 @@
     ]
     for copy in tables:
         copy.start()
-    copies = fetches(basis, head, tail, arrived, chunk, kept // chunk)
-    for copy, _ in copies:
-        copy.start()
-    for c in range(EXT3 // chunk):
-        if c * chunk < kept:
-            values = head[:, c * chunk : (c + 1) * chunk]
-        else:
-            copy, fetched = copies[c - kept // chunk]
-            copy.wait()
-            values = fetched[...]
-        weight = jnp.concatenate(
-            [
-                potential[t % 2, planes * c + t // 2 : planes * c + t // 2 + 1, :]
-                for t in range(chunk // LANES)
-            ],
-            axis=1,
-        )
-        weighted = (values.astype(jnp.float32) * weight).astype(jnp.bfloat16)
-        part = lax.dot_general(
-            weighted, values, (((1,), (1,)), ((), ())), preferred_element_type=jnp.float32
-        )
+    for c, part in enumerate(overlaps(far, potential)):
         if c == 0:
-            total[:, :rows] = part
+            total[:, :rows] = near_total[:, :rows] + part
             for copy in tables:
                 copy.wait()
             tabulate(groups, capacity, codes, owners_of, slots_of, counts, place, slot_rows)
@@ -254,38 +266,59 @@
     return [pltpu.with_memory_space_constraint(x, pltpu.HBM) for x in arrays]
 
 
-def integrated(head, basis, potential, pair_groups, owner, owner_slot, owners, capacity):
-    rows, pairs = basis.shape[0], pair_groups.shape[1]
-    groups = rows // BASIS
-    kept = head.shape[1]
+def padded(rows):
+    return -(-rows // LANES) * LANES
+
+
+def integrated_near(near, basis, potential):
+    rows = basis.shape[0]
     vmem, hbm = pl.BlockSpec(memory_space=pltpu.VMEM), pl.BlockSpec(memory_space=pltpu.HBM)
     return pl.pallas_call(
-        functools.partial(integrate_kernel, groups, capacity),
-        name="integrate",
+        near_kernel,
+        name="integrate_near",
+        out_shape=(
+            jax.ShapeDtypeStruct((rows, padded(rows)), jnp.float32),
+            jax.ShapeDtypeStruct((rows, EXT3 // 2), basis.dtype),
+        ),
+        in_specs=[vmem, vmem, hbm],
+        out_specs=[vmem, vmem],
+        scratch_shapes=[pltpu.SemaphoreType.DMA(())],
+        compiler_params=pltpu.CompilerParams(vmem_limit_bytes=24 << 20),
+        cost_estimate=pl.CostEstimate(
+            flops=rows * rows * EXT3, bytes_accessed=2 * rows * EXT3, transcendentals=0
+        ),
+    )(potential, near, *in_hbm(basis))
+
+
+def integrated_far(far, near_total, potential, pair_groups, owner, owner_slot, owners, capacity):
+    rows, pairs = far.shape[0], pair_groups.shape[1]
+    groups = rows // BASIS
+    vmem, hbm = pl.BlockSpec(memory_space=pltpu.VMEM), pl.BlockSpec(memory_space=pltpu.HBM)
+    return pl.pallas_call(
+        functools.partial(far_kernel, groups, capacity),
+        name="integrate_far",
         out_shape=jax.ShapeDtypeStruct((owners, capacity * BASIS // 2 + 8, LANES), jnp.bfloat16),
-        in_specs=[hbm, hbm, hbm, vmem, vmem, hbm],
+        in_specs=[hbm, hbm, hbm, vmem, vmem, vmem],
         out_specs=vmem,
         scratch_shapes=[
-            pltpu.VMEM((rows, EXT3 - kept), basis.dtype),
-            pltpu.VMEM((rows, -(-rows // LANES) * LANES), jnp.float32),
+            pltpu.VMEM((rows, padded(rows)), jnp.float32),
             pltpu.VMEM((owners, LANES), jnp.float32),
             pltpu.SMEM((2, pairs), jnp.int32),
             pltpu.SMEM((1, pairs), jnp.int32),
             pltpu.SMEM((1, pairs), jnp.int32),
             pltpu.SMEM((owners,), jnp.int32),
             pltpu.SMEM((2, groups * groups), jnp.int32),
-            pltpu.SemaphoreType.DMA((EXT // 2,)),
             pltpu.SemaphoreType.DMA((3,)),
         ],
         compiler_params=pltpu.CompilerParams(vmem_limit_bytes=24 << 20),
         cost_estimate=pl.CostEstimate(
-            flops=2 * rows * rows * EXT3, bytes_accessed=2 * rows * EXT3, transcendentals=0
+            flops=rows * rows * EXT3, bytes_accessed=2 * rows * EXT3, transcendentals=0
         ),
     )(
         *in_hbm(pair_groups, owner.reshape(1, pairs), owner_slot.reshape(1, pairs)),
         potential,
-        head,
-        *in_hbm(basis),
+        far,
+        near_total,
     )
 
 
@@ -348,19 +381,22 @@
     capacity = max(2, 2 * pairs // owners)
     groups = basis.shape[0]
     basis = basis.reshape(groups * BASIS, EXT3)
-    box, swapped, head = collocated(basis, density_blocks, pair_groups)
+    box, swapped, near_table = collocated(basis, density_blocks, pair_groups)
     box = merged_z(box, swapped, "gz")
-    y_low, y_high = merged(box[0], box[1], "gy")
-    box = jnp.stack([y_low, y_high])
-    x_low, x_high = merged(box[:, : EXT // 2], box[:, EXT // 2 :], "gx")
-    potential_ext = slater_potential(jnp.concatenate([x_low, x_high], axis=1))
-    potential = potential_ext.reshape(2, EXT, EXT // 2, EXT)[:, RIM : RIM + CELLS, :, RIM : RIM + CELLS]
-    potential = jnp.concatenate([potential[0, :, RIM:], potential[1, :, :RIM]], axis=1)
-
-    send = integrated(
-        head, basis, potential_ext, pair_groups, owner, owner_slot, owners, capacity
+    box = jnp.stack(merged(box[0], box[1], "gy"))
+    odd, near, far = merged_halves(box[:, : EXT // 2], box[:, EXT // 2 :], "gx")
+    near, far = slater_potential(near), slater_potential(far)
+
+    total, far_table = integrated_near(near_table, basis, near)
+    send = integrated_far(
+        far_table, total, far, pair_groups, owner, owner_slot, owners, capacity
     )
     got = lax.all_to_all(send, ("gx", "gy"), split_axis=0, concat_axis=0, tiled=True)
+
+    potential = jnp.concatenate(
+        [jnp.where(odd, near, far)[:, RIM:], jnp.where(odd, far, near)[:, :RIM]], axis=1
+    ).reshape(2, CELLS, EXT // 2, EXT)[..., RIM : RIM + CELLS]
+    potential = jnp.concatenate([potential[0, :, RIM:], potential[1, :, :RIM]], axis=1)
     return stored_blocks(got, pairs, capacity), potential
 
 

time: 51 us -> 49.9 us (0.978)
  Pallas kernels: 10.2 us -> 11.2 us
  starting transfers between devices: 15.2 us -> 14.2 us
  waiting for transfers between devices: 23.5 us -> 22.5 us
    pallas_call x1 -> x2, Pallas kernels: 3.7 us -> 5.15 us  [the longest x1 2.66 us: integrated_far(): pl.pallas_call(functools.partial(far_kernel, groups, capacity), name='int...]
    ppermute x4, waiting for transfers between devices: 2.94 us -> 1.64 us  [the longest x2 1.63 us: merged_halves(): far = far + lax.ppermute(far, axis, neighbour_swaps(count, 1))]
    all_to_all x1, starting transfers between devices: 8.23 us -> 7.29 us  [per_device(): lax.all_to_all(send, ('gx', 'gy'), split_axis=0, concat_axis=0, tiled=True)]
  transfers between devices with their start and end apart: 6 -> 6, of which waited for: 4 -> 3; matrix products, arithmetic and copies ran while one was open for 2% -> 2% of each run, Pallas kernels for 0% -> 5%
where the time goes in v5:
time: 49.9 us; the launch traced here: 49.5 us
  waiting for transfers between devices  22.5 us (45%)
  starting transfers between devices  14.2 us (28%)
  Pallas kernels  11.2 us (22%)
  other arithmetic  0.73 us (1%)
  between operations  0.71 us (1%)
    all_to_all x1, waiting for transfers between devices, per_device(): lax.all_to_all(send, ('gx', 'gy'), split_axis=0, concat_axis=0, tiled=True)  19.5 us
    all_to_all x1, starting transfers between devices, per_device(): lax.all_to_all(send, ('gx', 'gy'), split_axis=0, concat_axis=0, tiled=True)  7.29 us
    ppermute x2, starting transfers between devices, merged_halves(): far = far + lax.ppermute(far, axis, neighbour_swaps(count, 1))  5.56 us
    pallas_call x1, Pallas kernels, collocated(): pl.pallas_call(functools.partial(collocate_kernel, groups), name='colloca...  4.09 us
    pallas_call x1, Pallas kernels, integrated_far(): pl.pallas_call(functools.partial(far_kernel, groups, capacity), name='int...  2.66 us
    pallas_call x1, Pallas kernels, integrated_near(): pl.pallas_call(near_kernel, name='integrate_near', out_shape=(jax.ShapeDt...  2.49 us
    pallas_call x1, Pallas kernels, stored_blocks(): pl.pallas_call(functools.partial(store_kernel, capacity), name='store', o...  1.99 us
    ppermute x2, waiting for transfers between devices, merged_halves(): far = far + lax.ppermute(far, axis, neighbour_swaps(count, 1))  1.63 us
  transfers between devices with their start and end apart: 6, of which 3 were waited for; matrix products, arithmetic and copies ran while one was open for 2% of the time, Pallas kernels for 5%

profile of v5, /device:TPU:9, one launch (start us, length us, event | category | flops | bytes accessed | tf_op | source)
XLA Modules:
  0.0 49.5 jit_solution(14585538836981322631)
XLA Ops:
  0.6 4.1 %collocate.1 = (f32[2,16,128]{2,1,0:T(8,128)S(1)}, f32[2,16,128]{2,1,0:T(8,128)S(1)}, bf16[448,2048]{1,0:T(8,128)(2,1)S(1)}) custom-call(s32[2,48]{1,0:T(2,128)} %pair_groups.3, bf16[48,4096]{1,0:T(8,128)(2,1)} %blocks.1, bf16[448,4096]{1,0:T(8,128)(2,1)} %bitcast.15), custom_call_target="tpu_custom_call" | custom-call | flops 1644167168 | bytes 3670016 | tf_op jit(solution)/shard_map/collocate/pallas_call | solution.py:137
  4.7 1.3 %collective-permute-start = (f32[2,16,128]{2,1,0:T(8,128)S(1)}, f32[2,16,128]{2,1,0:T(8,128)S(1)}, u32[]{:S(2)}, u32[]{:S(2)}) collective-permute-start(f32[2,16,128]{2,1,0:T(8,128)S(1)} %get-tuple-element.8), channel_id=1, source_target_pairs={{0,1},{1,0},{2,3},{3,2},{4,5},{5,4},{6,7},{7,6},{8,9},{9,8},{10,11... | collective-permute-start | bytes 49160 | tf_op jit(solution)/shard_map/ppermute | solution.py:50
  6.0 1.4 %collective-permute-done = f32[2,16,128]{2,1,0:T(8,128)S(1)} collective-permute-done((f32[2,16,128]{2,1,0:T(8,128)S(1)}, f32[2,16,128]{2,1,0:T(8,128)S(1)}, u32[]{:S(2)}, u32[]{:S(2)}) %collective-permute-start) | collective-permute-done | bytes 16416 | tf_op jit(solution)/shard_map/ppermute | solution.py:50
  7.4 3.0 %collective-permute-start.2 = (f32[16,128]{1,0:T(8,128)S(1)}, f32[16,128]{1,0:T(8,128)S(1)}, u32[]{:S(2)}, u32[]{:S(2)}) collective-permute-start(f32[16,128]{1,0:T(8,128)S(1)} %get-tuple-element.21), channel_id=1, source_target_pairs={{2,4},{4,2},{6,0},{0,6},{3,5},{5,3},{7,1},{1,7},{10,12},{12,10},{1... | collective-permute-start | bytes 24584 | tf_op jit(solution)/shard_map/ppermute | solution.py:38
  10.4 0.0 collective-permute-start.1
  10.4 1.6 %collective-permute-done.2 = f32[16,128]{1,0:T(8,128)S(1)} collective-permute-done((f32[16,128]{1,0:T(8,128)S(1)}, f32[16,128]{1,0:T(8,128)S(1)}, u32[]{:S(2)}, u32[]{:S(2)}) %collective-permute-start.2) | collective-permute-done | bytes 8224 | tf_op jit(solution)/shard_map/ppermute | solution.py:38
  12.0 0.0 collective-permute-done.1
  12.0 0.1 collective-permute-start.4
  12.1 2.6 %collective-permute-start.3 = (f32[2,8,128]{2,1,0:T(8,128)S(1)}, f32[2,8,128]{2,1,0:T(8,128)S(1)}, u32[]{:S(2)}, u32[]{:S(2)}) collective-permute-start(f32[2,8,128]{2,1,0:T(8,128)S(1)} %get-tuple-element.19), channel_id=1, source_target_pairs={{8,16},{16,8},{24,0},{0,24},{9,17},{17,9},{25,1},{1,25},{10,18},{1... | collective-permute-start | bytes 24584 | tf_op jit(solution)/shard_map/ppermute | solution.py:38
  14.7 0.0 collective-permute-done.4
  14.7 2.5 %integrate_near.1 = (f32[448,512]{1,0:T(8,128)S(1)}, bf16[448,2048]{1,0:T(8,128)(2,1)S(1)}) custom-call(f32[2,8,128]{2,1,0:T(8,128)S(1)} %cbrt_divide_fusion.potential, bf16[448,2048]{1,0:T(8,128)(2,1)S(1)} %get-tuple-element.9.near, bf16[448,4096]{1,0:T(8,128)(2,1)} %bitcast.16), custom_call_target="tpu_custom_call" | custom-call | flops 822083584 | bytes 3670016 | tf_op jit(solution)/shard_map/integrate_near/pallas_call | solution.py:276
  17.2 0.0 collective-permute-done.3
  17.3 2.7 %integrate_far.1 = bf16[16,200,128]{2,1,0:T(8,128)(2,1)} custom-call(s32[2,48]{1,0:T(2,128)} %pair_groups.3, s32[1,48]{1,0:T(1,128)} %bitcast.17, s32[1,48]{1,0:T(1,128)} %bitcast.18, f32[2,8,128]{2,1,0:T(8,128)S(1)} %cbrt_divide_fusion.1.potential, bf16[448,2048]{1,0:T(8,128)(2,1)S(1)} %get-tuple-element.10.far, f32[448,512]{1,0:T(8,128)S(1)} %get-tuple-element.11.near_total), custom_call_target="tpu_custom_call" | custom-call | flops 822083584 | bytes 3670016 | tf_op jit(solution)/shard_map/integrate_far/pallas_call | solution.py:297
  19.9 7.3 %all-to-all-start = ((bf16[16,200,128]{2,1,0:T(8,128)(2,1)}), bf16[16,200,128]{2,1,0:T(8,128)(2,1)S(1)}, u32[]{:S(2)}, u32[]{:S(2)}) async-start(bf16[16,200,128]{2,1,0:T(8,128)(2,1)} %integrate_far.1), calls=%async_computation | async-start | bytes 1638400 | tf_op jit(solution)/shard_map/all_to_all | solution.py:394
  27.3 0.1 reshape.23
  27.3 0.1 slice_bitcast_fusion.1
  27.4 0.6 %pad_maximum_fusion = f32[8,8,8]{2,1,0:T(8,128)} fusion(f32[8,4,8]{2,1,0:T(4,128)S(1)} %get-tuple-element.13, f32[8,4,8]{2,1,0:T(4,128)S(1)} %get-tuple-element.12), kind=kLoop, calls=%fused_computation | loop fusion | flops 512 | bytes 4096 | tf_op jit(solution)/shard_map/concatenate | solution.py:399
  28.1 19.5 %all-to-all-done.got = bf16[16,200,128]{2,1,0:T(8,128)(2,1)S(1)} async-done(((bf16[16,200,128]{2,1,0:T(8,128)(2,1)}), bf16[16,200,128]{2,1,0:T(8,128)(2,1)S(1)}, u32[]{:S(2)}, u32[]{:S(2)}) %all-to-all-start) | async-done | bytes 819232 | tf_op jit(solution)/shard_map/all_to_all | solution.py:394
  47.5 2.0 %store.1 = bf16[48,4096]{1,0:T(8,128)(2,1)} custom-call(bf16[16,200,128]{2,1,0:T(8,128)(2,1)S(1)} %all-to-all-done.got), custom_call_target="tpu_custom_call" | custom-call | flops 409600 | bytes 819200 | tf_op jit(solution)/shard_map/store/pallas_call | solution.py:359
  (8 shorter events, 0.1 us)
Async XLA Ops:
  4.7 2.7 %collective-permute-start = (f32[2,16,128]{2,1,0:T(8,128)S(1)}, f32[2,16,128]{2,1,0:T(8,128)S(1)}, u32[]{:S(2)}, u32[]{:S(2)}) collective-permute-start(f32[2,16,128]{2,1,0:T(8,128)S(1)} %get-tuple-element.8), channel_id=1, source_target_pairs={{0,1},{1,0},{2,3},{3,2},{4,5},{5,4},{6,7},{7,6},{8,9},{9,8},{10,11... | collective-permute-start | bytes 49160 | tf_op jit(solution)/shard_map/ppermute | solution.py:50
  7.4 4.6 %collective-permute-start.2 = (f32[16,128]{1,0:T(8,128)S(1)}, f32[16,128]{1,0:T(8,128)S(1)}, u32[]{:S(2)}, u32[]{:S(2)}) collective-permute-start(f32[16,128]{1,0:T(8,128)S(1)} %get-tuple-element.21), channel_id=1, source_target_pairs={{2,4},{4,2},{6,0},{0,6},{3,5},{5,3},{7,1},{1,7},{10,12},{12,10},{1... | collective-permute-start | bytes 24584 | tf_op jit(solution)/shard_map/ppermute | solution.py:38
  10.4 1.6 %collective-permute-start.1 = (f32[16,128]{1,0:T(8,128)S(1)}, f32[16,128]{1,0:T(8,128)S(1)}, u32[]{:S(2)}, u32[]{:S(2)}) collective-permute-start(f32[16,128]{1,0:T(8,128)S(1)} %get-tuple-element.20), channel_id=1, source_target_pairs={{0,2},{2,0},{4,6},{6,4},{1,3},{3,1},{5,7},{7,5},{8,10},{10,8},{12,... | collective-permute-start | bytes 24584 | tf_op jit(solution)/shard_map/ppermute | solution.py:37
  12.0 2.7 %collective-permute-start.4 = (f32[2,8,128]{2,1,0:T(8,128)S(1)}, f32[2,8,128]{2,1,0:T(8,128)S(1)}, u32[]{:S(2)}, u32[]{:S(2)}) collective-permute-start(f32[2,8,128]{2,1,0:T(8,128)S(1)} %get-tuple-element.18), channel_id=1, source_target_pairs={{0,8},{8,0},{16,24},{24,16},{1,9},{9,1},{17,25},{25,17},{2,10},{10... | collective-permute-start | bytes 24584 | tf_op jit(solution)/shard_map/ppermute | solution.py:37
  12.1 5.1 %collective-permute-start.3 = (f32[2,8,128]{2,1,0:T(8,128)S(1)}, f32[2,8,128]{2,1,0:T(8,128)S(1)}, u32[]{:S(2)}, u32[]{:S(2)}) collective-permute-start(f32[2,8,128]{2,1,0:T(8,128)S(1)} %get-tuple-element.19), channel_id=1, source_target_pairs={{8,16},{16,8},{24,0},{0,24},{9,17},{17,9},{25,1},{1,25},{10,18},{1... | collective-permute-start | bytes 24584 | tf_op jit(solution)/shard_map/ppermute | solution.py:38
  19.9 27.6 %all-to-all-start = ((bf16[16,200,128]{2,1,0:T(8,128)(2,1)}), bf16[16,200,128]{2,1,0:T(8,128)(2,1)S(1)}, u32[]{:S(2)}, u32[]{:S(2)}) async-start(bf16[16,200,128]{2,1,0:T(8,128)(2,1)} %integrate_far.1), calls=%async_computation | async-start | bytes 1638400 | tf_op jit(solution)/shard_map/all_to_all | solution.py:394

commit v6 on v5

--- a/solution.py
+++ b/solution.py
@@ -1,4 +1,5 @@
 import functools
+import math
 
 import jax
 import jax.numpy as jnp
@@ -6,6 +7,7 @@
 from jax.experimental import pallas as pl
 from jax.experimental.pallas import tpu as pltpu
 from jax.sharding import PartitionSpec as P
+
 
 BASIS = 64
 CELLS = 8
@@ -161,23 +163,20 @@
     )(*in_hbm(pair_groups, density_blocks, basis))
 
 
-def tabulate(groups, capacity, codes, owner, slot, counts, place, slot_rows):
+def tabulate(groups, codes, owner, counts, place):
     pairs, owners = codes.shape[1], counts.shape[0]
+    lines = BASIS // 2
     for o in range(owners):
         counts[o] = 0
     for code in range(groups * groups):
         place[0, code] = -1
-    slot_rows[...] = jnp.full(slot_rows.shape, pairs, jnp.float32)
-    lane = lax.broadcasted_iota(jnp.int32, (1, LANES), 1)
     for p in range(pairs):
         o = owner[0, p]
         rank = counts[o]
         counts[o] = rank + 1
         code = codes[0, p] * groups + codes[1, p]
         place[0, code] = o
-        place[1, code] = rank
-        row = slot_rows[pl.ds(o, 1), :]
-        slot_rows[pl.ds(o, 1), :] = jnp.where(lane == rank, slot[0, p].astype(jnp.float32), row)
+        place[1, code] = rank * lines
     free_owner, free_rank = jnp.int32(0), counts[0]
     for o in range(1, owners):
         fewer = counts[o] < free_rank
@@ -185,7 +184,7 @@
         free_rank = jnp.where(fewer, counts[o], free_rank)
     for code in range(groups * groups):
         absent = place[0, code] < 0
-        place[1, code] = jnp.where(absent, free_rank, place[1, code])
+        place[1, code] = jnp.where(absent, free_rank * lines, place[1, code])
         place[0, code] = jnp.where(absent, free_owner, place[0, code])
 
 
@@ -206,45 +205,42 @@
         )
 
 
-def near_kernel(potential, near, basis, total, far, arrived):
+def near_kernel(
+    groups, pair_groups, owner, potential, near, basis, total, far, places,
+    codes, owners_of, counts, place, arrived, staged,
+):
     rows = near.shape[0]
     begin = pl.multiple_of(halves()[1], LANES)
-    copy = pltpu.make_async_copy(basis.at[:, pl.ds(begin, far.shape[1])], far, arrived)
-    copy.start()
+    far_copy = pltpu.make_async_copy(basis.at[:, pl.ds(begin, far.shape[1])], far, arrived)
+    codes_copy = pltpu.make_async_copy(pair_groups, codes, staged.at[0])
+    owner_copy = pltpu.make_async_copy(owner, owners_of, staged.at[1])
+    for copy in (codes_copy, owner_copy, far_copy):
+        copy.start()
     for c, part in enumerate(overlaps(near, potential)):
         if c == 0:
             total[:, :rows] = part
+            codes_copy.wait()
+            owner_copy.wait()
+            tabulate(groups, codes, owners_of, counts, place)
         else:
             total[:, :rows] += part
-    copy.wait()
-
-
-def far_kernel(
-    groups, capacity, pair_groups, owner, owner_slot, potential, far, near_total, send,
-    total, slot_rows, codes, owners_of, slots_of, counts, place, staged,
-):
+    places_copy = pltpu.make_async_copy(place, places, staged.at[2])
+    places_copy.start()
+    places_copy.wait()
+    far_copy.wait()
+
+
+def far_kernel(groups, places, potential, far, near_total, send, total, blocks, place, staged, sent):
     rows = groups * BASIS
     lines = BASIS // 2
-    tables = [
-        pltpu.make_async_copy(source, target, staged.at[i])
-        for i, (source, target) in enumerate(
-            [(pair_groups, codes), (owner, owners_of), (owner_slot, slots_of)]
-        )
-    ]
-    for copy in tables:
-        copy.start()
+    places_copy = pltpu.make_async_copy(places, place, staged)
+    places_copy.start()
     for c, part in enumerate(overlaps(far, potential)):
         if c == 0:
             total[:, :rows] = near_total[:, :rows] + part
-            for copy in tables:
-                copy.wait()
-            tabulate(groups, capacity, codes, owners_of, slots_of, counts, place, slot_rows)
         else:
             total[:, :rows] += part
-    for o in range(send.shape[0]):
-        send[o, capacity * lines :, :] = jnp.broadcast_to(
-            slot_rows[o : o + 1, :], (send.shape[1] - capacity * lines, LANES)
-        ).astype(send.dtype)
+    places_copy.wait()
     left = lax.broadcasted_iota(jnp.int32, (lines, LANES), 1) < BASIS
     for first in range(groups):
         for second in range(groups):
@@ -256,10 +252,12 @@
                 lower = pltpu.roll(lower, BASIS, axis=1)
             else:
                 upper = pltpu.roll(upper, BASIS, axis=1)
-            line = pl.multiple_of(place[1, code] * lines, lines)
-            send[place[0, code], pl.ds(line, lines), :] = (
-                jnp.where(left, upper, lower) * GRID_WEIGHT
-            ).astype(send.dtype)
+            blocks[code] = (jnp.where(left, upper, lower) * GRID_WEIGHT).astype(blocks.dtype)
+            line = pl.multiple_of(place[1, code], lines)
+            pltpu.make_async_copy(
+                blocks.at[code], send.at[place[0, code], pl.ds(line, lines), :], sent
+            ).start()
+    pltpu.make_async_copy(blocks, blocks, sent).wait()
 
 
 def in_hbm(*arrays):
@@ -270,68 +268,65 @@
     return -(-rows // LANES) * LANES
 
 
-def integrated_near(near, basis, potential):
-    rows = basis.shape[0]
+def integrated_near(near, basis, potential, pair_groups, owner, owners):
+    rows, pairs = basis.shape[0], pair_groups.shape[1]
+    groups = rows // BASIS
     vmem, hbm = pl.BlockSpec(memory_space=pltpu.VMEM), pl.BlockSpec(memory_space=pltpu.HBM)
     return pl.pallas_call(
-        near_kernel,
+        functools.partial(near_kernel, groups),
         name="integrate_near",
         out_shape=(
             jax.ShapeDtypeStruct((rows, padded(rows)), jnp.float32),
             jax.ShapeDtypeStruct((rows, EXT3 // 2), basis.dtype),
-        ),
-        in_specs=[vmem, vmem, hbm],
-        out_specs=[vmem, vmem],
-        scratch_shapes=[pltpu.SemaphoreType.DMA(())],
-        compiler_params=pltpu.CompilerParams(vmem_limit_bytes=24 << 20),
-        cost_estimate=pl.CostEstimate(
-            flops=rows * rows * EXT3, bytes_accessed=2 * rows * EXT3, transcendentals=0
-        ),
-    )(potential, near, *in_hbm(basis))
-
-
-def integrated_far(far, near_total, potential, pair_groups, owner, owner_slot, owners, capacity):
-    rows, pairs = far.shape[0], pair_groups.shape[1]
-    groups = rows // BASIS
-    vmem, hbm = pl.BlockSpec(memory_space=pltpu.VMEM), pl.BlockSpec(memory_space=pltpu.HBM)
-    return pl.pallas_call(
-        functools.partial(far_kernel, groups, capacity),
-        name="integrate_far",
-        out_shape=jax.ShapeDtypeStruct((owners, capacity * BASIS // 2 + 8, LANES), jnp.bfloat16),
-        in_specs=[hbm, hbm, hbm, vmem, vmem, vmem],
-        out_specs=vmem,
+            jax.ShapeDtypeStruct((2, groups * groups), jnp.int32),
+        ),
+        in_specs=[hbm, hbm, vmem, vmem, hbm],
+        out_specs=[vmem, vmem, hbm],
         scratch_shapes=[
-            pltpu.VMEM((rows, padded(rows)), jnp.float32),
-            pltpu.VMEM((owners, LANES), jnp.float32),
             pltpu.SMEM((2, pairs), jnp.int32),
-            pltpu.SMEM((1, pairs), jnp.int32),
             pltpu.SMEM((1, pairs), jnp.int32),
             pltpu.SMEM((owners,), jnp.int32),
             pltpu.SMEM((2, groups * groups), jnp.int32),
+            pltpu.SemaphoreType.DMA(()),
             pltpu.SemaphoreType.DMA((3,)),
         ],
         compiler_params=pltpu.CompilerParams(vmem_limit_bytes=24 << 20),
         cost_estimate=pl.CostEstimate(
             flops=rows * rows * EXT3, bytes_accessed=2 * rows * EXT3, transcendentals=0
         ),
-    )(
-        *in_hbm(pair_groups, owner.reshape(1, pairs), owner_slot.reshape(1, pairs)),
-        potential,
-        far,
-        near_total,
-    )
-
-
-def store_kernel(capacity, got, store, total, slots_vector, slots, moved):
+    )(*in_hbm(pair_groups, owner.reshape(1, pairs)), potential, near, *in_hbm(basis))
+
+
+def integrated_far(far, near_total, potential, places, owners, capacity):
+    rows = far.shape[0]
+    groups = rows // BASIS
+    vmem, hbm = pl.BlockSpec(memory_space=pltpu.VMEM), pl.BlockSpec(memory_space=pltpu.HBM)
+    return pl.pallas_call(
+        functools.partial(far_kernel, groups),
+        name="integrate_far",
+        out_shape=jax.ShapeDtypeStruct((owners, capacity * BASIS // 2, LANES), jnp.bfloat16),
+        in_specs=[hbm, vmem, vmem, vmem],
+        out_specs=hbm,
+        scratch_shapes=[
+            pltpu.VMEM((rows, padded(rows)), jnp.float32),
+            pltpu.VMEM((groups * groups, BASIS // 2, LANES), jnp.bfloat16),
+            pltpu.SMEM(places.shape, jnp.int32),
+            pltpu.SemaphoreType.DMA(()),
+            pltpu.SemaphoreType.DMA(()),
+        ],
+        compiler_params=pltpu.CompilerParams(vmem_limit_bytes=24 << 20),
+        cost_estimate=pl.CostEstimate(
+            flops=rows * rows * EXT3, bytes_accessed=2 * rows * EXT3, transcendentals=0
+        ),
+    )(places, potential, far, near_total)
+
+
+def store_kernel(capacity, got, slot_of, store, total, packed, slots, moved, written):
     lines = BASIS // 2
     pitch = lines + 1
     sources = got.shape[0]
     stored = store.shape[0]
-    for s in range(sources):
-        slots_vector[s : s + 1, :] = (
-            got[s, capacity * lines : capacity * lines + 8, :].astype(jnp.float32)[:1].astype(jnp.int32)
-        )
-    copy = pltpu.make_async_copy(slots_vector, slots, moved)
+    copy = pltpu.make_async_copy(slot_of, slots, moved)
     copy.start()
     total[...] = jnp.zeros_like(total)
     copy.wait()
@@ -344,35 +339,77 @@
 
     lax.fori_loop(0, sources, add, 0)
     in_low = lax.broadcasted_iota(jnp.int32, (stored, LANES), 1) < BASIS
-    for i in range(lines // 2):
-        even = total[pl.ds(2 * i, stored, stride=pitch), :]
-        odd = total[pl.ds(2 * i + 1, stored, stride=pitch), :]
-        for j, row in (
-            (i, jnp.where(in_low, even, pltpu.roll(odd, BASIS, axis=1))),
-            (i + lines // 2, jnp.where(in_low, pltpu.roll(even, BASIS, axis=1), odd)),
-        ):
-            store[:, j * LANES : (j + 1) * LANES] = row.astype(store.dtype)
-
-
-def stored_blocks(got, rows, capacity):
-    vmem = pl.BlockSpec(memory_space=pltpu.VMEM)
+    pieces = 4
+    span = lines // 2 // pieces
+    copies = []
+    for piece in range(pieces):
+        for i in range(piece * span, (piece + 1) * span):
+            even = total[pl.ds(2 * i, stored, stride=pitch), :]
+            odd = total[pl.ds(2 * i + 1, stored, stride=pitch), :]
+            for j, row in (
+                (i, jnp.where(in_low, even, pltpu.roll(odd, BASIS, axis=1))),
+                (i + lines // 2, jnp.where(in_low, pltpu.roll(even, BASIS, axis=1), odd)),
+            ):
+                packed[:, j * LANES : (j + 1) * LANES] = row.astype(packed.dtype)
+        for half in range(2):
+            columns = pl.ds((half * lines // 2 + piece * span) * LANES, span * LANES)
+            copies.append(
+                pltpu.make_async_copy(
+                    packed.at[:, columns], store.at[:, columns], written.at[len(copies)]
+                )
+            )
+            copies[-1].start()
+    for copy in copies:
+        copy.wait()
+
+
+def stored_blocks(got, slot_of, rows, capacity):
+    vmem, hbm = pl.BlockSpec(memory_space=pltpu.VMEM), pl.BlockSpec(memory_space=pltpu.HBM)
     return pl.pallas_call(
         functools.partial(store_kernel, capacity),
         name="store",
         out_shape=jax.ShapeDtypeStruct((rows, BASIS * BASIS), jnp.bfloat16),
-        in_specs=[vmem],
-        out_specs=vmem,
+        in_specs=[vmem, vmem],
+        out_specs=hbm,
         scratch_shapes=[
             pltpu.VMEM(((rows + 1) * (BASIS // 2 + 1) + 7, LANES), jnp.float32),
-            pltpu.VMEM((got.shape[0], LANES), jnp.int32),
-            pltpu.SMEM((got.shape[0], LANES), jnp.int32),
+            pltpu.VMEM((rows, BASIS * BASIS), jnp.bfloat16),
+            pltpu.SMEM(slot_of.shape, jnp.int32),
             pltpu.SemaphoreType.DMA(()),
+            pltpu.SemaphoreType.DMA((8,)),
         ],
         compiler_params=pltpu.CompilerParams(vmem_limit_bytes=24 << 20),
         cost_estimate=pl.CostEstimate(
             flops=got.size, bytes_accessed=2 * got.size, transcendentals=0
         ),
-    )(got)
+    )(got, slot_of)
+
+
+def gathered(row, axes):
+    sizes = [lax.axis_size(axis) for axis in axes]
+    count = math.prod(sizes)
+    member = lax.broadcasted_iota(jnp.int32, (count, row.shape[-1]), 0)
+    table = jnp.where(member == lax.axis_index(axes), row[None, :], 0.0)
+    for axis, size in zip(axes[::-1], sizes[::-1]):
+        step = 1
+        while step < size:
+            other = lax.ppermute(table, axis, [(i, i ^ step) for i in range(size)])
+            table = table + other
+            step *= 2
+    return table
+
+
+def slots_of_sources(owner, owner_slot, axes):
+    pairs = owner_slot.shape[0]
+    named = jnp.pad((owner[:, 0] * pairs + owner_slot + 1).astype(jnp.float32), (0, LANES - pairs))
+    named = gathered(named, axes)[:, :pairs].astype(jnp.int32) - 1
+    slot = named - lax.axis_index(axes) * pairs
+    mine = (slot >= 0) & (slot < pairs)
+    order = jnp.arange(pairs, dtype=jnp.int32)
+    before = mine[:, None, :] & (order[None, None, :] < order[None, :, None])
+    rank = jnp.where(mine, jnp.sum(before.astype(jnp.int32), axis=2), -1)
+    at_rank = rank[:, None, :] == jnp.arange(LANES, dtype=jnp.int32)[None, :, None]
+    return jnp.sum(jnp.where(at_rank, slot[:, None, :] - pairs, 0), axis=2) + pairs
 
 
 def per_device(basis, density_blocks, pair_groups, owner, owner_slot):
@@ -387,17 +424,19 @@
     odd, near, far = merged_halves(box[:, : EXT // 2], box[:, EXT // 2 :], "gx")
     near, far = slater_potential(near), slater_potential(far)
 
-    total, far_table = integrated_near(near_table, basis, near)
-    send = integrated_far(
-        far_table, total, far, pair_groups, owner, owner_slot, owners, capacity
+    total, far_table, places = integrated_near(
+        near_table, basis, near, pair_groups, owner, owners
     )
+    send = integrated_far(far_table, total, far, places, owners, capacity)
+    send, late_owner, late_slot = lax.optimization_barrier((send, owner, owner_slot))
     got = lax.all_to_all(send, ("gx", "gy"), split_axis=0, concat_axis=0, tiled=True)
+    slot_of = slots_of_sources(late_owner, late_slot, ("gx", "gy"))
 
     potential = jnp.concatenate(
         [jnp.where(odd, near, far)[:, RIM:], jnp.where(odd, far, near)[:, :RIM]], axis=1
     ).reshape(2, CELLS, EXT // 2, EXT)[..., RIM : RIM + CELLS]
     potential = jnp.concatenate([potential[0, :, RIM:], potential[1, :, :RIM]], axis=1)
-    return stored_blocks(got, pairs, capacity), potential
+    return stored_blocks(got, slot_of, pairs, capacity), potential
 
 
 def solution(mesh):

time: 49.9 us -> 51.7 us (1.036)
  the two profiles are of different devices: /device:TPU:9 before, /device:TPU:0 now
where the time goes in v6:
time: 51.7 us; the launch traced here: 51.4 us
  starting transfers between devices  21.2 us (41%)
  waiting for transfers between devices  17.2 us (33%)
  Pallas kernels  10.4 us (20%)
  other arithmetic  1.62 us (3%)
  between operations  0.83 us (2%)
    ppermute x4, waiting for transfers between devices, gathered(): other = lax.ppermute(table, axis, [(i, i ^ step) for i in range(size)])  13.8 us
    ppermute x4, starting transfers between devices, gathered(): other = lax.ppermute(table, axis, [(i, i ^ step) for i in range(size)])  6.44 us
    all_to_all x1, starting transfers between devices, per_device(): lax.all_to_all(send, ('gx', 'gy'), split_axis=0, concat_axis=0, tiled=True)  4.91 us
    pallas_call x1, Pallas kernels, collocated(): pl.pallas_call(functools.partial(collocate_kernel, groups), name='colloca...  4.09 us
    ppermute x2, starting transfers between devices, merged_halves(): near = near + lax.ppermute(near, axis, neighbour_swaps(count, 0))  4.02 us
    ppermute x1, starting transfers between devices, merged_z(): return box + lax.ppermute(swapped, axis, neighbour_swaps(count, 0))  3.06 us
    ppermute x2, starting transfers between devices, merged_halves(): far = far + lax.ppermute(far, axis, neighbour_swaps(count, 1))  2.82 us
    pallas_call x1, Pallas kernels, integrated_near(): pl.pallas_call(functools.partial(near_kernel, groups), name='integrate_ne...  2.25 us
  transfers between devices with their start and end apart: 10, of which 6 were waited for; matrix products, arithmetic and copies ran while one was open for 3% of the time, Pallas kernels for 4%

profile of v6, /device:TPU:0, one launch (start us, length us, event | category | flops | bytes accessed | tf_op | source)
XLA Modules:
  0.0 51.4 jit_solution(15094815460199373369)
XLA Ops:
  0.6 4.1 %collocate.1 = (f32[2,16,128]{2,1,0:T(8,128)S(1)}, f32[2,16,128]{2,1,0:T(8,128)S(1)}, bf16[448,2048]{1,0:T(8,128)(2,1)S(1)}) custom-call(s32[2,48]{1,0:T(2,128)} %pair_groups.3, bf16[48,4096]{1,0:T(8,128)(2,1)} %blocks.1, bf16[448,4096]{1,0:T(8,128)(2,1)} %bitcast.20), custom_call_target="tpu_custom_call" | custom-call | flops 1644167168 | bytes 3670016 | tf_op jit(solution)/shard_map/collocate/pallas_call | solution.py:139
  4.7 3.1 %collective-permute-start = (f32[2,16,128]{2,1,0:T(8,128)S(1)}, f32[2,16,128]{2,1,0:T(8,128)S(1)}, u32[]{:S(2)}, u32[]{:S(2)}) collective-permute-start(f32[2,16,128]{2,1,0:T(8,128)S(1)} %get-tuple-element.12), channel_id=1, source_target_pairs={{0,1},{1,0},{2,3},{3,2},{4,5},{5,4},{6,7},{7,6},{8,9},{9,8},{10,11... | collective-permute-start | bytes 49160 | tf_op jit(solution)/shard_map/ppermute | solution.py:52
  7.8 1.7 %collective-permute-done = f32[2,16,128]{2,1,0:T(8,128)S(1)} collective-permute-done((f32[2,16,128]{2,1,0:T(8,128)S(1)}, f32[2,16,128]{2,1,0:T(8,128)S(1)}, u32[]{:S(2)}, u32[]{:S(2)}) %collective-permute-start) | collective-permute-done | bytes 16416 | tf_op jit(solution)/shard_map/ppermute | solution.py:52
  9.5 0.3 collective-permute-start.2
  9.9 1.8 %collective-permute-start.1 = (f32[16,128]{1,0:T(8,128)S(1)}, f32[16,128]{1,0:T(8,128)S(1)}, u32[]{:S(2)}, u32[]{:S(2)}) collective-permute-start(f32[16,128]{1,0:T(8,128)S(1)} %get-tuple-element.28), channel_id=1, source_target_pairs={{0,2},{2,0},{4,6},{6,4},{1,3},{3,1},{5,7},{7,5},{8,10},{10,8},{12,... | collective-permute-start | bytes 24584 | tf_op jit(solution)/shard_map/ppermute | solution.py:39
  11.7 0.9 %collective-permute-done.2 = f32[16,128]{1,0:T(8,128)S(1)} collective-permute-done((f32[16,128]{1,0:T(8,128)S(1)}, f32[16,128]{1,0:T(8,128)S(1)}, u32[]{:S(2)}, u32[]{:S(2)}) %collective-permute-start.2) | collective-permute-done | bytes 8224 | tf_op jit(solution)/shard_map/ppermute | solution.py:40
  12.7 2.2 %collective-permute-start.3 = (f32[2,8,128]{2,1,0:T(8,128)S(1)}, f32[2,8,128]{2,1,0:T(8,128)S(1)}, u32[]{:S(2)}, u32[]{:S(2)}) collective-permute-start(f32[2,8,128]{2,1,0:T(8,128)S(1)} %get-tuple-element.27), channel_id=1, source_target_pairs={{0,8},{8,0},{16,24},{24,16},{1,9},{9,1},{17,25},{25,17},{2,10},{10... | collective-permute-start | bytes 24584 | tf_op jit(solution)/shard_map/ppermute | solution.py:39
  14.9 2.5 %collective-permute-start.4 = (f32[2,8,128]{2,1,0:T(8,128)S(1)}, f32[2,8,128]{2,1,0:T(8,128)S(1)}, u32[]{:S(2)}, u32[]{:S(2)}) collective-permute-start(f32[2,8,128]{2,1,0:T(8,128)S(1)} %get-tuple-element.26), channel_id=1, source_target_pairs={{8,16},{16,8},{24,0},{0,24},{9,17},{17,9},{25,1},{1,25},{10,18},{1... | collective-permute-start | bytes 24584 | tf_op jit(solution)/shard_map/ppermute | solution.py:40
  17.4 2.2 %integrate_near.1 = (f32[448,512]{1,0:T(8,128)S(1)}, bf16[448,2048]{1,0:T(8,128)(2,1)S(1)}, s32[2,49]{1,0:T(2,128)S(1)}) custom-call(s32[2,48]{1,0:T(2,128)} %pair_groups.3, s32[1,48]{1,0:T(1,128)} %bitcast.22, f32[2,8,128]{2,1,0:T(8,128)S(1)} %cbrt_divide_fusion.1.potential, bf16[448,2048]{1,0:T(8,128)(2,1)S(1)} %get-tuple-element.13.near, ...), custom_call_target="tpu_custom_call" | custom-call | flops 822083584 | bytes 3670016 | tf_op jit(solution)/shard_map/integrate_near/pallas_call | solution.py:275
  19.7 0.7 %collective-permute-done.4 = f32[2,8,128]{2,1,0:T(8,128)S(1)} collective-permute-done((f32[2,8,128]{2,1,0:T(8,128)S(1)}, f32[2,8,128]{2,1,0:T(8,128)S(1)}, u32[]{:S(2)}, u32[]{:S(2)}) %collective-permute-start.4) | collective-permute-done | bytes 8224 | tf_op jit(solution)/shard_map/ppermute | solution.py:40
  20.4 2.0 %integrate_far.1 = bf16[16,192,128]{2,1,0:T(8,128)(2,1)} custom-call(s32[2,49]{1,0:T(2,128)S(1)} %get-tuple-element.14.places, f32[2,8,128]{2,1,0:T(8,128)S(1)} %cbrt_divide_fusion.potential, bf16[448,2048]{1,0:T(8,128)(2,1)S(1)} %get-tuple-element.15.far, f32[448,512]{1,0:T(8,128)S(1)} %get-tuple-element.16.near_total), custom_call_target="tpu_custom_call" | custom-call | flops 822083584 | bytes 3670016 | tf_op jit(solution)/shard_map/integrate_far/pallas_call | solution.py:304
  22.6 4.9 %all-to-all-start = ((bf16[16,192,128]{2,1,0:T(8,128)(2,1)}), bf16[16,192,128]{2,1,0:T(8,128)(2,1)S(1)}, u32[]{:S(2)}, u32[]{:S(2)}) async-start(bf16[16,192,128]{2,1,0:T(8,128)(2,1)} %integrate_far.1), calls=%async_computation | async-start | bytes 1572864 | tf_op jit(solution)/shard_map/all_to_all | solution.py:432
  27.5 0.1 fusion.4
  27.6 1.9 %collective-permute-start.6 = (f32[16,128]{1,0:T(8,128)S(1)}, f32[16,128]{1,0:T(8,128)S(1)}, u32[]{:S(2)}, u32[]{:S(2)}) collective-permute-start(f32[16,128]{1,0:T(8,128)S(1)} %fusion.4), channel_id=1, source_target_pairs={{0,4},{2,6},{4,0},{6,2},{1,5},{3,7},{5,1},{7,3},{8,12},{10,14},{12... | collective-permute-start | bytes 24584 | tf_op jit(solution)/shard_map/ppermute | solution.py:396
  29.5 0.1 reshape.41
  29.6 4.9 %collective-permute-done.6 = f32[16,128]{1,0:T(8,128)S(1)} collective-permute-done((f32[16,128]{1,0:T(8,128)S(1)}, f32[16,128]{1,0:T(8,128)S(1)}, u32[]{:S(2)}, u32[]{:S(2)}) %collective-permute-start.6) | collective-permute-done | bytes 8224 | tf_op jit(solution)/shard_map/ppermute | solution.py:396
  34.5 0.1 slice_bitcast_fusion.1
  34.6 6.8 %collective-permute-done.7 = f32[16,128]{1,0:T(8,128)S(1)} collective-permute-done((f32[16,128]{1,0:T(8,128)S(1)}, f32[16,128]{1,0:T(8,128)S(1)}, u32[]{:S(2)}, u32[]{:S(2)}) %collective-permute-start.7) | collective-permute-done | bytes 8224 | tf_op jit(solution)/shard_map/ppermute | solution.py:396
  41.4 4.5 %collective-permute-start.8 = (f32[16,128]{1,0:T(8,128)S(1)}, f32[16,128]{1,0:T(8,128)S(1)}, u32[]{:S(2)}, u32[]{:S(2)}) collective-permute-start(f32[16,128]{1,0:T(8,128)S(1)} %add.79), channel_id=1, source_target_pairs={{0,16},{8,24},{16,0},{24,8},{1,17},{9,25},{17,1},{25,9},{2,18},{10... | collective-permute-start | bytes 24584 | tf_op jit(solution)/shard_map/ppermute | solution.py:396
  45.9 0.6 %pad_maximum_fusion = f32[8,8,8]{2,1,0:T(8,128)} fusion(f32[8,4,8]{2,1,0:T(4,128)S(1)} %get-tuple-element.21, f32[8,4,8]{2,1,0:T(4,128)S(1)} %get-tuple-element.20), kind=kLoop, calls=%fused_computation.3 | loop fusion | flops 512 | bytes 4096 | tf_op jit(solution)/shard_map/concatenate | solution.py:438
  46.5 2.2 %collective-permute-done.8 = f32[16,128]{1,0:T(8,128)S(1)} collective-permute-done((f32[16,128]{1,0:T(8,128)S(1)}, f32[16,128]{1,0:T(8,128)S(1)}, u32[]{:S(2)}, u32[]{:S(2)}) %collective-permute-start.8) | collective-permute-done | bytes 8224 | tf_op jit(solution)/shard_map/ppermute | solution.py:396
  48.7 0.4 convert_reduce_fusion
  49.1 0.3 select_reduce_fusion
  49.4 2.0 %store.1 = bf16[48,4096]{1,0:T(8,128)(2,1)} custom-call(bf16[16,192,128]{2,1,0:T(8,128)(2,1)S(1)} %all-to-all-done.got, s32[16,128]{1,0:T(8,128)S(1)} %broadcast_add_fusion.slot_of), custom_call_target="tpu_custom_call" | custom-call | flops 393216 | bytes 786432 | tf_op jit(solution)/shard_map/store/pallas_call | solution.py:368
  (28 shorter events, 0.3 us)
Async XLA Ops:
  4.7 4.8 %collective-permute-start = (f32[2,16,128]{2,1,0:T(8,128)S(1)}, f32[2,16,128]{2,1,0:T(8,128)S(1)}, u32[]{:S(2)}, u32[]{:S(2)}) collective-permute-start(f32[2,16,128]{2,1,0:T(8,128)S(1)} %get-tuple-element.12), channel_id=1, source_target_pairs={{0,1},{1,0},{2,3},{3,2},{4,5},{5,4},{6,7},{7,6},{8,9},{9,8},{10,11... | collective-permute-start | bytes 49160 | tf_op jit(solution)/shard_map/ppermute | solution.py:52
  9.5 3.1 %collective-permute-start.2 = (f32[16,128]{1,0:T(8,128)S(1)}, f32[16,128]{1,0:T(8,128)S(1)}, u32[]{:S(2)}, u32[]{:S(2)}) collective-permute-start(f32[16,128]{1,0:T(8,128)S(1)} %get-tuple-element.29), channel_id=1, source_target_pairs={{2,4},{4,2},{6,0},{0,6},{3,5},{5,3},{7,1},{1,7},{10,12},{12,10},{1... | collective-permute-start | bytes 24584 | tf_op jit(solution)/shard_map/ppermute | solution.py:40
  9.9 2.8 %collective-permute-start.1 = (f32[16,128]{1,0:T(8,128)S(1)}, f32[16,128]{1,0:T(8,128)S(1)}, u32[]{:S(2)}, u32[]{:S(2)}) collective-permute-start(f32[16,128]{1,0:T(8,128)S(1)} %get-tuple-element.28), channel_id=1, source_target_pairs={{0,2},{2,0},{4,6},{6,4},{1,3},{3,1},{5,7},{7,5},{8,10},{10,8},{12,... | collective-permute-start | bytes 24584 | tf_op jit(solution)/shard_map/ppermute | solution.py:39
  12.7 4.7 %collective-permute-start.3 = (f32[2,8,128]{2,1,0:T(8,128)S(1)}, f32[2,8,128]{2,1,0:T(8,128)S(1)}, u32[]{:S(2)}, u32[]{:S(2)}) collective-permute-start(f32[2,8,128]{2,1,0:T(8,128)S(1)} %get-tuple-element.27), channel_id=1, source_target_pairs={{0,8},{8,0},{16,24},{24,16},{1,9},{9,1},{17,25},{25,17},{2,10},{10... | collective-permute-start | bytes 24584 | tf_op jit(solution)/shard_map/ppermute | solution.py:39
  14.9 5.4 %collective-permute-start.4 = (f32[2,8,128]{2,1,0:T(8,128)S(1)}, f32[2,8,128]{2,1,0:T(8,128)S(1)}, u32[]{:S(2)}, u32[]{:S(2)}) collective-permute-start(f32[2,8,128]{2,1,0:T(8,128)S(1)} %get-tuple-element.26), channel_id=1, source_target_pairs={{8,16},{16,8},{24,0},{0,24},{9,17},{17,9},{25,1},{1,25},{10,18},{1... | collective-permute-start | bytes 24584 | tf_op jit(solution)/shard_map/ppermute | solution.py:40
  19.6 2.8 %copy-start = (s32[48,1]{0,1:T(1,128)S(1)}, s32[48,1]{0,1:T(1,128)}, u32[]{:S(2)}) copy-start(s32[48,1]{0,1:T(1,128)} %param.8) | copy-start | bytes 580
  19.7 2.8 %copy-start.1 = (s32[48]{0:T(128)S(1)}, s32[48]{0:T(128)}, u32[]{:S(2)}) copy-start(s32[48]{0:T(128)} %param.9) | copy-start | bytes 580
  22.5 5.0 %collective-permute-start.5 = (f32[16,128]{1,0:T(8,128)S(1)}, f32[16,128]{1,0:T(8,128)S(1)}, u32[]{:S(2)}, u32[]{:S(2)}) collective-permute-start(f32[16,128]{1,0:T(8,128)S(1)} %broadcast_select_fusion.1), channel_id=1, source_target_pairs={{0,2},{2,0},{4,6},{6,4},{1,3},{3,1},{5,7},{7,5},{8,10},{10,8},{12,... | collective-permute-start | bytes 24584 | tf_op jit(solution)/shard_map/ppermute | solution.py:396
  22.6 26.9 %all-to-all-start = ((bf16[16,192,128]{2,1,0:T(8,128)(2,1)}), bf16[16,192,128]{2,1,0:T(8,128)(2,1)S(1)}, u32[]{:S(2)}, u32[]{:S(2)}) async-start(bf16[16,192,128]{2,1,0:T(8,128)(2,1)} %integrate_far.1), calls=%async_computation | async-start | bytes 1572864 | tf_op jit(solution)/shard_map/all_to_all | solution.py:432
  27.6 6.9 %collective-permute-start.6 = (f32[16,128]{1,0:T(8,128)S(1)}, f32[16,128]{1,0:T(8,128)S(1)}, u32[]{:S(2)}, u32[]{:S(2)}) collective-permute-start(f32[16,128]{1,0:T(8,128)S(1)} %fusion.4), channel_id=1, source_target_pairs={{0,4},{2,6},{4,0},{6,2},{1,5},{3,7},{5,1},{7,3},{8,12},{10,14},{12... | collective-permute-start | bytes 24584 | tf_op jit(solution)/shard_map/ppermute | solution.py:396
  34.5 6.9 %collective-permute-start.7 = (f32[16,128]{1,0:T(8,128)S(1)}, f32[16,128]{1,0:T(8,128)S(1)}, u32[]{:S(2)}, u32[]{:S(2)}) collective-permute-start(f32[16,128]{1,0:T(8,128)S(1)} %fusion.7), channel_id=1, source_target_pairs={{0,8},{8,0},{16,24},{24,16},{1,9},{9,1},{17,25},{25,17},{2,10},{10... | collective-permute-start | bytes 24584 | tf_op jit(solution)/shard_map/ppermute | solution.py:396
  41.4 7.3 %collective-permute-start.8 = (f32[16,128]{1,0:T(8,128)S(1)}, f32[16,128]{1,0:T(8,128)S(1)}, u32[]{:S(2)}, u32[]{:S(2)}) collective-permute-start(f32[16,128]{1,0:T(8,128)S(1)} %add.79), channel_id=1, source_target_pairs={{0,16},{8,24},{16,0},{24,8},{1,17},{9,25},{17,1},{25,9},{2,18},{10... | collective-permute-start | bytes 24584 | tf_op jit(solution)/shard_map/ppermute | solution.py:396

commit v7 on v6

--- a/solution.py
+++ b/solution.py
@@ -1,5 +1,4 @@
 import functools
-import math
 
 import jax
 import jax.numpy as jnp
@@ -7,7 +6,6 @@
 from jax.experimental import pallas as pl
 from jax.experimental.pallas import tpu as pltpu
 from jax.sharding import PartitionSpec as P
-
 
 BASIS = 64
 CELLS = 8
@@ -163,9 +161,11 @@
     )(*in_hbm(pair_groups, density_blocks, basis))
 
 
-def tabulate(groups, codes, owner, counts, place):
+def tabulate(groups, codes, owner, slot, counts, place, slot_rows):
     pairs, owners = codes.shape[1], counts.shape[0]
     lines = BASIS // 2
+    slot_rows[...] = jnp.full(slot_rows.shape, pairs, jnp.float32)
+    lane = lax.broadcasted_iota(jnp.int32, (1, LANES), 1)
     for o in range(owners):
         counts[o] = 0
     for code in range(groups * groups):
@@ -177,6 +177,8 @@
         code = codes[0, p] * groups + codes[1, p]
         place[0, code] = o
         place[1, code] = rank * lines
+        row = slot_rows[pl.ds(o, 1), :]
+        slot_rows[pl.ds(o, 1), :] = jnp.where(lane == rank, slot[0, p].astype(jnp.float32), row)
     free_owner, free_rank = jnp.int32(0), counts[0]
     for o in range(1, owners):
         fewer = counts[o] < free_rank
@@ -206,35 +208,47 @@
 
 
 def near_kernel(
-    groups, pair_groups, owner, potential, near, basis, total, far, places,
-    codes, owners_of, counts, place, arrived, staged,
+    groups, pair_groups, owner, owner_slot, potential, near, basis, total, far, places, slots,
+    codes, owners_of, slots_of, counts, place, slot_rows, arrived, staged,
 ):
     rows = near.shape[0]
     begin = pl.multiple_of(halves()[1], LANES)
     far_copy = pltpu.make_async_copy(basis.at[:, pl.ds(begin, far.shape[1])], far, arrived)
-    codes_copy = pltpu.make_async_copy(pair_groups, codes, staged.at[0])
-    owner_copy = pltpu.make_async_copy(owner, owners_of, staged.at[1])
-    for copy in (codes_copy, owner_copy, far_copy):
+    tables = [
+        pltpu.make_async_copy(source, target, staged.at[i])
+        for i, (source, target) in enumerate(
+            [(pair_groups, codes), (owner, owners_of), (owner_slot, slots_of)]
+        )
+    ]
+    for copy in tables + [far_copy]:
         copy.start()
     for c, part in enumerate(overlaps(near, potential)):
         if c == 0:
             total[:, :rows] = part
-            codes_copy.wait()
-            owner_copy.wait()
-            tabulate(groups, codes, owners_of, counts, place)
+            for copy in tables:
+                copy.wait()
+            tabulate(groups, codes, owners_of, slots_of, counts, place, slot_rows)
         else:
             total[:, :rows] += part
-    places_copy = pltpu.make_async_copy(place, places, staged.at[2])
+    places_copy = pltpu.make_async_copy(place, places, staged.at[3])
     places_copy.start()
+    for o in range(slots.shape[0]):
+        slots[o] = jnp.broadcast_to(slot_rows[o : o + 1, :], slots.shape[1:]).astype(slots.dtype)
     places_copy.wait()
     far_copy.wait()
 
 
-def far_kernel(groups, places, potential, far, near_total, send, total, blocks, place, staged, sent):
+def far_kernel(
+    groups, places, slots, potential, far, near_total, send, total, blocks, place, staged, sent
+):
     rows = groups * BASIS
     lines = BASIS // 2
-    places_copy = pltpu.make_async_copy(places, place, staged)
+    places_copy = pltpu.make_async_copy(places, place, staged.at[0])
+    slots_copy = pltpu.make_async_copy(
+        slots, send.at[:, pl.ds(send.shape[1] - slots.shape[1], slots.shape[1]), :], staged.at[1]
+    )
     places_copy.start()
+    slots_copy.start()
     for c, part in enumerate(overlaps(far, potential)):
         if c == 0:
             total[:, :rows] = near_total[:, :rows] + part
@@ -257,6 +271,7 @@
             pltpu.make_async_copy(
                 blocks.at[code], send.at[place[0, code], pl.ds(line, lines), :], sent
             ).start()
+    slots_copy.wait()
     pltpu.make_async_copy(blocks, blocks, sent).wait()
 
 
@@ -268,7 +283,7 @@
     return -(-rows // LANES) * LANES
 
 
-def integrated_near(near, basis, potential, pair_groups, owner, owners):
+def integrated_near(near, basis, potential, pair_groups, owner, owner_slot, owners):
     rows, pairs = basis.shape[0], pair_groups.shape[1]
     groups = rows // BASIS
     vmem, hbm = pl.BlockSpec(memory_space=pltpu.VMEM), pl.BlockSpec(memory_space=pltpu.HBM)
@@ -279,65 +294,69 @@
             jax.ShapeDtypeStruct((rows, padded(rows)), jnp.float32),
             jax.ShapeDtypeStruct((rows, EXT3 // 2), basis.dtype),
             jax.ShapeDtypeStruct((2, groups * groups), jnp.int32),
-        ),
-        in_specs=[hbm, hbm, vmem, vmem, hbm],
-        out_specs=[vmem, vmem, hbm],
+            jax.ShapeDtypeStruct((owners, 8, LANES), jnp.bfloat16),
+        ),
+        in_specs=[hbm, hbm, hbm, vmem, vmem, hbm],
+        out_specs=[vmem, vmem, hbm, vmem],
         scratch_shapes=[
             pltpu.SMEM((2, pairs), jnp.int32),
             pltpu.SMEM((1, pairs), jnp.int32),
+            pltpu.SMEM((1, pairs), jnp.int32),
             pltpu.SMEM((owners,), jnp.int32),
             pltpu.SMEM((2, groups * groups), jnp.int32),
+            pltpu.VMEM((owners, LANES), jnp.float32),
             pltpu.SemaphoreType.DMA(()),
-            pltpu.SemaphoreType.DMA((3,)),
+            pltpu.SemaphoreType.DMA((4,)),
         ],
         compiler_params=pltpu.CompilerParams(vmem_limit_bytes=24 << 20),
         cost_estimate=pl.CostEstimate(
             flops=rows * rows * EXT3, bytes_accessed=2 * rows * EXT3, transcendentals=0
         ),
-    )(*in_hbm(pair_groups, owner.reshape(1, pairs)), potential, near, *in_hbm(basis))
-
-
-def integrated_far(far, near_total, potential, places, owners, capacity):
+    )(
+        *in_hbm(pair_groups, owner.reshape(1, pairs), owner_slot.reshape(1, pairs)),
+        potential,
+        near,
+        *in_hbm(basis),
+    )
+
+
+def integrated_far(far, near_total, potential, places, slots, capacity):
     rows = far.shape[0]
     groups = rows // BASIS
     vmem, hbm = pl.BlockSpec(memory_space=pltpu.VMEM), pl.BlockSpec(memory_space=pltpu.HBM)
     return pl.pallas_call(
         functools.partial(far_kernel, groups),
         name="integrate_far",
-        out_shape=jax.ShapeDtypeStruct((owners, capacity * BASIS // 2, LANES), jnp.bfloat16),
-        in_specs=[hbm, vmem, vmem, vmem],
+        out_shape=jax.ShapeDtypeStruct(
+            (slots.shape[0], capacity * BASIS // 2 + slots.shape[1], LANES), jnp.bfloat16
+        ),
+        in_specs=[hbm, vmem, vmem, vmem, vmem],
         out_specs=hbm,
         scratch_shapes=[
             pltpu.VMEM((rows, padded(rows)), jnp.float32),
             pltpu.VMEM((groups * groups, BASIS // 2, LANES), jnp.bfloat16),
             pltpu.SMEM(places.shape, jnp.int32),
-            pltpu.SemaphoreType.DMA(()),
+            pltpu.SemaphoreType.DMA((2,)),
             pltpu.SemaphoreType.DMA(()),
         ],
         compiler_params=pltpu.CompilerParams(vmem_limit_bytes=24 << 20),
         cost_estimate=pl.CostEstimate(
             flops=rows * rows * EXT3, bytes_accessed=2 * rows * EXT3, transcendentals=0
         ),
-    )(places, potential, far, near_total)
-
-
-def store_kernel(capacity, got, slot_of, store, total, packed, slots, moved, written):
+    )(places, slots, potential, far, near_total)
+
+
+def store_kernel(capacity, got, store, total, packed, written):
     lines = BASIS // 2
     pitch = lines + 1
-    sources = got.shape[0]
     stored = store.shape[0]
-    copy = pltpu.make_async_copy(slot_of, slots, moved)
-    copy.start()
     total[...] = jnp.zeros_like(total)
-    copy.wait()
-
-    def add(s, carry):
+    for s in range(got.shape[0]):
+        slots = got[s, capacity * lines : capacity * lines + 8, :].astype(jnp.float32)
+        slots = slots[:1].astype(jnp.int32)
         for r in range(capacity):
-            at = pl.ds(slots[s, r] * pitch, lines)
+            at = pl.ds(slots[0, r] * pitch, lines)
             total[at, :] += got[s, r * lines : (r + 1) * lines, :].astype(jnp.float32)
-        return carry
-
-    lax.fori_loop(0, sources, add, 0)
     in_low = lax.broadcasted_iota(jnp.int32, (stored, LANES), 1) < BASIS
     pieces = 4
     span = lines // 2 // pieces
@@ -363,53 +382,24 @@
         copy.wait()
 
 
-def stored_blocks(got, slot_of, rows, capacity):
+def stored_blocks(got, rows, capacity):
     vmem, hbm = pl.BlockSpec(memory_space=pltpu.VMEM), pl.BlockSpec(memory_space=pltpu.HBM)
     return pl.pallas_call(
         functools.partial(store_kernel, capacity),
         name="store",
         out_shape=jax.ShapeDtypeStruct((rows, BASIS * BASIS), jnp.bfloat16),
-        in_specs=[vmem, vmem],
+        in_specs=[vmem],
         out_specs=hbm,
         scratch_shapes=[
             pltpu.VMEM(((rows + 1) * (BASIS // 2 + 1) + 7, LANES), jnp.float32),
             pltpu.VMEM((rows, BASIS * BASIS), jnp.bfloat16),
-            pltpu.SMEM(slot_of.shape, jnp.int32),
-            pltpu.SemaphoreType.DMA(()),
             pltpu.SemaphoreType.DMA((8,)),
         ],
         compiler_params=pltpu.CompilerParams(vmem_limit_bytes=24 << 20),
         cost_estimate=pl.CostEstimate(
             flops=got.size, bytes_accessed=2 * got.size, transcendentals=0
         ),
-    )(got, slot_of)
-
-
-def gathered(row, axes):
-    sizes = [lax.axis_size(axis) for axis in axes]
-    count = math.prod(sizes)
-    member = lax.broadcasted_iota(jnp.int32, (count, row.shape[-1]), 0)
-    table = jnp.where(member == lax.axis_index(axes), row[None, :], 0.0)
-    for axis, size in zip(axes[::-1], sizes[::-1]):
-        step = 1
-        while step < size:
-            other = lax.ppermute(table, axis, [(i, i ^ step) for i in range(size)])
-            table = table + other
-            step *= 2
-    return table
-
-
-def slots_of_sources(owner, owner_slot, axes):
-    pairs = owner_slot.shape[0]
-    named = jnp.pad((owner[:, 0] * pairs + owner_slot + 1).astype(jnp.float32), (0, LANES - pairs))
-    named = gathered(named, axes)[:, :pairs].astype(jnp.int32) - 1
-    slot = named - lax.axis_index(axes) * pairs
-    mine = (slot >= 0) & (slot < pairs)
-    order = jnp.arange(pairs, dtype=jnp.int32)
-    before = mine[:, None, :] & (order[None, None, :] < order[None, :, None])
-    rank = jnp.where(mine, jnp.sum(before.astype(jnp.int32), axis=2), -1)
-    at_rank = rank[:, None, :] == jnp.arange(LANES, dtype=jnp.int32)[None, :, None]
-    return jnp.sum(jnp.where(at_rank, slot[:, None, :] - pairs, 0), axis=2) + pairs
+    )(got)
 
 
 def per_device(basis, density_blocks, pair_groups, owner, owner_slot):
@@ -424,19 +414,17 @@
     odd, near, far = merged_halves(box[:, : EXT // 2], box[:, EXT // 2 :], "gx")
     near, far = slater_potential(near), slater_potential(far)
 
-    total, far_table, places = integrated_near(
-        near_table, basis, near, pair_groups, owner, owners
+    total, far_table, places, slots = integrated_near(
+        near_table, basis, near, pair_groups, owner, owner_slot, owners
     )
-    send = integrated_far(far_table, total, far, places, owners, capacity)
-    send, late_owner, late_slot = lax.optimization_barrier((send, owner, owner_slot))
+    send = integrated_far(far_table, total, far, places, slots, capacity)
     got = lax.all_to_all(send, ("gx", "gy"), split_axis=0, concat_axis=0, tiled=True)
-    slot_of = slots_of_sources(late_owner, late_slot, ("gx", "gy"))
 
     potential = jnp.concatenate(
         [jnp.where(odd, near, far)[:, RIM:], jnp.where(odd, far, near)[:, :RIM]], axis=1
     ).reshape(2, CELLS, EXT // 2, EXT)[..., RIM : RIM + CELLS]
     potential = jnp.concatenate([potential[0, :, RIM:], potential[1, :, :RIM]], axis=1)
-    return stored_blocks(got, slot_of, pairs, capacity), potential
+    return stored_blocks(got, pairs, capacity), potential
 
 
 def solution(mesh):

time: 51.7 us -> 48.5 us (0.938)
  the two profiles are of different devices: /device:TPU:0 before, /device:TPU:9 now
where the time goes in v7:
time: 48.5 us; the launch traced here: 48.3 us
  waiting for transfers between devices  22.5 us (46%)
  starting transfers between devices  14.2 us (29%)
  Pallas kernels  9.99 us (21%)
  other arithmetic  0.73 us (2%)
  between operations  0.71 us (1%)
    all_to_all x1, waiting for transfers between devices, per_device(): lax.all_to_all(send, ('gx', 'gy'), split_axis=0, concat_axis=0, tiled=True)  19.5 us
    all_to_all x1, starting transfers between devices, per_device(): lax.all_to_all(send, ('gx', 'gy'), split_axis=0, concat_axis=0, tiled=True)  7.29 us
    ppermute x2, starting transfers between devices, merged_halves(): far = far + lax.ppermute(far, axis, neighbour_swaps(count, 1))  5.56 us
    pallas_call x1, Pallas kernels, collocated(): pl.pallas_call(functools.partial(collocate_kernel, groups), name='colloca...  4.09 us
    pallas_call x1, Pallas kernels, integrated_near(): pl.pallas_call(functools.partial(near_kernel, groups), name='integrate_ne...  2.29 us
    pallas_call x1, Pallas kernels, integrated_far(): pl.pallas_call(functools.partial(far_kernel, groups), name='integrate_far...  2.07 us
    ppermute x2, waiting for transfers between devices, merged_halves(): far = far + lax.ppermute(far, axis, neighbour_swaps(count, 1))  1.63 us
    pallas_call x1, Pallas kernels, stored_blocks(): pl.pallas_call(functools.partial(store_kernel, capacity), name='store', o...  1.53 us
  transfers between devices with their start and end apart: 6, of which 3 were waited for; matrix products, arithmetic and copies ran while one was open for 2% of the time, Pallas kernels for 5%

profile of v7, /device:TPU:9, one launch (start us, length us, event | category | flops | bytes accessed | tf_op | source)
XLA Modules:
  0.0 48.3 jit_solution(2387936787744376163)
XLA Ops:
  0.6 4.1 %collocate.1 = (f32[2,16,128]{2,1,0:T(8,128)S(1)}, f32[2,16,128]{2,1,0:T(8,128)S(1)}, bf16[448,2048]{1,0:T(8,128)(2,1)S(1)}) custom-call(s32[2,48]{1,0:T(2,128)} %pair_groups.3, bf16[48,4096]{1,0:T(8,128)(2,1)} %blocks.1, bf16[448,4096]{1,0:T(8,128)(2,1)} %bitcast.15), custom_call_target="tpu_custom_call" | custom-call | flops 1644167168 | bytes 3670016 | tf_op jit(solution)/shard_map/collocate/pallas_call | solution.py:137
  4.7 1.3 %collective-permute-start = (f32[2,16,128]{2,1,0:T(8,128)S(1)}, f32[2,16,128]{2,1,0:T(8,128)S(1)}, u32[]{:S(2)}, u32[]{:S(2)}) collective-permute-start(f32[2,16,128]{2,1,0:T(8,128)S(1)} %get-tuple-element.10), channel_id=1, source_target_pairs={{0,1},{1,0},{2,3},{3,2},{4,5},{5,4},{6,7},{7,6},{8,9},{9,8},{10,11... | collective-permute-start | bytes 49160 | tf_op jit(solution)/shard_map/ppermute | solution.py:50
  6.0 1.4 %collective-permute-done = f32[2,16,128]{2,1,0:T(8,128)S(1)} collective-permute-done((f32[2,16,128]{2,1,0:T(8,128)S(1)}, f32[2,16,128]{2,1,0:T(8,128)S(1)}, u32[]{:S(2)}, u32[]{:S(2)}) %collective-permute-start) | collective-permute-done | bytes 16416 | tf_op jit(solution)/shard_map/ppermute | solution.py:50
  7.4 3.0 %collective-permute-start.2 = (f32[16,128]{1,0:T(8,128)S(1)}, f32[16,128]{1,0:T(8,128)S(1)}, u32[]{:S(2)}, u32[]{:S(2)}) collective-permute-start(f32[16,128]{1,0:T(8,128)S(1)} %get-tuple-element.25), channel_id=1, source_target_pairs={{2,4},{4,2},{6,0},{0,6},{3,5},{5,3},{7,1},{1,7},{10,12},{12,10},{1... | collective-permute-start | bytes 24584 | tf_op jit(solution)/shard_map/ppermute | solution.py:38
  10.4 0.0 collective-permute-start.1
  10.4 1.6 %collective-permute-done.2 = f32[16,128]{1,0:T(8,128)S(1)} collective-permute-done((f32[16,128]{1,0:T(8,128)S(1)}, f32[16,128]{1,0:T(8,128)S(1)}, u32[]{:S(2)}, u32[]{:S(2)}) %collective-permute-start.2) | collective-permute-done | bytes 8224 | tf_op jit(solution)/shard_map/ppermute | solution.py:38
  12.0 0.0 collective-permute-done.1
  12.0 0.1 collective-permute-start.3
  12.1 2.6 %collective-permute-start.4 = (f32[2,8,128]{2,1,0:T(8,128)S(1)}, f32[2,8,128]{2,1,0:T(8,128)S(1)}, u32[]{:S(2)}, u32[]{:S(2)}) collective-permute-start(f32[2,8,128]{2,1,0:T(8,128)S(1)} %get-tuple-element.22), channel_id=1, source_target_pairs={{8,16},{16,8},{24,0},{0,24},{9,17},{17,9},{25,1},{1,25},{10,18},{1... | collective-permute-start | bytes 24584 | tf_op jit(solution)/shard_map/ppermute | solution.py:38
  14.7 0.0 collective-permute-done.3
  14.7 2.3 %integrate_near.1 = (f32[448,512]{1,0:T(8,128)S(1)}, bf16[448,2048]{1,0:T(8,128)(2,1)S(1)}, s32[2,49]{1,0:T(2,128)S(1)}, bf16[16,8,128]{2,1,0:T(8,128)(2,1)S(1)}) custom-call(s32[2,48]{1,0:T(2,128)} %pair_groups.3, s32[1,48]{1,0:T(1,128)} %bitcast.17, s32[1,48]{1,0:T(1,128)} %bitcast.18, f32[2,8,128]{2,1,0:T(8,128)S(1)} %cbrt_divide_fusion.1.potential, ...), custom_call_target="tpu_custom_call" | custom-call | flops 822083584 | bytes 3670016 | tf_op jit(solution)/shard_map/integrate_near/pallas_call | solution.py:290
  17.0 0.0 collective-permute-done.4
  17.1 2.1 %integrate_far.1 = bf16[16,200,128]{2,1,0:T(8,128)(2,1)} custom-call(s32[2,49]{1,0:T(2,128)S(1)} %get-tuple-element.12.places, bf16[16,8,128]{2,1,0:T(8,128)(2,1)S(1)} %get-tuple-element.13.slots, f32[2,8,128]{2,1,0:T(8,128)S(1)} %cbrt_divide_fusion.potential, bf16[448,2048]{1,0:T(8,128)(2,1)S(1)} %get-tuple-element.14.far, ...), custom_call_target="tpu_custom_call" | custom-call | flops 822083584 | bytes 3670016 | tf_op jit(solution)/shard_map/integrate_far/pallas_call | solution.py:327
  19.1 7.3 %all-to-all-start = ((bf16[16,200,128]{2,1,0:T(8,128)(2,1)}), bf16[16,200,128]{2,1,0:T(8,128)(2,1)S(1)}, u32[]{:S(2)}, u32[]{:S(2)}) async-start(bf16[16,200,128]{2,1,0:T(8,128)(2,1)} %integrate_far.1), calls=%async_computation | async-start | bytes 1638400 | tf_op jit(solution)/shard_map/all_to_all | solution.py:421
  26.5 0.1 reshape.23
  26.5 0.1 slice_bitcast_fusion.1
  26.6 0.6 %pad_maximum_fusion = f32[8,8,8]{2,1,0:T(8,128)} fusion(f32[8,4,8]{2,1,0:T(4,128)S(1)} %get-tuple-element.17, f32[8,4,8]{2,1,0:T(4,128)S(1)} %get-tuple-element.16), kind=kLoop, calls=%fused_computation | loop fusion | flops 512 | bytes 4096 | tf_op jit(solution)/shard_map/concatenate | solution.py:426
  27.3 19.5 %all-to-all-done.got = bf16[16,200,128]{2,1,0:T(8,128)(2,1)S(1)} async-done(((bf16[16,200,128]{2,1,0:T(8,128)(2,1)}), bf16[16,200,128]{2,1,0:T(8,128)(2,1)S(1)}, u32[]{:S(2)}, u32[]{:S(2)}) %all-to-all-start) | async-done | bytes 819232 | tf_op jit(solution)/shard_map/all_to_all | solution.py:421
  46.7 1.5 %store.1 = bf16[48,4096]{1,0:T(8,128)(2,1)} custom-call(bf16[16,200,128]{2,1,0:T(8,128)(2,1)S(1)} %all-to-all-done.got), custom_call_target="tpu_custom_call" | custom-call | flops 409600 | bytes 819200 | tf_op jit(solution)/shard_map/store/pallas_call | solution.py:387
  (8 shorter events, 0.1 us)
Async XLA Ops:
  4.7 2.7 %collective-permute-start = (f32[2,16,128]{2,1,0:T(8,128)S(1)}, f32[2,16,128]{2,1,0:T(8,128)S(1)}, u32[]{:S(2)}, u32[]{:S(2)}) collective-permute-start(f32[2,16,128]{2,1,0:T(8,128)S(1)} %get-tuple-element.10), channel_id=1, source_target_pairs={{0,1},{1,0},{2,3},{3,2},{4,5},{5,4},{6,7},{7,6},{8,9},{9,8},{10,11... | collective-permute-start | bytes 49160 | tf_op jit(solution)/shard_map/ppermute | solution.py:50
  7.4 4.6 %collective-permute-start.2 = (f32[16,128]{1,0:T(8,128)S(1)}, f32[16,128]{1,0:T(8,128)S(1)}, u32[]{:S(2)}, u32[]{:S(2)}) collective-permute-start(f32[16,128]{1,0:T(8,128)S(1)} %get-tuple-element.25), channel_id=1, source_target_pairs={{2,4},{4,2},{6,0},{0,6},{3,5},{5,3},{7,1},{1,7},{10,12},{12,10},{1... | collective-permute-start | bytes 24584 | tf_op jit(solution)/shard_map/ppermute | solution.py:38
  10.4 1.6 %collective-permute-start.1 = (f32[16,128]{1,0:T(8,128)S(1)}, f32[16,128]{1,0:T(8,128)S(1)}, u32[]{:S(2)}, u32[]{:S(2)}) collective-permute-start(f32[16,128]{1,0:T(8,128)S(1)} %get-tuple-element.24), channel_id=1, source_target_pairs={{0,2},{2,0},{4,6},{6,4},{1,3},{3,1},{5,7},{7,5},{8,10},{10,8},{12,... | collective-permute-start | bytes 24584 | tf_op jit(solution)/shard_map/ppermute | solution.py:37
  12.0 2.7 %collective-permute-start.3 = (f32[2,8,128]{2,1,0:T(8,128)S(1)}, f32[2,8,128]{2,1,0:T(8,128)S(1)}, u32[]{:S(2)}, u32[]{:S(2)}) collective-permute-start(f32[2,8,128]{2,1,0:T(8,128)S(1)} %get-tuple-element.23), channel_id=1, source_target_pairs={{0,8},{8,0},{16,24},{24,16},{1,9},{9,1},{17,25},{25,17},{2,10},{10... | collective-permute-start | bytes 24584 | tf_op jit(solution)/shard_map/ppermute | solution.py:37
  12.1 4.9 %collective-permute-start.4 = (f32[2,8,128]{2,1,0:T(8,128)S(1)}, f32[2,8,128]{2,1,0:T(8,128)S(1)}, u32[]{:S(2)}, u32[]{:S(2)}) collective-permute-start(f32[2,8,128]{2,1,0:T(8,128)S(1)} %get-tuple-element.22), channel_id=1, source_target_pairs={{8,16},{16,8},{24,0},{0,24},{9,17},{17,9},{25,1},{1,25},{10,18},{1... | collective-permute-start | bytes 24584 | tf_op jit(solution)/shard_map/ppermute | solution.py:38
  19.1 27.6 %all-to-all-start = ((bf16[16,200,128]{2,1,0:T(8,128)(2,1)}), bf16[16,200,128]{2,1,0:T(8,128)(2,1)S(1)}, u32[]{:S(2)}, u32[]{:S(2)}) async-start(bf16[16,200,128]{2,1,0:T(8,128)(2,1)} %integrate_far.1), calls=%async_computation | async-start | bytes 1638400 | tf_op jit(solution)/shard_map/all_to_all | solution.py:421

commit v8 on v7

--- a/solution.py
+++ b/solution.py
@@ -346,25 +346,30 @@
     )(places, slots, potential, far, near_total)
 
 
-def store_kernel(capacity, got, store, total, packed, written):
+def store_kernel(capacity, got, store, total, other, packed, written):
     lines = BASIS // 2
     pitch = lines + 1
     stored = store.shape[0]
     total[...] = jnp.zeros_like(total)
+    other[...] = jnp.zeros_like(other)
     for s in range(got.shape[0]):
         slots = got[s, capacity * lines : capacity * lines + 8, :].astype(jnp.float32)
         slots = slots[:1].astype(jnp.int32)
         for r in range(capacity):
             at = pl.ds(slots[0, r] * pitch, lines)
-            total[at, :] += got[s, r * lines : (r + 1) * lines, :].astype(jnp.float32)
+            sums = (total, other)[r % 2]
+            sums[at, :] += got[s, r * lines : (r + 1) * lines, :].astype(jnp.float32)
     in_low = lax.broadcasted_iota(jnp.int32, (stored, LANES), 1) < BASIS
     pieces = 4
     span = lines // 2 // pieces
     copies = []
     for piece in range(pieces):
         for i in range(piece * span, (piece + 1) * span):
-            even = total[pl.ds(2 * i, stored, stride=pitch), :]
-            odd = total[pl.ds(2 * i + 1, stored, stride=pitch), :]
+            even, odd = [
+                total[pl.ds(line, stored, stride=pitch), :]
+                + other[pl.ds(line, stored, stride=pitch), :]
+                for line in (2 * i, 2 * i + 1)
+            ]
             for j, row in (
                 (i, jnp.where(in_low, even, pltpu.roll(odd, BASIS, axis=1))),
                 (i + lines // 2, jnp.where(in_low, pltpu.roll(even, BASIS, axis=1), odd)),
@@ -392,6 +397,7 @@
         out_specs=hbm,
         scratch_shapes=[
             pltpu.VMEM(((rows + 1) * (BASIS // 2 + 1) + 7, LANES), jnp.float32),
+            pltpu.VMEM(((rows + 1) * (BASIS // 2 + 1) + 7, LANES), jnp.float32),
             pltpu.VMEM((rows, BASIS * BASIS), jnp.bfloat16),
             pltpu.SemaphoreType.DMA((8,)),
         ],

time: 48.5 us -> 48.3 us (level)
  no operation moved by 1% of the time
where the time goes in v8:
time: 48.3 us; the launch traced here: 48.1 us
  waiting for transfers between devices  22.5 us (47%)
  starting transfers between devices  14.2 us (29%)
  Pallas kernels  9.82 us (20%)
  other arithmetic  0.73 us (2%)
  between operations  0.71 us (1%)
    all_to_all x1, waiting for transfers between devices, per_device(): lax.all_to_all(send, ('gx', 'gy'), split_axis=0, concat_axis=0, tiled=True)  19.5 us
    all_to_all x1, starting transfers between devices, per_device(): lax.all_to_all(send, ('gx', 'gy'), split_axis=0, concat_axis=0, tiled=True)  7.28 us
    ppermute x2, starting transfers between devices, merged_halves(): far = far + lax.ppermute(far, axis, neighbour_swaps(count, 1))  5.56 us
    pallas_call x1, Pallas kernels, collocated(): pl.pallas_call(functools.partial(collocate_kernel, groups), name='colloca...  4.09 us
    pallas_call x1, Pallas kernels, integrated_near(): pl.pallas_call(functools.partial(near_kernel, groups), name='integrate_ne...  2.28 us
    pallas_call x1, Pallas kernels, integrated_far(): pl.pallas_call(functools.partial(far_kernel, groups), name='integrate_far...  2.08 us
    ppermute x2, waiting for transfers between devices, merged_halves(): far = far + lax.ppermute(far, axis, neighbour_swaps(count, 1))  1.63 us
    pallas_call x1, Pallas kernels, stored_blocks(): pl.pallas_call(functools.partial(store_kernel, capacity), name='store', o...  1.36 us
  transfers between devices with their start and end apart: 6, of which 3 were waited for; matrix products, arithmetic and copies ran while one was open for 2% of the time, Pallas kernels for 5%

profile of v8, /device:TPU:9, one launch (start us, length us, event | category | flops | bytes accessed | tf_op | source)
XLA Modules:
  0.0 48.1 jit_solution(3713636274694768834)
XLA Ops:
  0.6 4.1 %collocate.1 = (f32[2,16,128]{2,1,0:T(8,128)S(1)}, f32[2,16,128]{2,1,0:T(8,128)S(1)}, bf16[448,2048]{1,0:T(8,128)(2,1)S(1)}) custom-call(s32[2,48]{1,0:T(2,128)} %pair_groups.3, bf16[48,4096]{1,0:T(8,128)(2,1)} %blocks.1, bf16[448,4096]{1,0:T(8,128)(2,1)} %bitcast.15), custom_call_target="tpu_custom_call" | custom-call | flops 1644167168 | bytes 3670016 | tf_op jit(solution)/shard_map/collocate/pallas_call | solution.py:137
  4.7 1.3 %collective-permute-start = (f32[2,16,128]{2,1,0:T(8,128)S(1)}, f32[2,16,128]{2,1,0:T(8,128)S(1)}, u32[]{:S(2)}, u32[]{:S(2)}) collective-permute-start(f32[2,16,128]{2,1,0:T(8,128)S(1)} %get-tuple-element.10), channel_id=1, source_target_pairs={{0,1},{1,0},{2,3},{3,2},{4,5},{5,4},{6,7},{7,6},{8,9},{9,8},{10,11... | collective-permute-start | bytes 49160 | tf_op jit(solution)/shard_map/ppermute | solution.py:50
  6.0 1.4 %collective-permute-done = f32[2,16,128]{2,1,0:T(8,128)S(1)} collective-permute-done((f32[2,16,128]{2,1,0:T(8,128)S(1)}, f32[2,16,128]{2,1,0:T(8,128)S(1)}, u32[]{:S(2)}, u32[]{:S(2)}) %collective-permute-start) | collective-permute-done | bytes 16416 | tf_op jit(solution)/shard_map/ppermute | solution.py:50
  7.4 3.0 %collective-permute-start.2 = (f32[16,128]{1,0:T(8,128)S(1)}, f32[16,128]{1,0:T(8,128)S(1)}, u32[]{:S(2)}, u32[]{:S(2)}) collective-permute-start(f32[16,128]{1,0:T(8,128)S(1)} %get-tuple-element.25), channel_id=1, source_target_pairs={{2,4},{4,2},{6,0},{0,6},{3,5},{5,3},{7,1},{1,7},{10,12},{12,10},{1... | collective-permute-start | bytes 24584 | tf_op jit(solution)/shard_map/ppermute | solution.py:38
  10.4 0.0 collective-permute-start.1
  10.4 1.6 %collective-permute-done.2 = f32[16,128]{1,0:T(8,128)S(1)} collective-permute-done((f32[16,128]{1,0:T(8,128)S(1)}, f32[16,128]{1,0:T(8,128)S(1)}, u32[]{:S(2)}, u32[]{:S(2)}) %collective-permute-start.2) | collective-permute-done | bytes 8224 | tf_op jit(solution)/shard_map/ppermute | solution.py:38
  12.0 0.0 collective-permute-done.1
  12.0 0.1 collective-permute-start.3
  12.1 2.6 %collective-permute-start.4 = (f32[2,8,128]{2,1,0:T(8,128)S(1)}, f32[2,8,128]{2,1,0:T(8,128)S(1)}, u32[]{:S(2)}, u32[]{:S(2)}) collective-permute-start(f32[2,8,128]{2,1,0:T(8,128)S(1)} %get-tuple-element.22), channel_id=1, source_target_pairs={{8,16},{16,8},{24,0},{0,24},{9,17},{17,9},{25,1},{1,25},{10,18},{1... | collective-permute-start | bytes 24584 | tf_op jit(solution)/shard_map/ppermute | solution.py:38
  14.7 0.0 collective-permute-done.3
  14.7 2.3 %integrate_near.1 = (f32[448,512]{1,0:T(8,128)S(1)}, bf16[448,2048]{1,0:T(8,128)(2,1)S(1)}, s32[2,49]{1,0:T(2,128)S(1)}, bf16[16,8,128]{2,1,0:T(8,128)(2,1)S(1)}) custom-call(s32[2,48]{1,0:T(2,128)} %pair_groups.3, s32[1,48]{1,0:T(1,128)} %bitcast.17, s32[1,48]{1,0:T(1,128)} %bitcast.18, f32[2,8,128]{2,1,0:T(8,128)S(1)} %cbrt_divide_fusion.1.potential, ...), custom_call_target="tpu_custom_call" | custom-call | flops 822083584 | bytes 3670016 | tf_op jit(solution)/shard_map/integrate_near/pallas_call | solution.py:290
  17.0 0.0 collective-permute-done.4
  17.1 2.1 %integrate_far.1 = bf16[16,200,128]{2,1,0:T(8,128)(2,1)} custom-call(s32[2,49]{1,0:T(2,128)S(1)} %get-tuple-element.12.places, bf16[16,8,128]{2,1,0:T(8,128)(2,1)S(1)} %get-tuple-element.13.slots, f32[2,8,128]{2,1,0:T(8,128)S(1)} %cbrt_divide_fusion.potential, bf16[448,2048]{1,0:T(8,128)(2,1)S(1)} %get-tuple-element.14.far, ...), custom_call_target="tpu_custom_call" | custom-call | flops 822083584 | bytes 3670016 | tf_op jit(solution)/shard_map/integrate_far/pallas_call | solution.py:327
  19.2 7.3 %all-to-all-start = ((bf16[16,200,128]{2,1,0:T(8,128)(2,1)}), bf16[16,200,128]{2,1,0:T(8,128)(2,1)S(1)}, u32[]{:S(2)}, u32[]{:S(2)}) async-start(bf16[16,200,128]{2,1,0:T(8,128)(2,1)} %integrate_far.1), calls=%async_computation | async-start | bytes 1638400 | tf_op jit(solution)/shard_map/all_to_all | solution.py:427
  26.5 0.1 reshape.23
  26.5 0.1 slice_bitcast_fusion.1
  26.6 0.6 %pad_maximum_fusion = f32[8,8,8]{2,1,0:T(8,128)} fusion(f32[8,4,8]{2,1,0:T(4,128)S(1)} %get-tuple-element.17, f32[8,4,8]{2,1,0:T(4,128)S(1)} %get-tuple-element.16), kind=kLoop, calls=%fused_computation | loop fusion | flops 512 | bytes 4096 | tf_op jit(solution)/shard_map/concatenate | solution.py:432
  27.3 19.5 %all-to-all-done.got = bf16[16,200,128]{2,1,0:T(8,128)(2,1)S(1)} async-done(((bf16[16,200,128]{2,1,0:T(8,128)(2,1)}), bf16[16,200,128]{2,1,0:T(8,128)(2,1)S(1)}, u32[]{:S(2)}, u32[]{:S(2)}) %all-to-all-start) | async-done | bytes 819232 | tf_op jit(solution)/shard_map/all_to_all | solution.py:427
  46.7 1.4 %store.1 = bf16[48,4096]{1,0:T(8,128)(2,1)} custom-call(bf16[16,200,128]{2,1,0:T(8,128)(2,1)S(1)} %all-to-all-done.got), custom_call_target="tpu_custom_call" | custom-call | flops 409600 | bytes 819200 | tf_op jit(solution)/shard_map/store/pallas_call | solution.py:392
  (8 shorter events, 0.1 us)
Async XLA Ops:
  4.7 2.7 %collective-permute-start = (f32[2,16,128]{2,1,0:T(8,128)S(1)}, f32[2,16,128]{2,1,0:T(8,128)S(1)}, u32[]{:S(2)}, u32[]{:S(2)}) collective-permute-start(f32[2,16,128]{2,1,0:T(8,128)S(1)} %get-tuple-element.10), channel_id=1, source_target_pairs={{0,1},{1,0},{2,3},{3,2},{4,5},{5,4},{6,7},{7,6},{8,9},{9,8},{10,11... | collective-permute-start | bytes 49160 | tf_op jit(solution)/shard_map/ppermute | solution.py:50
  7.4 4.6 %collective-permute-start.2 = (f32[16,128]{1,0:T(8,128)S(1)}, f32[16,128]{1,0:T(8,128)S(1)}, u32[]{:S(2)}, u32[]{:S(2)}) collective-permute-start(f32[16,128]{1,0:T(8,128)S(1)} %get-tuple-element.25), channel_id=1, source_target_pairs={{2,4},{4,2},{6,0},{0,6},{3,5},{5,3},{7,1},{1,7},{10,12},{12,10},{1... | collective-permute-start | bytes 24584 | tf_op jit(solution)/shard_map/ppermute | solution.py:38
  10.4 1.6 %collective-permute-start.1 = (f32[16,128]{1,0:T(8,128)S(1)}, f32[16,128]{1,0:T(8,128)S(1)}, u32[]{:S(2)}, u32[]{:S(2)}) collective-permute-start(f32[16,128]{1,0:T(8,128)S(1)} %get-tuple-element.24), channel_id=1, source_target_pairs={{0,2},{2,0},{4,6},{6,4},{1,3},{3,1},{5,7},{7,5},{8,10},{10,8},{12,... | collective-permute-start | bytes 24584 | tf_op jit(solution)/shard_map/ppermute | solution.py:37
  12.0 2.7 %collective-permute-start.3 = (f32[2,8,128]{2,1,0:T(8,128)S(1)}, f32[2,8,128]{2,1,0:T(8,128)S(1)}, u32[]{:S(2)}, u32[]{:S(2)}) collective-permute-start(f32[2,8,128]{2,1,0:T(8,128)S(1)} %get-tuple-element.23), channel_id=1, source_target_pairs={{0,8},{8,0},{16,24},{24,16},{1,9},{9,1},{17,25},{25,17},{2,10},{10... | collective-permute-start | bytes 24584 | tf_op jit(solution)/shard_map/ppermute | solution.py:37
  12.1 4.9 %collective-permute-start.4 = (f32[2,8,128]{2,1,0:T(8,128)S(1)}, f32[2,8,128]{2,1,0:T(8,128)S(1)}, u32[]{:S(2)}, u32[]{:S(2)}) collective-permute-start(f32[2,8,128]{2,1,0:T(8,128)S(1)} %get-tuple-element.22), channel_id=1, source_target_pairs={{8,16},{16,8},{24,0},{0,24},{9,17},{17,9},{25,1},{1,25},{10,18},{1... | collective-permute-start | bytes 24584 | tf_op jit(solution)/shard_map/ppermute | solution.py:38
  19.2 27.6 %all-to-all-start = ((bf16[16,200,128]{2,1,0:T(8,128)(2,1)}), bf16[16,200,128]{2,1,0:T(8,128)(2,1)S(1)}, u32[]{:S(2)}, u32[]{:S(2)}) async-start(bf16[16,200,128]{2,1,0:T(8,128)(2,1)} %integrate_far.1), calls=%async_computation | async-start | bytes 1638400 | tf_op jit(solution)/shard_map/all_to_all | solution.py:427

commit v9 on v8

--- a/solution.py
+++ b/solution.py
@@ -161,7 +161,7 @@
     )(*in_hbm(pair_groups, density_blocks, basis))
 
 
-def tabulate(groups, codes, owner, slot, counts, place, slot_rows):
+def tabulate(groups, span, codes, owner, slot, counts, place, slot_rows):
     pairs, owners = codes.shape[1], counts.shape[0]
     lines = BASIS // 2
     slot_rows[...] = jnp.full(slot_rows.shape, pairs, jnp.float32)
@@ -175,8 +175,7 @@
         rank = counts[o]
         counts[o] = rank + 1
         code = codes[0, p] * groups + codes[1, p]
-        place[0, code] = o
-        place[1, code] = rank * lines
+        place[0, code] = o * span + rank * lines
         row = slot_rows[pl.ds(o, 1), :]
         slot_rows[pl.ds(o, 1), :] = jnp.where(lane == rank, slot[0, p].astype(jnp.float32), row)
     free_owner, free_rank = jnp.int32(0), counts[0]
@@ -184,10 +183,10 @@
         fewer = counts[o] < free_rank
         free_owner = jnp.where(fewer, o, free_owner)
         free_rank = jnp.where(fewer, counts[o], free_rank)
+    free_row = free_owner * span + free_rank * lines
     for code in range(groups * groups):
-        absent = place[0, code] < 0
-        place[1, code] = jnp.where(absent, free_rank * lines, place[1, code])
-        place[0, code] = jnp.where(absent, free_owner, place[0, code])
+        row = place[0, code]
+        place[0, code] = jnp.where(row < 0, free_row, row)
 
 
 def overlaps(table, potential, planes=4):
@@ -208,7 +207,7 @@
 
 
 def near_kernel(
-    groups, pair_groups, owner, owner_slot, potential, near, basis, total, far, places, slots,
+    groups, span, pair_groups, owner, owner_slot, potential, near, basis, total, far, places, slots,
     codes, owners_of, slots_of, counts, place, slot_rows, arrived, staged,
 ):
     rows = near.shape[0]
@@ -227,7 +226,7 @@
             total[:, :rows] = part
             for copy in tables:
                 copy.wait()
-            tabulate(groups, codes, owners_of, slots_of, counts, place, slot_rows)
+            tabulate(groups, span, codes, owners_of, slots_of, counts, place, slot_rows)
         else:
             total[:, :rows] += part
     places_copy = pltpu.make_async_copy(place, places, staged.at[3])
@@ -244,11 +243,11 @@
     rows = groups * BASIS
     lines = BASIS // 2
     places_copy = pltpu.make_async_copy(places, place, staged.at[0])
-    slots_copy = pltpu.make_async_copy(
-        slots, send.at[:, pl.ds(send.shape[1] - slots.shape[1], slots.shape[1]), :], staged.at[1]
-    )
     places_copy.start()
-    slots_copy.start()
+    span = send.shape[0] // slots.shape[0]
+    for o in range(slots.shape[0]):
+        rows_of = pl.ds((o + 1) * span - slots.shape[1], slots.shape[1])
+        pltpu.make_async_copy(slots.at[o], send.at[rows_of, :], staged.at[1]).start()
     for c, part in enumerate(overlaps(far, potential)):
         if c == 0:
             total[:, :rows] = near_total[:, :rows] + part
@@ -267,11 +266,11 @@
             else:
                 upper = pltpu.roll(upper, BASIS, axis=1)
             blocks[code] = (jnp.where(left, upper, lower) * GRID_WEIGHT).astype(blocks.dtype)
-            line = pl.multiple_of(place[1, code], lines)
+            row = pl.multiple_of(place[0, code], 8)
             pltpu.make_async_copy(
-                blocks.at[code], send.at[place[0, code], pl.ds(line, lines), :], sent
+                blocks.at[code], send.at[pl.ds(row, lines), :], sent
             ).start()
-    slots_copy.wait()
+    pltpu.make_async_copy(slots, slots, staged.at[1]).wait()
     pltpu.make_async_copy(blocks, blocks, sent).wait()
 
 
@@ -283,17 +282,17 @@
     return -(-rows // LANES) * LANES
 
 
-def integrated_near(near, basis, potential, pair_groups, owner, owner_slot, owners):
+def integrated_near(near, basis, potential, pair_groups, owner, owner_slot, owners, capacity):
     rows, pairs = basis.shape[0], pair_groups.shape[1]
     groups = rows // BASIS
     vmem, hbm = pl.BlockSpec(memory_space=pltpu.VMEM), pl.BlockSpec(memory_space=pltpu.HBM)
     return pl.pallas_call(
-        functools.partial(near_kernel, groups),
+        functools.partial(near_kernel, groups, capacity * BASIS // 2 + 8),
         name="integrate_near",
         out_shape=(
             jax.ShapeDtypeStruct((rows, padded(rows)), jnp.float32),
             jax.ShapeDtypeStruct((rows, EXT3 // 2), basis.dtype),
-            jax.ShapeDtypeStruct((2, groups * groups), jnp.int32),
+            jax.ShapeDtypeStruct((1, groups * groups), jnp.int32),
             jax.ShapeDtypeStruct((owners, 8, LANES), jnp.bfloat16),
         ),
         in_specs=[hbm, hbm, hbm, vmem, vmem, hbm],
@@ -303,7 +302,7 @@
             pltpu.SMEM((1, pairs), jnp.int32),
             pltpu.SMEM((1, pairs), jnp.int32),
             pltpu.SMEM((owners,), jnp.int32),
-            pltpu.SMEM((2, groups * groups), jnp.int32),
+            pltpu.SMEM((1, groups * groups), jnp.int32),
             pltpu.VMEM((owners, LANES), jnp.float32),
             pltpu.SemaphoreType.DMA(()),
             pltpu.SemaphoreType.DMA((4,)),
@@ -328,7 +327,7 @@
         functools.partial(far_kernel, groups),
         name="integrate_far",
         out_shape=jax.ShapeDtypeStruct(
-            (slots.shape[0], capacity * BASIS // 2 + slots.shape[1], LANES), jnp.bfloat16
+            (slots.shape[0] * (capacity * BASIS // 2 + slots.shape[1]), LANES), jnp.bfloat16
         ),
         in_specs=[hbm, vmem, vmem, vmem, vmem],
         out_specs=hbm,
@@ -421,9 +420,10 @@
     near, far = slater_potential(near), slater_potential(far)
 
     total, far_table, places, slots = integrated_near(
-        near_table, basis, near, pair_groups, owner, owner_slot, owners
+        near_table, basis, near, pair_groups, owner, owner_slot, owners, capacity
     )
     send = integrated_far(far_table, total, far, places, slots, capacity)
+    send = send.reshape(owners, -1, LANES)
     got = lax.all_to_all(send, ("gx", "gy"), split_axis=0, concat_axis=0, tiled=True)
 
     potential = jnp.concatenate(

time: 48.3 us -> 48.3 us (level)
  transfers between devices with their start and end apart: 6 -> 6, of which waited for: 3 -> 3; matrix products, arithmetic and copies ran while one was open for 2% -> 2% of each run, Pallas kernels for 5% -> 4%
where the time goes in v9:
time: 48.3 us; the launch traced here: 48 us
  waiting for transfers between devices  22.5 us (47%)
  starting transfers between devices  14.3 us (30%)
  Pallas kernels  9.69 us (20%)
  other arithmetic  0.73 us (2%)
  between operations  0.71 us (1%)
    all_to_all x1, waiting for transfers between devices, per_device(): lax.all_to_all(send, ('gx', 'gy'), split_axis=0, concat_axis=0, tiled=True)  19.5 us
    all_to_all x1, starting transfers between devices, per_device(): lax.all_to_all(send, ('gx', 'gy'), split_axis=0, concat_axis=0, tiled=True)  7.32 us
    ppermute x2, starting transfers between devices, merged_halves(): far = far + lax.ppermute(far, axis, neighbour_swaps(count, 1))  5.56 us
    pallas_call x1, Pallas kernels, collocated(): pl.pallas_call(functools.partial(collocate_kernel, groups), name='colloca...  4.09 us
    pallas_call x1, Pallas kernels, integrated_near(): pl.pallas_call(functools.partial(near_kernel, groups, capacity * BASIS //...  2.16 us
    pallas_call x1, Pallas kernels, integrated_far(): pl.pallas_call(functools.partial(far_kernel, groups), name='integrate_far...  2.07 us
    ppermute x2, waiting for transfers between devices, merged_halves(): far = far + lax.ppermute(far, axis, neighbour_swaps(count, 1))  1.63 us
    pallas_call x1, Pallas kernels, stored_blocks(): pl.pallas_call(functools.partial(store_kernel, capacity), name='store', o...  1.37 us
  transfers between devices with their start and end apart: 6, of which 3 were waited for; matrix products, arithmetic and copies ran while one was open for 2% of the time, Pallas kernels for 4%

profile of v9, /device:TPU:9, one launch (start us, length us, event | category | flops | bytes accessed | tf_op | source)
XLA Modules:
  0.0 48.0 jit_solution(15551816616098032027)
XLA Ops:
  0.6 4.1 %collocate.1 = (f32[2,16,128]{2,1,0:T(8,128)S(1)}, f32[2,16,128]{2,1,0:T(8,128)S(1)}, bf16[448,2048]{1,0:T(8,128)(2,1)S(1)}) custom-call(s32[2,48]{1,0:T(2,128)} %pair_groups.3, bf16[48,4096]{1,0:T(8,128)(2,1)} %blocks.1, bf16[448,4096]{1,0:T(8,128)(2,1)} %bitcast.16), custom_call_target="tpu_custom_call" | custom-call | flops 1644167168 | bytes 3670016 | tf_op jit(solution)/shard_map/collocate/pallas_call | solution.py:137
  4.7 1.3 %collective-permute-start = (f32[2,16,128]{2,1,0:T(8,128)S(1)}, f32[2,16,128]{2,1,0:T(8,128)S(1)}, u32[]{:S(2)}, u32[]{:S(2)}) collective-permute-start(f32[2,16,128]{2,1,0:T(8,128)S(1)} %get-tuple-element.10), channel_id=1, source_target_pairs={{0,1},{1,0},{2,3},{3,2},{4,5},{5,4},{6,7},{7,6},{8,9},{9,8},{10,11... | collective-permute-start | bytes 49160 | tf_op jit(solution)/shard_map/ppermute | solution.py:50
  6.0 1.4 %collective-permute-done = f32[2,16,128]{2,1,0:T(8,128)S(1)} collective-permute-done((f32[2,16,128]{2,1,0:T(8,128)S(1)}, f32[2,16,128]{2,1,0:T(8,128)S(1)}, u32[]{:S(2)}, u32[]{:S(2)}) %collective-permute-start) | collective-permute-done | bytes 16416 | tf_op jit(solution)/shard_map/ppermute | solution.py:50
  7.4 3.0 %collective-permute-start.2 = (f32[16,128]{1,0:T(8,128)S(1)}, f32[16,128]{1,0:T(8,128)S(1)}, u32[]{:S(2)}, u32[]{:S(2)}) collective-permute-start(f32[16,128]{1,0:T(8,128)S(1)} %get-tuple-element.25), channel_id=1, source_target_pairs={{2,4},{4,2},{6,0},{0,6},{3,5},{5,3},{7,1},{1,7},{10,12},{12,10},{1... | collective-permute-start | bytes 24584 | tf_op jit(solution)/shard_map/ppermute | solution.py:38
  10.4 0.0 collective-permute-start.1
  10.4 1.6 %collective-permute-done.2 = f32[16,128]{1,0:T(8,128)S(1)} collective-permute-done((f32[16,128]{1,0:T(8,128)S(1)}, f32[16,128]{1,0:T(8,128)S(1)}, u32[]{:S(2)}, u32[]{:S(2)}) %collective-permute-start.2) | collective-permute-done | bytes 8224 | tf_op jit(solution)/shard_map/ppermute | solution.py:38
  12.0 0.0 collective-permute-done.1
  12.0 0.1 collective-permute-start.3
  12.1 2.6 %collective-permute-start.4 = (f32[2,8,128]{2,1,0:T(8,128)S(1)}, f32[2,8,128]{2,1,0:T(8,128)S(1)}, u32[]{:S(2)}, u32[]{:S(2)}) collective-permute-start(f32[2,8,128]{2,1,0:T(8,128)S(1)} %get-tuple-element.22), channel_id=1, source_target_pairs={{8,16},{16,8},{24,0},{0,24},{9,17},{17,9},{25,1},{1,25},{10,18},{1... | collective-permute-start | bytes 24584 | tf_op jit(solution)/shard_map/ppermute | solution.py:38
  14.7 0.0 collective-permute-done.3
  14.7 2.2 %integrate_near.1 = (f32[448,512]{1,0:T(8,128)S(1)}, bf16[448,2048]{1,0:T(8,128)(2,1)S(1)}, s32[1,49]{1,0:T(1,128)S(1)}, bf16[16,8,128]{2,1,0:T(8,128)(2,1)S(1)}) custom-call(s32[2,48]{1,0:T(2,128)} %pair_groups.3, s32[1,48]{1,0:T(1,128)} %bitcast.18, s32[1,48]{1,0:T(1,128)} %bitcast.19, f32[2,8,128]{2,1,0:T(8,128)S(1)} %cbrt_divide_fusion.1.potential, ...), custom_call_target="tpu_custom_call" | custom-call | flops 822083584 | bytes 3670016 | tf_op jit(solution)/shard_map/integrate_near/pallas_call | solution.py:289
  16.9 0.0 collective-permute-done.4
  16.9 2.1 %integrate_far.1 = bf16[3200,128]{1,0:T(8,128)(2,1)} custom-call(s32[1,49]{1,0:T(1,128)S(1)} %get-tuple-element.12.places, bf16[16,8,128]{2,1,0:T(8,128)(2,1)S(1)} %get-tuple-element.13.slots, f32[2,8,128]{2,1,0:T(8,128)S(1)} %cbrt_divide_fusion.potential, bf16[448,2048]{1,0:T(8,128)(2,1)S(1)} %get-tuple-element.14.far, ...), custom_call_target="tpu_custom_call" | custom-call | flops 822083584 | bytes 3670016 | tf_op jit(solution)/shard_map/integrate_far/pallas_call | solution.py:326
  19.0 7.3 %all-to-all-start = ((bf16[16,200,128]{2,1,0:T(8,128)(2,1)}), bf16[16,200,128]{2,1,0:T(8,128)(2,1)S(1)}, u32[]{:S(2)}, u32[]{:S(2)}) async-start(bf16[16,200,128]{2,1,0:T(8,128)(2,1)} %bitcast.7), calls=%async_computation | async-start | bytes 1638400 | tf_op jit(solution)/shard_map/all_to_all | solution.py:427
  26.4 0.1 reshape.27
  26.4 0.1 slice_bitcast_fusion.1
  26.5 0.6 %pad_maximum_fusion = f32[8,8,8]{2,1,0:T(8,128)} fusion(f32[8,4,8]{2,1,0:T(4,128)S(1)} %get-tuple-element.17, f32[8,4,8]{2,1,0:T(4,128)S(1)} %get-tuple-element.16), kind=kLoop, calls=%fused_computation | loop fusion | flops 512 | bytes 4096 | tf_op jit(solution)/shard_map/concatenate | solution.py:432
  27.2 19.5 %all-to-all-done.got = bf16[16,200,128]{2,1,0:T(8,128)(2,1)S(1)} async-done(((bf16[16,200,128]{2,1,0:T(8,128)(2,1)}), bf16[16,200,128]{2,1,0:T(8,128)(2,1)S(1)}, u32[]{:S(2)}, u32[]{:S(2)}) %all-to-all-start) | async-done | bytes 819232 | tf_op jit(solution)/shard_map/all_to_all | solution.py:427
  46.6 1.4 %store.1 = bf16[48,4096]{1,0:T(8,128)(2,1)} custom-call(bf16[16,200,128]{2,1,0:T(8,128)(2,1)S(1)} %all-to-all-done.got), custom_call_target="tpu_custom_call" | custom-call | flops 409600 | bytes 819200 | tf_op jit(solution)/shard_map/store/pallas_call | solution.py:391
  (8 shorter events, 0.1 us)
Async XLA Ops:
  4.7 2.7 %collective-permute-start = (f32[2,16,128]{2,1,0:T(8,128)S(1)}, f32[2,16,128]{2,1,0:T(8,128)S(1)}, u32[]{:S(2)}, u32[]{:S(2)}) collective-permute-start(f32[2,16,128]{2,1,0:T(8,128)S(1)} %get-tuple-element.10), channel_id=1, source_target_pairs={{0,1},{1,0},{2,3},{3,2},{4,5},{5,4},{6,7},{7,6},{8,9},{9,8},{10,11... | collective-permute-start | bytes 49160 | tf_op jit(solution)/shard_map/ppermute | solution.py:50
  7.4 4.6 %collective-permute-start.2 = (f32[16,128]{1,0:T(8,128)S(1)}, f32[16,128]{1,0:T(8,128)S(1)}, u32[]{:S(2)}, u32[]{:S(2)}) collective-permute-start(f32[16,128]{1,0:T(8,128)S(1)} %get-tuple-element.25), channel_id=1, source_target_pairs={{2,4},{4,2},{6,0},{0,6},{3,5},{5,3},{7,1},{1,7},{10,12},{12,10},{1... | collective-permute-start | bytes 24584 | tf_op jit(solution)/shard_map/ppermute | solution.py:38
  10.4 1.6 %collective-permute-start.1 = (f32[16,128]{1,0:T(8,128)S(1)}, f32[16,128]{1,0:T(8,128)S(1)}, u32[]{:S(2)}, u32[]{:S(2)}) collective-permute-start(f32[16,128]{1,0:T(8,128)S(1)} %get-tuple-element.24), channel_id=1, source_target_pairs={{0,2},{2,0},{4,6},{6,4},{1,3},{3,1},{5,7},{7,5},{8,10},{10,8},{12,... | collective-permute-start | bytes 24584 | tf_op jit(solution)/shard_map/ppermute | solution.py:37
  12.0 2.7 %collective-permute-start.3 = (f32[2,8,128]{2,1,0:T(8,128)S(1)}, f32[2,8,128]{2,1,0:T(8,128)S(1)}, u32[]{:S(2)}, u32[]{:S(2)}) collective-permute-start(f32[2,8,128]{2,1,0:T(8,128)S(1)} %get-tuple-element.23), channel_id=1, source_target_pairs={{0,8},{8,0},{16,24},{24,16},{1,9},{9,1},{17,25},{25,17},{2,10},{10... | collective-permute-start | bytes 24584 | tf_op jit(solution)/shard_map/ppermute | solution.py:37
  12.1 4.8 %collective-permute-start.4 = (f32[2,8,128]{2,1,0:T(8,128)S(1)}, f32[2,8,128]{2,1,0:T(8,128)S(1)}, u32[]{:S(2)}, u32[]{:S(2)}) collective-permute-start(f32[2,8,128]{2,1,0:T(8,128)S(1)} %get-tuple-element.22), channel_id=1, source_target_pairs={{8,16},{16,8},{24,0},{0,24},{9,17},{17,9},{25,1},{1,25},{10,18},{1... | collective-permute-start | bytes 24584 | tf_op jit(solution)/shard_map/ppermute | solution.py:38
  19.0 27.6 %all-to-all-start = ((bf16[16,200,128]{2,1,0:T(8,128)(2,1)}), bf16[16,200,128]{2,1,0:T(8,128)(2,1)S(1)}, u32[]{:S(2)}, u32[]{:S(2)}) async-start(bf16[16,200,128]{2,1,0:T(8,128)(2,1)} %bitcast.7), calls=%async_computation | async-start | bytes 1638400 | tf_op jit(solution)/shard_map/all_to_all | solution.py:427
